TPU v7x, 128 devices: a whole 4x4x4 slice. The times are simulated.
128 devices in a mesh: dp: 8 (over y_lo, z), tensor: 16 (over y_hi, x, core).
Axes of the slice: x: 4, y: 4 (y_hi: 2, y_lo: 2; y = y_hi * 2 + y_lo), z: 4, core: 2. Of those that a mesh axis runs over, the one named last changes fastest.
Arguments:
- tokens: bfloat16 [2048, 4096], P('dp', 'tensor'), may hold values from -0.25 to 0.25
- small_weights: bfloat16 [2, 3328, 8960], P(None, ('dp', 'tensor')), may hold values from -6 to 6
- ffn_growth: bfloat16 [11008, 8960], P('tensor'), may hold values from -0.0625 to 0.0625
- width_growth: bfloat16 [4096, 3328], P('dp'), may hold values from -0.109375 to 0.109375
Outputs:
- grown_weights: bfloat16 [2, 4096, 11008], P(None, 'dp', 'tensor')
- hidden: bfloat16 [2048, 11008], P('dp', 'tensor')
All inputs are finite; a program needn't handle non-finite values.
Results may differ from a plain program's by a relative error of at most 0.0071.
Values may be sent and summed in bfloat16 or wider, within the bound.
A program may use at most 128 MiB of HBM per device.

v0:
```python
import jax
import jax.numpy as jnp
from jax import lax
from jax.sharding import PartitionSpec as P


def on_device(tokens, small_weights, ffn_growth, width_growth):
    gathered = lax.all_gather(tokens, "tensor", axis=1, tiled=True)
    panels = jnp.einsum(
        "msf,cf->msc",
        lax.all_gather(small_weights, "tensor", axis=1, tiled=True),
        ffn_growth,
        preferred_element_type=jnp.float32,
    ).astype(jnp.bfloat16)
    summed = jnp.einsum(
        "rs,msc->mrc",
        width_growth,
        lax.all_gather(panels, "dp", axis=1, tiled=True),
        preferred_element_type=jnp.float32,
    )
    grown_weights = summed.astype(jnp.bfloat16)
    pre_values = jnp.einsum(
        "tr,mrc->tmc",
        gathered,
        lax.all_gather(grown_weights, "dp", axis=1, tiled=True),
        preferred_element_type=jnp.float32,
    )
    hidden = (jax.nn.silu(pre_values[:, 0, :]) * pre_values[:, 1, :]).astype(jnp.bfloat16)
    return (grown_weights, hidden)


def solution(mesh):
    placed = (P("dp", "tensor"), P(None, ("dp", "tensor"), None), P("tensor", None), P("dp", None))
    return jax.shard_map(
        on_device,
        mesh=mesh,
        in_specs=placed,
        out_specs=(P(None, "dp", "tensor"), P("dp", "tensor")),
        check_vma=False,
    )
```

profile of v0, /device:TPU:6, one launch (start us, length us, event | category | flops | bytes accessed | tf_op | source)
XLA Modules:
  0.0 427.0 jit_solution(18096152187608463315)
XLA Ops:
  7.2 0.0 copy-start
  7.2 0.0 all-gather.5.cloned.1.call-start
  7.2 0.7 all-gather.5.cloned.1.call-update
  7.9 0.0 all-gather.7.cloned.1.call-start
  8.0 104.7 %all-gather.5.cloned.1.call-done = bf16[2,416,8960]{2,0,1:T(2,128)(2,1)} async-done(((bf16[2,26,8960]{2,0,1:T(2,128)(2,1)}), bf16[2,416,8960]{2,0,1:T(2,128)(2,1)}) %all-gather.5.cloned.1.call-update) | async-done | bytes 14909456 | tf_op jit(solution)/shard_map/all_gather | solution.py:11
  112.7 20.6 %fusion.10 = bf16[2,416,688]{2,1,0:T(8,128)(2,1)} fusion(bf16[688,8960]{1,0:T(8,128)(2,1)} %param.6, bf16[2,416,8960]{2,0,1:T(2,128)(2,1)} %all-gather.5.cloned.1.call-done), kind=kOutput, calls=%fused_computation.8 | convolution fusion | flops 10258267136 | bytes 28383232 | tf_op jit(solution)/shard_map/msf,cf->msc/dot_general | solution.py:9
  133.2 0.0 all-gather.7.cloned.1.call-update
  133.3 0.0 all-gather.11.cloned.1.call-start
  133.3 0.7 all-gather.11.cloned.1.call-update
  134.0 0.0 all-gather.9.cloned.1.call-start
  134.0 108.4 %all-gather.7.cloned.1.call-done = bf16[2,3328,688]{2,1,0:T(8,128)(2,1)} async-done(((bf16[2,416,688]{2,1,0:T(8,128)(2,1)}), bf16[2,3328,688]{2,1,0:T(8,128)(2,1)}) %all-gather.7.cloned.1.call-update) | async-done | bytes 9158672 | tf_op jit(solution)/shard_map/all_gather | solution.py:18
  242.4 0.0 copy-done
  242.4 10.5 %fusion.15 = bf16[2,512,688]{1,2,0:T(8,128)(2,1)} fusion(bf16[2,3328,688]{2,1,0:T(8,128)(2,1)} %all-gather.7.cloned.1.call-done, bf16[512,3328]{1,0:T(8,128)(2,1)S(1)} %copy-done), kind=kOutput, calls=%fused_computation.9 | convolution fusion | flops 4689936384 | bytes 13975552 | tf_op jit(solution)/shard_map/rs,msc->mrc/dot_general | solution.py:15
  252.9 0.0 all-gather.9.cloned.1.call-update
  252.9 39.6 %all-gather.11.cloned.1.call-done = bf16[256,4096]{1,0:T(8,128)(2,1)} async-done(((bf16[256,256]{1,0:T(8,128)(2,1)}), bf16[256,4096]{1,0:T(8,128)(2,1)}) %all-gather.11.cloned.1.call-update) | async-done | bytes 2097168 | tf_op jit(solution)/shard_map/all_gather | solution.py:8
  292.5 120.4 %all-gather.9.cloned.1.call-done = bf16[2,4096,688]{1,2,0:T(8,128)(2,1)} async-done(((bf16[2,512,688]{1,2,0:T(8,128)(2,1)}), bf16[2,4096,688]{1,2,0:T(8,128)(2,1)}) %all-gather.9.cloned.1.call-update) | async-done | bytes 11272208 | tf_op jit(solution)/shard_map/all_gather | solution.py:25
  412.9 6.6 %fusion.18 = f32[256,2,688]{0,2,1:T(8,128)S(1)} fusion(bf16[2,4096,688]{1,2,0:T(8,128)(2,1)} %all-gather.9.cloned.1.call-done, bf16[256,4096]{1,0:T(8,128)(2,1)} %all-gather.11.cloned.1.call-done), kind=kOutput, calls=%fused_computation.10 | convolution fusion | flops 2885681152 | bytes 14778368 | tf_op jit(solution)/shard_map/tr,mrc->tmc/dot_general | solution.py:22
  419.5 0.9 fusion.22
Async XLA Ops:
  7.2 235.2 %copy-start = (bf16[512,3328]{1,0:T(8,128)(2,1)S(1)}, bf16[512,3328]{1,0:T(8,128)(2,1)}, u32[]{:S(2)}) copy-start(bf16[512,3328]{1,0:T(8,128)(2,1)} %param.7) | copy-start | bytes 10223620
  7.2 105.5 %all-gather.5.cloned.1.call-start = ((), (), s32[]{:S(2)}) async-start(), calls=%async_computation | async-start | bytes 15841280 | tf_op jit(solution)/shard_map/all_gather | solution.py:11
  7.9 234.5 %all-gather.7.cloned.1.call-start = ((), (), s32[]{:S(2)}) async-start(), calls=%async_computation.1 | async-start | bytes 11501568 | tf_op jit(solution)/shard_map/all_gather | solution.py:18
  133.3 159.3 %all-gather.11.cloned.1.call-start = ((), (), s32[]{:S(2)}) async-start(), calls=%async_computation.3 | async-start | bytes 2228224 | tf_op jit(solution)/shard_map/all_gather | solution.py:8
  134.0 278.9 %all-gather.9.cloned.1.call-start = ((), (), s32[]{:S(2)}) async-start(), calls=%async_computation.2 | async-start | bytes 12681216 | tf_op jit(solution)/shard_map/all_gather | solution.py:25
Sparse Core Ops, SparseCore 0:
  10.6 102.0 all-gather.4
  133.4 108.9 all-gather.6
  244.7 47.8 all-gather.10
  294.6 118.2 all-gather.8
where the time goes:
time: 428 us; the launch traced here: 427 us
  waiting for transfers between devices  374 us (87%)
  matrix products  37.7 us (9%)
  between operations  13.8 us (3%)
    all_gather x1, waiting for transfers between devices, on_device(): lax.all_gather(grown_weights, 'dp', axis=1, tiled=True)  120 us
    all_gather x1, waiting for transfers between devices, on_device(): lax.all_gather(panels, 'dp', axis=1, tiled=True)  108 us
    all_gather x1, waiting for transfers between devices, on_device(): lax.all_gather(small_weights, 'tensor', axis=1, tiled=True)  105 us
    all_gather x1, waiting for transfers between devices, on_device(): gathered = lax.all_gather(tokens, 'tensor', axis=1, tiled=True)  39.6 us
    dot_general x1, matrix products, on_device(): jnp.einsum('msf,cf->msc', lax.all_gather(small_weights, 'tensor', axis=1,...  20.6 us
    dot_general x1, matrix products, on_device(): jnp.einsum('rs,msc->mrc', width_growth, lax.all_gather(panels, 'dp', axis...  10.5 us
  transfers between devices with their start and end apart: 4, of which 4 were waited for; matrix products, arithmetic and copies ran while one was open for 2% of the time, Pallas kernels for 0%

commit v1 on v0

--- a/solution.py
+++ b/solution.py
@@ -5,24 +5,33 @@
 
 
 def on_device(tokens, small_weights, ffn_growth, width_growth):
+    n_t = lax.axis_size("tensor")
+    t = lax.axis_index("tensor")
+    ds = width_growth.shape[1]
+    xw = ds // n_t
     gathered = lax.all_gather(tokens, "tensor", axis=1, tiled=True)
+    w_cols = lax.dynamic_slice_in_dim(width_growth, t * xw, xw, axis=1)
+    w_cols = lax.all_gather(w_cols, "dp", axis=0, tiled=True)
+    tw_part = jnp.dot(gathered, w_cols, preferred_element_type=jnp.float32)
+    tw_t = lax.all_gather(tw_part.astype(jnp.bfloat16).T, "tensor", axis=0, tiled=True)
     panels = jnp.einsum(
         "msf,cf->msc",
         lax.all_gather(small_weights, "tensor", axis=1, tiled=True),
         ffn_growth,
         preferred_element_type=jnp.float32,
     ).astype(jnp.bfloat16)
+    all_panels = lax.all_gather(panels, "dp", axis=1, tiled=True)
     summed = jnp.einsum(
         "rs,msc->mrc",
         width_growth,
-        lax.all_gather(panels, "dp", axis=1, tiled=True),
+        all_panels,
         preferred_element_type=jnp.float32,
     )
     grown_weights = summed.astype(jnp.bfloat16)
     pre_values = jnp.einsum(
-        "tr,mrc->tmc",
-        gathered,
-        lax.all_gather(grown_weights, "dp", axis=1, tiled=True),
+        "st,msc->tmc",
+        tw_t,
+        all_panels,
         preferred_element_type=jnp.float32,
     )
     hidden = (jax.nn.silu(pre_values[:, 0, :]) * pre_values[:, 1, :]).astype(jnp.bfloat16)

time: 428 us -> 390 us (0.911)
  waiting for transfers between devices: 374 us -> 332 us
    all_gather x2 -> x3, waiting for transfers between devices: 229 us -> 182 us  [the longest x1 111 us: on_device(): all_panels = lax.all_gather(panels, 'dp', axis=1, tiled=True)]
    all_gather x1, waiting for transfers between devices: 39.6 us -> 50.4 us  [on_device(): gathered = lax.all_gather(tokens, 'tensor', axis=1, tiled=True)]
    all_gather x1, waiting for transfers between devices: 105 us -> 97.7 us  [on_device(): lax.all_gather(small_weights, 'tensor', axis=1, tiled=True)]
    dot_general x2 -> x3, matrix products: 17.1 us -> 19 us  [the longest x1 8.54 us: on_device(): jnp.einsum('st,msc->tmc', tw_t, all_panels, preferred_element_type=jnp.fl...]
  transfers between devices with their start and end apart: 4 -> 5, of which waited for: 4 -> 5; matrix products, arithmetic and copies ran while one was open for 2% -> 6% of each run, Pallas kernels for 0% -> 0%
where the time goes in v1:
time: 390 us; the launch traced here: 389 us
  waiting for transfers between devices  332 us (85%)
  matrix products  39.5 us (10%)
  between operations  13.8 us (4%)
    all_gather x1, waiting for transfers between devices, on_device(): all_panels = lax.all_gather(panels, 'dp', axis=1, tiled=True)  111 us
    all_gather x1, waiting for transfers between devices, on_device(): lax.all_gather(small_weights, 'tensor', axis=1, tiled=True)  97.7 us
    all_gather x1, waiting for transfers between devices, on_device(): gathered = lax.all_gather(tokens, 'tensor', axis=1, tiled=True)  50.4 us
    all_gather x1, waiting for transfers between devices, on_device(): w_cols = lax.all_gather(w_cols, 'dp', axis=0, tiled=True)  42.9 us
    all_gather x1, waiting for transfers between devices, on_device(): lax.all_gather(tw_part.astype(jnp.bfloat16).T, 'tensor', axis=0, tiled=True)  28.7 us
    dot_general x1, matrix products, on_device(): jnp.einsum('msf,cf->msc', lax.all_gather(small_weights, 'tensor', axis=1,...  20.6 us
    dot_general x1, matrix products, on_device(): jnp.einsum('st,msc->tmc', tw_t, all_panels, preferred_element_type=jnp.fl...  8.54 us
  transfers between devices with their start and end apart: 5, of which 5 were waited for; matrix products, arithmetic and copies ran while one was open for 6% of the time, Pallas kernels for 0%

profile of v1, /device:TPU:6, one launch (start us, length us, event | category | flops | bytes accessed | tf_op | source)
XLA Modules:
  0.0 389.0 jit_solution(3943867910137675745)
XLA Ops:
  7.2 0.0 copy-start
  7.2 0.0 all-gather.10.cloned.1.call-start
  7.2 1.9 copy-done
  9.1 0.8 constant_dynamic-slice_fusion
  10.0 0.0 all-gather.10.cloned.1.call-update
  10.0 0.0 all-gather.12.cloned.1.call-start
  10.1 0.7 all-gather.12.cloned.1.call-update
  10.8 0.0 all-gather.6.cloned.1.call-start
  10.8 0.7 all-gather.6.cloned.1.call-update
  11.5 0.0 all-gather.14.cloned.1.call-start
  11.5 42.9 %all-gather.10.cloned.1.call-done = bf16[4096,208]{1,0:T(8,128)(2,1)} async-done(((bf16[512,208]{1,0:T(8,128)(2,1)}), bf16[4096,208]{1,0:T(8,128)(2,1)}) %all-gather.10.cloned.1.call-update) | async-done | bytes 1703952 | tf_op jit(solution)/shard_map/all_gather | solution.py:14
  54.5 50.4 %all-gather.12.cloned.1.call-done = bf16[256,4096]{1,0:T(8,128)(2,1)} async-done(((bf16[256,256]{1,0:T(8,128)(2,1)}), bf16[256,4096]{1,0:T(8,128)(2,1)}) %all-gather.12.cloned.1.call-update) | async-done | bytes 2097168 | tf_op jit(solution)/shard_map/all_gather | solution.py:12
  104.9 3.7 convolution_convert_fusion
  108.6 0.0 all-gather.14.cloned.1.call-update
  108.7 0.0 all-gather.8.cloned.1.call-start
  108.7 97.7 %all-gather.6.cloned.1.call-done = bf16[2,416,8960]{2,0,1:T(2,128)(2,1)} async-done(((bf16[2,26,8960]{2,0,1:T(2,128)(2,1)}), bf16[2,416,8960]{2,0,1:T(2,128)(2,1)}) %all-gather.6.cloned.1.call-update) | async-done | bytes 14909456 | tf_op jit(solution)/shard_map/all_gather | solution.py:19
  206.4 20.6 %fusion.10 = bf16[2,416,688]{2,1,0:T(8,128)(2,1)} fusion(bf16[688,8960]{1,0:T(8,128)(2,1)} %param.6, bf16[2,416,8960]{2,0,1:T(2,128)(2,1)} %all-gather.6.cloned.1.call-done), kind=kOutput, calls=%fused_computation.8 | convolution fusion | flops 10258267136 | bytes 28383232 | tf_op jit(solution)/shard_map/msf,cf->msc/dot_general | solution.py:17
  226.9 0.0 all-gather.8.cloned.1.call-update
  227.0 28.7 %all-gather.14.cloned.1.call-done = bf16[3328,256]{1,0:T(8,128)(2,1)} async-done(((bf16[208,256]{1,0:T(8,128)(2,1)}), bf16[3328,256]{1,0:T(8,128)(2,1)}) %all-gather.14.cloned.1.call-update) | async-done | bytes 1703952 | tf_op jit(solution)/shard_map/all_gather | solution.py:16
  255.7 110.6 %all-gather.8.cloned.1.call-done = bf16[2,3328,688]{2,1,0:T(8,128)(2,1)} async-done(((bf16[2,416,688]{2,1,0:T(8,128)(2,1)}), bf16[2,3328,688]{2,1,0:T(8,128)(2,1)}) %all-gather.8.cloned.1.call-update) | async-done | bytes 9158672 | tf_op jit(solution)/shard_map/all_gather | solution.py:23
  366.2 0.0 copy-start.1
  366.2 8.5 %fusion.5 = f32[256,2,688]{0,2,1:T(8,128)S(1)} fusion(bf16[2,3328,688]{2,1,0:T(8,128)(2,1)} %all-gather.8.cloned.1.call-done, bf16[3328,256]{1,0:T(8,128)(2,1)} %all-gather.14.cloned.1.call-done), kind=kOutput, calls=%fused_computation.5 | convolution fusion | flops 2344615936 | bytes 12271616 | tf_op jit(solution)/shard_map/st,msc->tmc/dot_general | solution.py:31
  374.8 0.9 fusion.19
  375.7 0.0 copy-done.1
  375.7 6.7 %fusion.15 = bf16[2,512,688]{1,2,0:T(8,128)(2,1)} fusion(bf16[2,3328,688]{2,1,0:T(8,128)(2,1)S(1)} %copy-done.1, bf16[512,3328]{1,0:T(8,128)(2,1)S(1)} %copy-done), kind=kOutput, calls=%fused_computation.9 | convolution fusion | flops 4689936384 | bytes 13975552 | tf_op jit(solution)/shard_map/rs,msc->mrc/dot_general | solution.py:24
Async XLA Ops:
  7.2 2.0 copy-start
  7.2 47.3 %all-gather.10.cloned.1.call-start = ((), (), s32[]{:S(2)}) async-start(), calls=%async_computation.2 | async-start | bytes 2359296 | tf_op jit(solution)/shard_map/all_gather | solution.py:14
  10.0 94.9 %all-gather.12.cloned.1.call-start = ((), (), s32[]{:S(2)}) async-start(), calls=%async_computation.3 | async-start | bytes 2228224 | tf_op jit(solution)/shard_map/all_gather | solution.py:12
  10.8 195.6 %all-gather.6.cloned.1.call-start = ((), (), s32[]{:S(2)}) async-start(), calls=%async_computation | async-start | bytes 15841280 | tf_op jit(solution)/shard_map/all_gather | solution.py:19
  11.5 244.2 %all-gather.14.cloned.1.call-start = ((), (), s32[]{:S(2)}) async-start(), calls=%async_computation.4 | async-start | bytes 1810432 | tf_op jit(solution)/shard_map/all_gather | solution.py:16
  108.7 257.6 %all-gather.8.cloned.1.call-start = ((), (), s32[]{:S(2)}) async-start(), calls=%async_computation.1 | async-start | bytes 11501568 | tf_op jit(solution)/shard_map/all_gather | solution.py:23
  366.2 9.5 %copy-start.1 = (bf16[2,3328,688]{2,1,0:T(8,128)(2,1)S(1)}, bf16[2,3328,688]{2,1,0:T(8,128)(2,1)}, u32[]{:S(2)}) copy-start(bf16[2,3328,688]{2,1,0:T(8,128)(2,1)} %all-gather.8.cloned.1.call-done) | copy-start | bytes 27475972
Sparse Core Ops, SparseCore 0:
  10.2 44.2 all-gather.9
  56.7 48.1 all-gather.11
  107.5 98.8 all-gather.5
  209.2 46.4 all-gather.13
  257.7 108.4 all-gather.7

commit v2 on v1

--- a/solution.py
+++ b/solution.py
@@ -1,14 +1,126 @@
+import functools
+
 import jax
 import jax.numpy as jnp
 from jax import lax
+from jax.experimental import pallas as pl
+from jax.experimental.pallas import tpu as pltpu
 from jax.sharding import PartitionSpec as P
+
+MESH = pl.DeviceIdType.MESH
+
+
+def _ring_pos(d):
+    h = d // 4
+    return h * 7 + (1 - 2 * h) * (d % 4)
+
+
+def _ring_dev(p):
+    h = p // 4
+    return h * 4 + h * 3 + (1 - 2 * h) * (p % 4)
+
+
+def _dp_ring_kernel(n, p_ref, w3_ref, grown_ref, pall_ref, recv, acc, ssem, rsem, lsem, osem):
+    t = lax.axis_index("tensor")
+    d = lax.axis_index("dp")
+    pos = _ring_pos(d)
+    right = _ring_dev((pos + 1) % n)
+    left = _ring_dev((pos + n - 1) % n)
+
+    barrier = pltpu.get_barrier_semaphore()
+    for nb in (left, right):
+        pl.semaphore_signal(barrier, inc=1, device_id=(nb, t), device_id_type=MESH)
+    pl.semaphore_wait(barrier, 2)
+
+    own = []
+    for m in range(2):
+        c = pltpu.make_async_copy(p_ref.at[m], recv.at[m, d], osem.at[m])
+        c.start()
+        own.append(c)
+    for c in own:
+        c.wait()
+    for m in range(2):
+        pltpu.make_async_copy(recv.at[m, d], pall_ref.at[m, d], lsem.at[m, d]).start()
+
+    def step(k, carry):
+        o0 = _ring_dev((pos - k + n) % n)
+        o1 = _ring_dev((pos + k) % n)
+        c0 = pltpu.make_async_remote_copy(
+            src_ref=recv.at[0, o0], dst_ref=recv.at[0, o0],
+            send_sem=ssem.at[0, k], recv_sem=rsem.at[0, k],
+            device_id=(right, t), device_id_type=MESH)
+        c1 = pltpu.make_async_remote_copy(
+            src_ref=recv.at[1, o1], dst_ref=recv.at[1, o1],
+            send_sem=ssem.at[1, k], recv_sem=rsem.at[1, k],
+            device_id=(left, t), device_id_type=MESH)
+        c0.start()
+        c1.start()
+        g0 = jnp.dot(w3_ref[o0], recv[0, o0], preferred_element_type=jnp.float32)
+        g1 = jnp.dot(w3_ref[o1], recv[1, o1], preferred_element_type=jnp.float32)
+
+        @pl.when(k == 0)
+        def _():
+            acc[0] = g0
+            acc[1] = g1
+
+        @pl.when(k > 0)
+        def _():
+            acc[0] += g0
+            acc[1] += g1
+
+        c0.wait()
+        c1.wait()
+        n0 = _ring_dev((pos - k - 1 + n) % n)
+        n1 = _ring_dev((pos + k + 1) % n)
+        pltpu.make_async_copy(recv.at[0, n0], pall_ref.at[0, n0], lsem.at[0, n0]).start()
+        pltpu.make_async_copy(recv.at[1, n1], pall_ref.at[1, n1], lsem.at[1, n1]).start()
+        return carry
+
+    lax.fori_loop(0, n - 1, step, 0)
+    o0 = _ring_dev((pos - (n - 1) + n) % n)
+    o1 = _ring_dev((pos + n - 1) % n)
+    acc[0] += jnp.dot(w3_ref[o0], recv[0, o0], preferred_element_type=jnp.float32)
+    acc[1] += jnp.dot(w3_ref[o1], recv[1, o1], preferred_element_type=jnp.float32)
+    grown_ref[...] = acc[...].astype(grown_ref.dtype)
+    for m in range(2):
+        for o in range(n):
+            pltpu.make_async_copy(recv.at[m, o], pall_ref.at[m, o], lsem.at[m, o]).wait()
+
+
+def _dp_ring(panels, w3):
+    n, rows, blk = w3.shape
+    _, _, cols = panels.shape
+    flops = 2 * 2 * rows * blk * cols * n
+    return pl.pallas_call(
+        functools.partial(_dp_ring_kernel, n),
+        out_shape=(
+            jax.ShapeDtypeStruct((2, rows, cols), jnp.bfloat16),
+            jax.ShapeDtypeStruct((2, n, blk, cols), jnp.bfloat16),
+        ),
+        in_specs=[pl.BlockSpec(memory_space=pltpu.VMEM)] * 2,
+        out_specs=(pl.BlockSpec(memory_space=pltpu.VMEM), pl.BlockSpec(memory_space=pl.ANY)),
+        scratch_shapes=[
+            pltpu.VMEM((2, n, blk, cols), jnp.bfloat16),
+            pltpu.VMEM((2, rows, cols), jnp.float32),
+            pltpu.SemaphoreType.DMA((2, n - 1)),
+            pltpu.SemaphoreType.DMA((2, n - 1)),
+            pltpu.SemaphoreType.DMA((2, n)),
+            pltpu.SemaphoreType.DMA((2,)),
+        ],
+        compiler_params=pltpu.CompilerParams(
+            collective_id=0, has_side_effects=True, vmem_limit_bytes=56 * 1024 * 1024),
+        cost_estimate=pl.CostEstimate(
+            flops=flops, transcendentals=0, bytes_accessed=2 * 2 * n * blk * cols * 2),
+    )(panels, w3)
 
 
 def on_device(tokens, small_weights, ffn_growth, width_growth):
     n_t = lax.axis_size("tensor")
+    n_d = lax.axis_size("dp")
     t = lax.axis_index("tensor")
-    ds = width_growth.shape[1]
+    rows, ds = width_growth.shape
     xw = ds // n_t
+    blk = ds // n_d
     gathered = lax.all_gather(tokens, "tensor", axis=1, tiled=True)
     w_cols = lax.dynamic_slice_in_dim(width_growth, t * xw, xw, axis=1)
     w_cols = lax.all_gather(w_cols, "dp", axis=0, tiled=True)
@@ -20,14 +132,9 @@
         ffn_growth,
         preferred_element_type=jnp.float32,
     ).astype(jnp.bfloat16)
-    all_panels = lax.all_gather(panels, "dp", axis=1, tiled=True)
-    summed = jnp.einsum(
-        "rs,msc->mrc",
-        width_growth,
-        all_panels,
-        preferred_element_type=jnp.float32,
-    )
-    grown_weights = summed.astype(jnp.bfloat16)
+    w3 = width_growth.reshape(rows, n_d, blk).transpose(1, 0, 2)
+    grown_weights, pall = _dp_ring(panels, w3)
+    all_panels = pall.reshape(2, ds, panels.shape[2])
     pre_values = jnp.einsum(
         "st,msc->tmc",
         tw_t,

time: 390 us -> 360 us (0.923)
  waiting for transfers between devices: 332 us -> 185 us
  Pallas kernels: 0 us -> 113 us
  local copies, waits for them, and re-layouts: 2.76 us -> 13.2 us
  matrix products: 39.5 us -> 32.7 us
    pallas_call x0 -> x1, Pallas kernels: none -> 113 us  [_dp_ring(): pl.pallas_call(functools.partial(_dp_ring_kernel, n), out_shape=(jax.Shap...]
    all_gather x1 -> x0, waiting for transfers between devices: 111 us -> none  [on_device(): all_panels = lax.all_gather(panels, 'dp', axis=1, tiled=True)]
    all_gather x1, waiting for transfers between devices: 28.7 us -> 0.01 us  [on_device(): lax.all_gather(tw_part.astype(jnp.bfloat16).T, 'tensor', axis=0, tiled=True)]
    all_gather x1, waiting for transfers between devices: 42.9 us -> 35 us  [on_device(): w_cols = lax.all_gather(w_cols, 'dp', axis=0, tiled=True)]
    dot_general x1 -> x0, matrix products: 6.7 us -> none  [on_device(): jnp.einsum('rs,msc->mrc', width_growth, all_panels, preferred_element_typ...]
    unnamed x4 -> x2, local copies, waits for them, and re-layouts: 1.92 us -> 6.77 us
    reshape x0 -> x1, local copies, waits for them, and re-layouts: none -> 4.57 us  [on_device(): w3 = width_growth.reshape(rows, n_d, blk).transpose(1, 0, 2)]
  transfers between devices with their start and end apart: 5 -> 4, of which waited for: 5 -> 3; matrix products, arithmetic and copies ran while one was open for 6% -> 10% of each run, Pallas kernels for 0% -> 31%
where the time goes in v2:
time: 360 us; the launch traced here: 358 us
  waiting for transfers between devices  185 us (51%)
  Pallas kernels  113 us (31%)
  matrix products  32.7 us (9%)
  between operations  13.8 us (4%)
  local copies, waits for them, and re-layouts  13.2 us (4%)
    pallas_call x1, Pallas kernels, _dp_ring(): pl.pallas_call(functools.partial(_dp_ring_kernel, n), out_shape=(jax.Shap...  113 us
    all_gather x1, waiting for transfers between devices, on_device(): lax.all_gather(small_weights, 'tensor', axis=1, tiled=True)  97.7 us
    all_gather x1, waiting for transfers between devices, on_device(): gathered = lax.all_gather(tokens, 'tensor', axis=1, tiled=True)  50.4 us
    all_gather x1, waiting for transfers between devices, on_device(): w_cols = lax.all_gather(w_cols, 'dp', axis=0, tiled=True)  35 us
    dot_general x1, matrix products, on_device(): jnp.einsum('msf,cf->msc', lax.all_gather(small_weights, 'tensor', axis=1,...  20.6 us
    dot_general x1, matrix products, on_device(): jnp.einsum('st,msc->tmc', tw_t, all_panels, preferred_element_type=jnp.fl...  8.41 us
  transfers between devices with their start and end apart: 4, of which 3 were waited for; matrix products, arithmetic and copies ran while one was open for 10% of the time, Pallas kernels for 31%

profile of v2, /device:TPU:6, one launch (start us, length us, event | category | flops | bytes accessed | tf_op | source)
XLA Modules:
  0.0 358.0 jit_solution(9511310563181013006)
XLA Ops:
  7.2 0.0 all-gather.7.cloned.1.call-start
  7.2 1.8 constant_dynamic-slice_fusion
  9.1 0.0 all-gather.7.cloned.1.call-update
  9.1 0.0 all-gather.9.cloned.1.call-start
  9.1 0.7 all-gather.9.cloned.1.call-update
  9.8 0.0 all-gather.5.cloned.1.call-start
  9.9 0.7 all-gather.5.cloned.1.call-update
  10.6 0.0 all-gather.11.cloned.1.call-start
  10.6 4.3 %copy.15 = bf16[512,3328]{0,1:T(8,128)(2,1)S(1)} copy(bf16[512,3328]{1,0:T(8,128)(2,1)} %param.7) | data formatting | bytes 6815744 | tf_op args[3]
  14.9 4.6 %copy.16 = bf16[512,8,416]{2,0,1:T(8,128)(2,1)} copy(bf16[512,8,416]{0,2,1:T(8,128)(2,1)S(1)} %bitcast.24) | data formatting | bytes 6815744 | tf_op jit(solution)/shard_map/reshape | solution.py:135
  19.5 35.0 %all-gather.7.cloned.1.call-done = bf16[4096,208]{1,0:T(8,128)(2,1)} async-done(((bf16[512,208]{1,0:T(8,128)(2,1)}), bf16[4096,208]{1,0:T(8,128)(2,1)}) %all-gather.7.cloned.1.call-update) | async-done | bytes 1703952 | tf_op jit(solution)/shard_map/all_gather | solution.py:126
  54.5 50.4 %all-gather.9.cloned.1.call-done = bf16[256,4096]{1,0:T(8,128)(2,1)} async-done(((bf16[256,256]{1,0:T(8,128)(2,1)}), bf16[256,4096]{1,0:T(8,128)(2,1)}) %all-gather.9.cloned.1.call-update) | async-done | bytes 2097168 | tf_op jit(solution)/shard_map/all_gather | solution.py:124
  104.9 3.7 %convolution_convert_fusion = bf16[208,256]{1,0:T(8,128)(2,1)} fusion(bf16[4096,208]{1,0:T(8,128)(2,1)} %all-gather.7.cloned.1.call-done, bf16[256,4096]{1,0:T(8,128)(2,1)} %all-gather.9.cloned.1.call-done), kind=kOutput, calls=%fused_computation.6 | convolution fusion | flops 436260864 | bytes 3907584 | tf_op jit(solution)/shard_map/dot_general | solution.py:127
  108.6 0.0 all-gather.11.cloned.1.call-update
  108.6 97.7 %all-gather.5.cloned.1.call-done = bf16[2,416,8960]{2,0,1:T(2,128)(2,1)} async-done(((bf16[2,26,8960]{2,0,1:T(2,128)(2,1)}), bf16[2,416,8960]{2,0,1:T(2,128)(2,1)}) %all-gather.5.cloned.1.call-update) | async-done | bytes 14909456 | tf_op jit(solution)/shard_map/all_gather | solution.py:131
  206.3 20.6 %fusion.5.p_ref = bf16[2,416,688]{2,1,0:T(8,128)(2,1)} fusion(bf16[688,8960]{1,0:T(8,128)(2,1)} %param.6, bf16[2,416,8960]{2,0,1:T(2,128)(2,1)} %all-gather.5.cloned.1.call-done), kind=kOutput, calls=%fused_computation.5 | convolution fusion | flops 10258267136 | bytes 28383232 | tf_op jit(solution)/shard_map/msf,cf->msc/dot_general | solution.py:129
  226.9 112.6 %shard_map.59 = (bf16[2,512,688]{2,1,0:T(8,128)(2,1)}, bf16[2,8,416,688]{3,2,1,0:T(8,128)(2,1)}) custom-call(bf16[2,416,688]{2,1,0:T(8,128)(2,1)} %fusion.5.p_ref, bf16[8,512,416]{2,1,0:T(8,128)(2,1)} %bitcast.25), custom_call_target="tpu_custom_call" | custom-call | flops 4689231872 | bytes 18317312 | tf_op jit(solution)/shard_map/pallas_call | solution.py:94
  339.6 2.5 copy.18
  342.1 0.0 all-gather.11.cloned.1.call-done
  342.1 8.4 %fusion.3 = f32[256,2,688]{0,2,1:T(8,128)S(1)} fusion(bf16[2,3328,688]{2,1,0:T(8,128)(2,1)} %bitcast.26, bf16[3328,256]{1,0:T(8,128)(2,1)} %all-gather.11.cloned.1.call-done), kind=kOutput, calls=%fused_computation.3 | convolution fusion | flops 2344615936 | bytes 12271616 | tf_op jit(solution)/shard_map/st,msc->tmc/dot_general | solution.py:138
  350.5 0.9 fusion.11
Async XLA Ops:
  7.2 47.3 %all-gather.7.cloned.1.call-start = ((), (), s32[]{:S(2)}) async-start(), calls=%async_computation.1 | async-start | bytes 2359296 | tf_op jit(solution)/shard_map/all_gather | solution.py:126
  9.1 95.8 %all-gather.9.cloned.1.call-start = ((), (), s32[]{:S(2)}) async-start(), calls=%async_computation.2 | async-start | bytes 2228224 | tf_op jit(solution)/shard_map/all_gather | solution.py:124
  9.8 196.5 %all-gather.5.cloned.1.call-start = ((), (), s32[]{:S(2)}) async-start(), calls=%async_computation | async-start | bytes 15841280 | tf_op jit(solution)/shard_map/all_gather | solution.py:131
  10.6 331.5 %all-gather.11.cloned.1.call-start = ((), (), s32[]{:S(2)}) async-start(), calls=%async_computation.3 | async-start | bytes 1810432 | tf_op jit(solution)/shard_map/all_gather | solution.py:128
Sparse Core Ops, SparseCore 0:
  10.2 44.2 all-gather.6
  56.7 48.1 all-gather.8
  107.5 98.8 all-gather.4
  209.2 50.7 all-gather.10

commit v3 on v2

--- a/solution.py
+++ b/solution.py
@@ -114,6 +114,140 @@
     )(panels, w3)
 
 
+def _tw_kernel(nt, nd, tok_ref, wcol_ref, out_ref, tbuf, wbuf, xbuf,
+               ts_sem, tr_sem, ws_sem, wr_sem, xs_sem, xr_sem, l_sem):
+    t = lax.axis_index("tensor")
+    d = lax.axis_index("dp")
+    rb = tok_ref.shape[1]
+
+    barrier = pltpu.get_barrier_semaphore()
+
+    def greet_t(j, c):
+        pl.semaphore_signal(barrier, inc=1, device_id=(d, (t + j) % nt), device_id_type=MESH)
+        return c
+
+    def greet_d(j, c):
+        pl.semaphore_signal(barrier, inc=1, device_id=((d + j) % nd, t), device_id_type=MESH)
+        return c
+
+    lax.fori_loop(1, nt, greet_t, 0)
+    lax.fori_loop(1, nd, greet_d, 0)
+    pl.semaphore_wait(barrier, nt - 1 + nd - 1)
+
+    c0 = pltpu.make_async_copy(tok_ref, tbuf.at[t], l_sem.at[0])
+    c1 = pltpu.make_async_copy(wcol_ref, wbuf.at[d], l_sem.at[1])
+    c0.start()
+    c1.start()
+
+    def t_copy(p):
+        return pltpu.make_async_remote_copy(
+            src_ref=tok_ref, dst_ref=tbuf.at[t], send_sem=ts_sem.at[p], recv_sem=tr_sem.at[t],
+            device_id=(d, p), device_id_type=MESH)
+
+    def t_recv(p):
+        return pltpu.make_async_remote_copy(
+            src_ref=tok_ref, dst_ref=tbuf.at[p], send_sem=ts_sem.at[p], recv_sem=tr_sem.at[p],
+            device_id=(d, p), device_id_type=MESH)
+
+    def w_copy(p):
+        return pltpu.make_async_remote_copy(
+            src_ref=wcol_ref, dst_ref=wbuf.at[d], send_sem=ws_sem.at[p], recv_sem=wr_sem.at[d],
+            device_id=(p, t), device_id_type=MESH)
+
+    def w_recv(p):
+        return pltpu.make_async_remote_copy(
+            src_ref=wcol_ref, dst_ref=wbuf.at[p], send_sem=ws_sem.at[p], recv_sem=wr_sem.at[p],
+            device_id=(p, t), device_id_type=MESH)
+
+    def send_t(j, c):
+        t_copy((t + j) % nt).start()
+        return c
+
+    def send_d(j, c):
+        w_copy((d + j) % nd).start()
+        return c
+
+    lax.fori_loop(1, nt, send_t, 0)
+    lax.fori_loop(1, nd, send_d, 0)
+
+    def wait_t(j, c):
+        p = (t + j) % nt
+        t_copy(p).wait_send()
+        t_recv(p).wait_recv()
+        return c
+
+    def wait_d(j, c):
+        p = (d + j) % nd
+        w_copy(p).wait_send()
+        w_recv(p).wait_recv()
+        return c
+
+    lax.fori_loop(1, nt, wait_t, 0)
+    lax.fori_loop(1, nd, wait_d, 0)
+    c0.wait()
+    c1.wait()
+
+    per = nt // nd
+    acc = None
+    for q in range(nt):
+        part = jnp.dot(tbuf[q], wbuf[q // per, pl.ds((q % per) * rb, rb), :],
+                       preferred_element_type=jnp.float32)
+        acc = part if acc is None else acc + part
+    xbuf[t] = acc.astype(xbuf.dtype)
+
+    def x_copy(p):
+        return pltpu.make_async_remote_copy(
+            src_ref=xbuf.at[t], dst_ref=xbuf.at[t], send_sem=xs_sem.at[p], recv_sem=xr_sem.at[t],
+            device_id=(d, p), device_id_type=MESH)
+
+    def x_recv(p):
+        return pltpu.make_async_remote_copy(
+            src_ref=xbuf.at[p], dst_ref=xbuf.at[p], send_sem=xs_sem.at[p], recv_sem=xr_sem.at[p],
+            device_id=(d, p), device_id_type=MESH)
+
+    def send_x(j, c):
+        x_copy((t + j) % nt).start()
+        return c
+
+    def wait_x(j, c):
+        p = (t + j) % nt
+        x_copy(p).wait_send()
+        x_recv(p).wait_recv()
+        return c
+
+    lax.fori_loop(1, nt, send_x, 0)
+    lax.fori_loop(1, nt, wait_x, 0)
+    out_ref[...] = xbuf[...]
+
+
+def _tw(tokens, wcol, nt, nd):
+    tok, rb = tokens.shape
+    rows, xw = wcol.shape
+    return pl.pallas_call(
+        functools.partial(_tw_kernel, nt, nd),
+        out_shape=jax.ShapeDtypeStruct((nt, tok, xw), jnp.bfloat16),
+        in_specs=[pl.BlockSpec(memory_space=pltpu.VMEM)] * 2,
+        out_specs=pl.BlockSpec(memory_space=pltpu.VMEM),
+        scratch_shapes=[
+            pltpu.VMEM((nt, tok, rb), jnp.bfloat16),
+            pltpu.VMEM((nd, rows, xw), jnp.bfloat16),
+            pltpu.VMEM((nt, tok, xw), jnp.bfloat16),
+            pltpu.SemaphoreType.DMA((nt,)),
+            pltpu.SemaphoreType.DMA((nt,)),
+            pltpu.SemaphoreType.DMA((nd,)),
+            pltpu.SemaphoreType.DMA((nd,)),
+            pltpu.SemaphoreType.DMA((nt,)),
+            pltpu.SemaphoreType.DMA((nt,)),
+            pltpu.SemaphoreType.DMA((2,)),
+        ],
+        compiler_params=pltpu.CompilerParams(
+            collective_id=1, has_side_effects=True, vmem_limit_bytes=32 * 1024 * 1024),
+        cost_estimate=pl.CostEstimate(
+            flops=2 * tok * rb * nt * xw, transcendentals=0,
+            bytes_accessed=(nt * tok * rb + nd * rows * xw + 2 * nt * tok * xw) * 2),
+    )(tokens, wcol)
+
+
 def on_device(tokens, small_weights, ffn_growth, width_growth):
     n_t = lax.axis_size("tensor")
     n_d = lax.axis_size("dp")
@@ -121,11 +255,8 @@
     rows, ds = width_growth.shape
     xw = ds // n_t
     blk = ds // n_d
-    gathered = lax.all_gather(tokens, "tensor", axis=1, tiled=True)
     w_cols = lax.dynamic_slice_in_dim(width_growth, t * xw, xw, axis=1)
-    w_cols = lax.all_gather(w_cols, "dp", axis=0, tiled=True)
-    tw_part = jnp.dot(gathered, w_cols, preferred_element_type=jnp.float32)
-    tw_t = lax.all_gather(tw_part.astype(jnp.bfloat16).T, "tensor", axis=0, tiled=True)
+    tw_blocks = _tw(tokens, w_cols, n_t, n_d)
     panels = jnp.einsum(
         "msf,cf->msc",
         lax.all_gather(small_weights, "tensor", axis=1, tiled=True),
@@ -134,10 +265,10 @@
     ).astype(jnp.bfloat16)
     w3 = width_growth.reshape(rows, n_d, blk).transpose(1, 0, 2)
     grown_weights, pall = _dp_ring(panels, w3)
-    all_panels = pall.reshape(2, ds, panels.shape[2])
+    all_panels = pall.reshape(2, n_t, xw, panels.shape[2])
     pre_values = jnp.einsum(
-        "st,msc->tmc",
-        tw_t,
+        "kts,mksc->tmc",
+        tw_blocks,
         all_panels,
         preferred_element_type=jnp.float32,
     )

time: 360 us -> 314 us (0.87)
  waiting for transfers between devices: 185 us -> 46.6 us
  Pallas kernels: 113 us -> 208 us
  matrix products: 32.7 us -> 28 us
    pallas_call x0 -> x1, Pallas kernels: none -> 97.1 us  [_tw(): pl.pallas_call(functools.partial(_tw_kernel, nt, nd), out_shape=jax.Shape...]
    all_gather x3 -> x0, waiting for transfers between devices: 85.4 us -> none  [the longest x1 50.4 us: on_device(): gathered = lax.all_gather(tokens, 'tensor', axis=1, tiled=True)]
    all_gather x1, waiting for transfers between devices: 97.7 us -> 45.9 us  [on_device(): lax.all_gather(small_weights, 'tensor', axis=1, tiled=True)]
    dot_general x2 -> x1, matrix products: 12.1 us -> 7.4 us  [on_device(): jnp.einsum('kts,mksc->tmc', tw_blocks, all_panels, preferred_element_type...]
    unnamed x2 -> x4, local copies, waits for them, and re-layouts: 6.77 us -> 8.13 us
  transfers between devices with their start and end apart: 4 -> 1, of which waited for: 3 -> 1; matrix products, arithmetic and copies ran while one was open for 10% -> 4% of each run, Pallas kernels for 31% -> 31%
where the time goes in v3:
time: 314 us; the launch traced here: 313 us
  Pallas kernels  208 us (66%)
  waiting for transfers between devices  46.6 us (15%)
  matrix products  28 us (9%)
  local copies, waits for them, and re-layouts  15.6 us (5%)
  between operations  14.1 us (4%)
    pallas_call x1, Pallas kernels, _dp_ring(): pl.pallas_call(functools.partial(_dp_ring_kernel, n), out_shape=(jax.Shap...  111 us
    pallas_call x1, Pallas kernels, _tw(): pl.pallas_call(functools.partial(_tw_kernel, nt, nd), out_shape=jax.Shape...  97.1 us
    all_gather x1, waiting for transfers between devices, on_device(): lax.all_gather(small_weights, 'tensor', axis=1, tiled=True)  45.9 us
    dot_general x1, matrix products, on_device(): jnp.einsum('msf,cf->msc', lax.all_gather(small_weights, 'tensor', axis=1,...  20.6 us
    unnamed x4, local copies, waits for them, and re-layouts  8.13 us
    dot_general x1, matrix products, on_device(): jnp.einsum('kts,mksc->tmc', tw_blocks, all_panels, preferred_element_type...  7.4 us
    reshape x1, local copies, waits for them, and re-layouts, on_device(): w3 = width_growth.reshape(rows, n_d, blk).transpose(1, 0, 2)  6.29 us
  transfers between devices with their start and end apart: 1, of which 1 were waited for; matrix products, arithmetic and copies ran while one was open for 4% of the time, Pallas kernels for 31%

profile of v3, /device:TPU:6, one launch (start us, length us, event | category | flops | bytes accessed | tf_op | source)
XLA Modules:
  0.0 313.0 jit_solution(17899900325251749305)
XLA Ops:
  7.2 0.0 all-gather.2.cloned.1.call-start
  7.2 0.7 all-gather.2.cloned.1.call-update
  7.9 5.6 %copy.15 = bf16[512,3328]{0,1:T(8,128)(2,1)} copy(bf16[512,3328]{1,0:T(8,128)(2,1)} %param.7) | data formatting | bytes 6815744 | tf_op args[3]
  13.5 0.0 copy-start
  13.5 6.3 %copy.16 = bf16[512,8,416]{2,0,1:T(8,128)(2,1)} copy(bf16[512,8,416]{0,2,1:T(8,128)(2,1)} %bitcast.27) | data formatting | bytes 6815744 | tf_op jit(solution)/shard_map/reshape | solution.py:266
  19.8 1.1 constant_dynamic-slice_fusion.wcol_ref
  20.9 0.0 copy-done
  20.9 97.1 %shard_map.60 = bf16[16,256,208]{2,1,0:T(8,128)(2,1)S(1)} custom-call(bf16[256,256]{1,0:T(8,128)(2,1)S(1)} %copy-done, bf16[512,208]{1,0:T(8,128)(2,1)S(1)} %constant_dynamic-slice_fusion.wcol_ref), custom_call_target="tpu_custom_call" | custom-call | flops 436207616 | bytes 7208960 | tf_op jit(solution)/shard_map/pallas_call | solution.py:226
  118.1 45.9 %all-gather.2.cloned.1.call-done = bf16[2,416,8960]{2,0,1:T(2,128)(2,1)} async-done(((bf16[2,26,8960]{2,0,1:T(2,128)(2,1)}), bf16[2,416,8960]{2,0,1:T(2,128)(2,1)}) %all-gather.2.cloned.1.call-update) | async-done | bytes 14909456 | tf_op jit(solution)/shard_map/all_gather | solution.py:262
  164.0 20.6 %fusion.5.p_ref = bf16[2,416,688]{2,1,0:T(8,128)(2,1)} fusion(bf16[688,8960]{1,0:T(8,128)(2,1)} %param.6, bf16[2,416,8960]{2,0,1:T(2,128)(2,1)} %all-gather.2.cloned.1.call-done), kind=kOutput, calls=%fused_computation.5 | convolution fusion | flops 10258267136 | bytes 28383232 | tf_op jit(solution)/shard_map/msf,cf->msc/dot_general | solution.py:260
  184.6 110.7 %shard_map.59 = (bf16[2,512,688]{2,1,0:T(8,128)(2,1)}, bf16[2,8,416,688]{3,2,1,0:T(8,128)(2,1)}) custom-call(bf16[2,416,688]{2,1,0:T(8,128)(2,1)} %fusion.5.p_ref, bf16[8,512,416]{2,1,0:T(8,128)(2,1)} %bitcast.28), custom_call_target="tpu_custom_call" | custom-call | flops 4689231872 | bytes 18317312 | tf_op jit(solution)/shard_map/pallas_call | solution.py:94
  295.3 2.5 copy.18
  297.8 7.4 %fusion.10 = f32[256,2,688]{0,2,1:T(8,128)S(1)} fusion(bf16[2,16,208,688]{3,2,1,0:T(8,128)(2,1)} %bitcast.29, bf16[16,256,208]{2,1,0:T(8,128)(2,1)S(1)} %shard_map.60), kind=kOutput, calls=%fused_computation.6 | convolution fusion | flops 2344615936 | bytes 12271616 | tf_op jit(solution)/shard_map/kts,mksc->tmc/dot_general | solution.py:269
  305.2 0.9 fusion.14
Async XLA Ops:
  7.2 156.8 %all-gather.2.cloned.1.call-start = ((), (), s32[]{:S(2)}) async-start(), calls=%async_computation | async-start | bytes 15841280 | tf_op jit(solution)/shard_map/all_gather | solution.py:262
  13.5 7.4 %copy-start = (bf16[256,256]{1,0:T(8,128)(2,1)S(1)}, bf16[256,256]{1,0:T(8,128)(2,1)}, u32[]{:S(2)}) copy-start(bf16[256,256]{1,0:T(8,128)(2,1)} %tok_ref.1) | copy-start | bytes 393220
Sparse Core Ops, SparseCore 0:
  10.5 153.4 all-gather.1

commit v4 on v2

v4 whole, which is shorter than its diff:
```python
import functools

import jax
import jax.numpy as jnp
from jax import lax
from jax.experimental import pallas as pl
from jax.experimental.pallas import tpu as pltpu
from jax.sharding import PartitionSpec as P

MESH = pl.DeviceIdType.MESH


def _ring_pos(d):
    h = d // 4
    return h * 7 + (1 - 2 * h) * (d % 4)


def _ring_dev(p):
    h = p // 4
    return h * 4 + h * 3 + (1 - 2 * h) * (p % 4)


def _layer_kernel(n, nt, p_ref, w3_ref, tok_ref, wcol_ref, grown_ref, hid_ref,
                  recv, acc, tbuf, wbuf, xbuf, ssem, rsem,
                  ts_sem, tr_sem, ws_sem, wr_sem, xs_sem, xr_sem, osem):
    t = lax.axis_index("tensor")
    d = lax.axis_index("dp")
    pos = _ring_pos(d)
    right = _ring_dev((pos + 1) % n)
    left = _ring_dev((pos + n - 1) % n)
    rb = tok_ref.shape[1]
    xw = wcol_ref.shape[1]
    blk = p_ref.shape[1]

    barrier = pltpu.get_barrier_semaphore()

    def greet_t(j, c):
        pl.semaphore_signal(barrier, inc=1, device_id=(d, (t + j) % nt), device_id_type=MESH)
        return c

    def greet_d(j, c):
        pl.semaphore_signal(barrier, inc=1, device_id=((d + j) % n, t), device_id_type=MESH)
        return c

    lax.fori_loop(1, nt, greet_t, 0)
    lax.fori_loop(1, n, greet_d, 0)
    pl.semaphore_wait(barrier, nt - 1 + n - 1)

    own = [
        pltpu.make_async_copy(p_ref.at[0], recv.at[0, d], osem.at[0]),
        pltpu.make_async_copy(p_ref.at[1], recv.at[1, d], osem.at[1]),
        pltpu.make_async_copy(tok_ref, tbuf.at[t], osem.at[2]),
        pltpu.make_async_copy(wcol_ref, wbuf.at[d], osem.at[3]),
    ]
    for c in own:
        c.start()

    def t_copy(p):
        return pltpu.make_async_remote_copy(
            src_ref=tok_ref, dst_ref=tbuf.at[t], send_sem=ts_sem.at[p], recv_sem=tr_sem.at[t],
            device_id=(d, p), device_id_type=MESH)

    def t_recv(p):
        return pltpu.make_async_remote_copy(
            src_ref=tok_ref, dst_ref=tbuf.at[p], send_sem=ts_sem.at[p], recv_sem=tr_sem.at[p],
            device_id=(d, p), device_id_type=MESH)

    def w_copy(p):
        return pltpu.make_async_remote_copy(
            src_ref=wcol_ref, dst_ref=wbuf.at[d], send_sem=ws_sem.at[p], recv_sem=wr_sem.at[d],
            device_id=(p, t), device_id_type=MESH)

    def w_recv(p):
        return pltpu.make_async_remote_copy(
            src_ref=wcol_ref, dst_ref=wbuf.at[p], send_sem=ws_sem.at[p], recv_sem=wr_sem.at[p],
            device_id=(p, t), device_id_type=MESH)

    def x_copy(p):
        return pltpu.make_async_remote_copy(
            src_ref=xbuf.at[t], dst_ref=xbuf.at[t], send_sem=xs_sem.at[p], recv_sem=xr_sem.at[t],
            device_id=(d, p), device_id_type=MESH)

    def x_recv(p):
        return pltpu.make_async_remote_copy(
            src_ref=xbuf.at[p], dst_ref=xbuf.at[p], send_sem=xs_sem.at[p], recv_sem=xr_sem.at[p],
            device_id=(d, p), device_id_type=MESH)

    def send_t(j, c):
        t_copy((t + j) % nt).start()
        return c

    def send_d(j, c):
        w_copy((d + j) % n).start()
        return c

    lax.fori_loop(1, nt, send_t, 0)
    lax.fori_loop(1, n, send_d, 0)
    for c in own:
        c.wait()

    def step(k, carry):
        o0 = _ring_dev((pos - k + n) % n)
        o1 = _ring_dev((pos + k) % n)
        c0 = pltpu.make_async_remote_copy(
            src_ref=recv.at[0, o0], dst_ref=recv.at[0, o0],
            send_sem=ssem.at[0, k], recv_sem=rsem.at[0, k],
            device_id=(right, t), device_id_type=MESH)
        c1 = pltpu.make_async_remote_copy(
            src_ref=recv.at[1, o1], dst_ref=recv.at[1, o1],
            send_sem=ssem.at[1, k], recv_sem=rsem.at[1, k],
            device_id=(left, t), device_id_type=MESH)
        c0.start()
        c1.start()
        g0 = jnp.dot(w3_ref[o0], recv[0, o0], preferred_element_type=jnp.float32)
        g1 = jnp.dot(w3_ref[o1], recv[1, o1], preferred_element_type=jnp.float32)

        @pl.when(k == 0)
        def _():
            acc[0] = g0
            acc[1] = g1

        @pl.when(k > 0)
        def _():
            acc[0] += g0
            acc[1] += g1

        c0.wait()
        c1.wait()
        return carry

    lax.fori_loop(0, 1, step, 0)

    def wait_t(j, c):
        p = (t + j) % nt
        t_copy(p).wait_send()
        t_recv(p).wait_recv()
        return c

    def wait_d(j, c):
        p = (d + j) % n
        w_copy(p).wait_send()
        w_recv(p).wait_recv()
        return c

    lax.fori_loop(1, nt, wait_t, 0)
    lax.fori_loop(1, n, wait_d, 0)
    per = nt // n
    tw = None
    for q in range(nt):
        part = jnp.dot(tbuf[q], wbuf[q // per, pl.ds((q % per) * rb, rb), :],
                       preferred_element_type=jnp.float32)
        tw = part if tw is None else tw + part
    xbuf[t] = tw.astype(xbuf.dtype)

    def send_x(j, c):
        x_copy((t + j) % nt).start()
        return c

    lax.fori_loop(1, nt, send_x, 0)
    lax.fori_loop(1, n - 1, step, 0)
    o0 = _ring_dev((pos - (n - 1) + n) % n)
    o1 = _ring_dev((pos + n - 1) % n)
    acc[0] += jnp.dot(w3_ref[o0], recv[0, o0], preferred_element_type=jnp.float32)
    acc[1] += jnp.dot(w3_ref[o1], recv[1, o1], preferred_element_type=jnp.float32)
    grown_ref[...] = acc[...].astype(grown_ref.dtype)

    def wait_x(j, c):
        p = (t + j) % nt
        x_copy(p).wait_send()
        x_recv(p).wait_recv()
        return c

    lax.fori_loop(1, nt, wait_x, 0)
    half = blk // xw
    pre = []
    for m in range(2):
        s = None
        for q in range(nt):
            part = jnp.dot(xbuf[q], recv[m, q // half, pl.ds((q % half) * xw, xw), :],
                           preferred_element_type=jnp.float32)
            s = part if s is None else s + part
        pre.append(s)
    gate = pre[0]
    hid_ref[...] = (gate / (1.0 + jnp.exp(-gate)) * pre[1]).astype(hid_ref.dtype)


def _layer(panels, w3, tokens, wcol, nt):
    n, rows, blk = w3.shape
    _, _, cols = panels.shape
    tok, rb = tokens.shape
    xw = wcol.shape[1]
    flops = 2 * 2 * rows * blk * cols * n + 2 * tok * rb * nt * xw + 2 * 2 * tok * xw * nt * cols
    return pl.pallas_call(
        functools.partial(_layer_kernel, n, nt),
        out_shape=(
            jax.ShapeDtypeStruct((2, rows, cols), jnp.bfloat16),
            jax.ShapeDtypeStruct((tok, cols), jnp.bfloat16),
        ),
        in_specs=[pl.BlockSpec(memory_space=pltpu.VMEM)] * 4,
        out_specs=(pl.BlockSpec(memory_space=pltpu.VMEM), pl.BlockSpec(memory_space=pltpu.VMEM)),
        scratch_shapes=[
            pltpu.VMEM((2, n, blk, cols), jnp.bfloat16),
            pltpu.VMEM((2, rows, cols), jnp.float32),
            pltpu.VMEM((nt, tok, rb), jnp.bfloat16),
            pltpu.VMEM((n, rows, xw), jnp.bfloat16),
            pltpu.VMEM((nt, tok, xw), jnp.bfloat16),
            pltpu.SemaphoreType.DMA((2, n - 1)),
            pltpu.SemaphoreType.DMA((2, n - 1)),
            pltpu.SemaphoreType.DMA((nt,)),
            pltpu.SemaphoreType.DMA((nt,)),
            pltpu.SemaphoreType.DMA((n,)),
            pltpu.SemaphoreType.DMA((n,)),
            pltpu.SemaphoreType.DMA((nt,)),
            pltpu.SemaphoreType.DMA((nt,)),
            pltpu.SemaphoreType.DMA((4,)),
        ],
        compiler_params=pltpu.CompilerParams(
            collective_id=0, has_side_effects=True, vmem_limit_bytes=60 * 1024 * 1024),
        cost_estimate=pl.CostEstimate(
            flops=flops, transcendentals=tok * cols,
            bytes_accessed=2 * 2 * n * blk * cols * 2),
    )(panels, w3, tokens, wcol)


def on_device(tokens, small_weights, ffn_growth, width_growth):
    n_t = lax.axis_size("tensor")
    n_d = lax.axis_size("dp")
    t = lax.axis_index("tensor")
    rows, ds = width_growth.shape
    xw = ds // n_t
    blk = ds // n_d
    w_cols = lax.dynamic_slice_in_dim(width_growth, t * xw, xw, axis=1)
    panels = jnp.einsum(
        "msf,cf->msc",
        lax.all_gather(small_weights, "tensor", axis=1, tiled=True),
        ffn_growth,
        preferred_element_type=jnp.float32,
    ).astype(jnp.bfloat16)
    w3 = width_growth.reshape(rows, n_d, blk).transpose(1, 0, 2)
    grown_weights, hidden = _layer(panels, w3, tokens, w_cols, n_t)
    return (grown_weights, hidden)


def solution(mesh):
    placed = (P("dp", "tensor"), P(None, ("dp", "tensor"), None), P("tensor", None), P("dp", None))
    return jax.shard_map(
        on_device,
        mesh=mesh,
        in_specs=placed,
        out_specs=(P(None, "dp", "tensor"), P("dp", "tensor")),
        check_vma=False,
    )
```

time: 360 us -> 340 us (0.944)
  waiting for transfers between devices: 185 us -> 94.7 us
  Pallas kernels: 113 us -> 190 us
  matrix products: 32.7 us -> 20.6 us
    all_gather x3 -> x0, waiting for transfers between devices: 85.4 us -> none  [the longest x1 50.4 us: on_device(): gathered = lax.all_gather(tokens, 'tensor', axis=1, tiled=True)]
    pallas_call x1, Pallas kernels: 113 us -> 190 us  [_layer(): pl.pallas_call(functools.partial(_layer_kernel, n, nt), out_shape=(jax.Sh...]
    dot_general x2 -> x0, matrix products: 12.1 us -> none  [the longest x1 8.41 us: on_device(): jnp.einsum('st,msc->tmc', tw_t, all_panels, preferred_element_type=jnp.fl...]
    pallas_call x0 -> x2, local copies, waits for them, and re-layouts: none -> 4.42 us  [_layer(): pl.pallas_call(functools.partial(_layer_kernel, n, nt), out_shape=(jax.Sh...]
    all_gather x1, waiting for transfers between devices: 97.7 us -> 94 us  [on_device(): lax.all_gather(small_weights, 'tensor', axis=1, tiled=True)]
  transfers between devices with their start and end apart: 4 -> 1, of which waited for: 3 -> 1; matrix products, arithmetic and copies ran while one was open for 10% -> 3% of each run, Pallas kernels for 31% -> 0%
where the time goes in v4:
time: 340 us; the launch traced here: 335 us
  Pallas kernels  190 us (56%)
  waiting for transfers between devices  94.7 us (28%)
  matrix products  20.6 us (6%)
  local copies, waits for them, and re-layouts  15.1 us (4%)
  between operations  14 us (4%)
    pallas_call x1, Pallas kernels, _layer(): pl.pallas_call(functools.partial(_layer_kernel, n, nt), out_shape=(jax.Sh...  190 us
    all_gather x1, waiting for transfers between devices, on_device(): lax.all_gather(small_weights, 'tensor', axis=1, tiled=True)  94 us
    dot_general x1, matrix products, on_device(): jnp.einsum('msf,cf->msc', lax.all_gather(small_weights, 'tensor', axis=1,...  20.6 us
  transfers between devices with their start and end apart: 1, of which 1 were waited for; matrix products, arithmetic and copies ran while one was open for 3% of the time, Pallas kernels for 0%

profile of v4, /device:TPU:6, one launch (start us, length us, event | category | flops | bytes accessed | tf_op | source)
XLA Modules:
  0.0 334.8 jit_solution(27302884678000658)
XLA Ops:
  7.2 0.0 all-gather.2.cloned.1.call-start
  7.2 0.7 all-gather.2.cloned.1.call-update
  7.9 4.3 %copy.15 = bf16[512,3328]{0,1:T(8,128)(2,1)S(1)} copy(bf16[512,3328]{1,0:T(8,128)(2,1)} %param.7) | data formatting | bytes 6815744 | tf_op args[3]
  12.2 4.6 %copy.16 = bf16[512,8,416]{2,0,1:T(8,128)(2,1)} copy(bf16[512,8,416]{0,2,1:T(8,128)(2,1)S(1)} %bitcast.7) | data formatting | bytes 6815744 | tf_op jit(solution)/shard_map/reshape | solution.py:239
  16.8 1.8 constant_dynamic-slice_fusion.wcol_ref
  18.6 94.0 %all-gather.2.cloned.1.call-done = bf16[2,416,8960]{2,0,1:T(2,128)(2,1)} async-done(((bf16[2,26,8960]{2,0,1:T(2,128)(2,1)}), bf16[2,416,8960]{2,0,1:T(2,128)(2,1)}) %all-gather.2.cloned.1.call-update) | async-done | bytes 14909456 | tf_op jit(solution)/shard_map/all_gather | solution.py:235
  112.6 20.6 %fusion.3.p_ref = bf16[2,416,688]{2,1,0:T(8,128)(2,1)} fusion(bf16[688,8960]{1,0:T(8,128)(2,1)} %param.6, bf16[2,416,8960]{2,0,1:T(2,128)(2,1)} %all-gather.2.cloned.1.call-done), kind=kOutput, calls=%fused_computation.3 | convolution fusion | flops 10258267136 | bytes 28383232 | tf_op jit(solution)/shard_map/msf,cf->msc/dot_general | solution.py:233
  133.2 190.3 %shard_map.59 = (bf16[2,512,688]{2,1,0:T(8,128)(2,1)}, bf16[256,688]{1,0:T(8,128)(2,1)}) custom-call(bf16[2,416,688]{2,1,0:T(8,128)(2,1)} %fusion.3.p_ref, bf16[8,512,416]{2,1,0:T(8,128)(2,1)} %bitcast.8, bf16[256,256]{1,0:T(8,128)(2,1)} %tok_ref.1, bf16[512,208]{1,0:T(8,128)(2,1)} %constant_dynamic-slice_fusion.wcol_ref), custom_call_target="tpu_custom_call" | custom-call | flops 7470055424 | bytes 18317312 | tf_op jit(solution)/shard_map/pallas_call | solution.py:193
  323.6 2.5 copy.17
  326.1 1.9 copy.18
Async XLA Ops:
  7.2 105.5 %all-gather.2.cloned.1.call-start = ((), (), s32[]{:S(2)}) async-start(), calls=%async_computation | async-start | bytes 15841280 | tf_op jit(solution)/shard_map/all_gather | solution.py:235
Sparse Core Ops, SparseCore 0:
  10.5 102.0 all-gather.1

commit v5 on v3

--- a/solution.py
+++ b/solution.py
@@ -40,7 +40,7 @@
     for c in own:
         c.wait()
     for m in range(2):
-        pltpu.make_async_copy(recv.at[m, d], pall_ref.at[m, d], lsem.at[m, d]).start()
+        pltpu.make_async_copy(recv.at[m, d], pall_ref.at[d, m], lsem.at[m, d]).start()
 
     def step(k, carry):
         o0 = _ring_dev((pos - k + n) % n)
@@ -55,63 +55,61 @@
             device_id=(left, t), device_id_type=MESH)
         c0.start()
         c1.start()
-        g0 = jnp.dot(w3_ref[o0], recv[0, o0], preferred_element_type=jnp.float32)
-        g1 = jnp.dot(w3_ref[o1], recv[1, o1], preferred_element_type=jnp.float32)
+        g0 = jnp.dot(w3_ref[o0, 0], recv[0, o0], preferred_element_type=jnp.float32)
+        g1 = jnp.dot(w3_ref[o1, 1], recv[1, o1], preferred_element_type=jnp.float32)
 
         @pl.when(k == 0)
         def _():
-            acc[0] = g0
-            acc[1] = g1
+            acc[...] = g0 + g1
 
         @pl.when(k > 0)
         def _():
-            acc[0] += g0
-            acc[1] += g1
+            acc[...] += g0 + g1
 
         c0.wait()
         c1.wait()
         n0 = _ring_dev((pos - k - 1 + n) % n)
         n1 = _ring_dev((pos + k + 1) % n)
-        pltpu.make_async_copy(recv.at[0, n0], pall_ref.at[0, n0], lsem.at[0, n0]).start()
-        pltpu.make_async_copy(recv.at[1, n1], pall_ref.at[1, n1], lsem.at[1, n1]).start()
+        pltpu.make_async_copy(recv.at[0, n0], pall_ref.at[n0, 0], lsem.at[0, n0]).start()
+        pltpu.make_async_copy(recv.at[1, n1], pall_ref.at[n1, 1], lsem.at[1, n1]).start()
         return carry
 
     lax.fori_loop(0, n - 1, step, 0)
     o0 = _ring_dev((pos - (n - 1) + n) % n)
     o1 = _ring_dev((pos + n - 1) % n)
-    acc[0] += jnp.dot(w3_ref[o0], recv[0, o0], preferred_element_type=jnp.float32)
-    acc[1] += jnp.dot(w3_ref[o1], recv[1, o1], preferred_element_type=jnp.float32)
+    acc[...] += (jnp.dot(w3_ref[o0, 0], recv[0, o0], preferred_element_type=jnp.float32)
+                 + jnp.dot(w3_ref[o1, 1], recv[1, o1], preferred_element_type=jnp.float32))
     grown_ref[...] = acc[...].astype(grown_ref.dtype)
     for m in range(2):
         for o in range(n):
-            pltpu.make_async_copy(recv.at[m, o], pall_ref.at[m, o], lsem.at[m, o]).wait()
-
-
-def _dp_ring(panels, w3):
-    n, rows, blk = w3.shape
+            pltpu.make_async_copy(recv.at[m, o], pall_ref.at[o, m], lsem.at[m, o]).wait()
+
+
+def _dp_ring(panels, w3h, cid):
+    n, _, rows, hb = w3h.shape
     _, _, cols = panels.shape
-    flops = 2 * 2 * rows * blk * cols * n
+    flops = 2 * 2 * rows * hb * cols * n
     return pl.pallas_call(
         functools.partial(_dp_ring_kernel, n),
         out_shape=(
-            jax.ShapeDtypeStruct((2, rows, cols), jnp.bfloat16),
-            jax.ShapeDtypeStruct((2, n, blk, cols), jnp.bfloat16),
+            jax.ShapeDtypeStruct((rows, cols), jnp.bfloat16),
+            jax.ShapeDtypeStruct((n, 2, hb, cols), jnp.bfloat16),
         ),
         in_specs=[pl.BlockSpec(memory_space=pltpu.VMEM)] * 2,
         out_specs=(pl.BlockSpec(memory_space=pltpu.VMEM), pl.BlockSpec(memory_space=pl.ANY)),
         scratch_shapes=[
-            pltpu.VMEM((2, n, blk, cols), jnp.bfloat16),
-            pltpu.VMEM((2, rows, cols), jnp.float32),
+            pltpu.VMEM((2, n, hb, cols), jnp.bfloat16),
+            pltpu.VMEM((rows, cols), jnp.float32),
             pltpu.SemaphoreType.DMA((2, n - 1)),
             pltpu.SemaphoreType.DMA((2, n - 1)),
             pltpu.SemaphoreType.DMA((2, n)),
             pltpu.SemaphoreType.DMA((2,)),
         ],
         compiler_params=pltpu.CompilerParams(
-            collective_id=0, has_side_effects=True, vmem_limit_bytes=56 * 1024 * 1024),
+            collective_id=cid, has_side_effects=True, vmem_limit_bytes=48 * 1024 * 1024),
         cost_estimate=pl.CostEstimate(
-            flops=flops, transcendentals=0, bytes_accessed=2 * 2 * n * blk * cols * 2),
-    )(panels, w3)
+            flops=flops, transcendentals=0, bytes_accessed=2 * n * 2 * hb * cols * 2),
+    )(panels, w3h)
 
 
 def _tw_kernel(nt, nd, tok_ref, wcol_ref, out_ref, tbuf, wbuf, xbuf,
@@ -241,10 +239,10 @@
             pltpu.SemaphoreType.DMA((2,)),
         ],
         compiler_params=pltpu.CompilerParams(
-            collective_id=1, has_side_effects=True, vmem_limit_bytes=32 * 1024 * 1024),
+            collective_id=2, has_side_effects=True, vmem_limit_bytes=32 * 1024 * 1024),
         cost_estimate=pl.CostEstimate(
             flops=2 * tok * rb * nt * xw, transcendentals=0,
-            bytes_accessed=(nt * tok * rb + nd * rows * xw + 2 * nt * tok * xw) * 2),
+            bytes_accessed=(nt * tok * rb + nd * rows * xw + 2 * nt * tok * xw) * 2 * 64),
     )(tokens, wcol)
 
 
@@ -257,15 +255,22 @@
     blk = ds // n_d
     w_cols = lax.dynamic_slice_in_dim(width_growth, t * xw, xw, axis=1)
     tw_blocks = _tw(tokens, w_cols, n_t, n_d)
-    panels = jnp.einsum(
-        "msf,cf->msc",
-        lax.all_gather(small_weights, "tensor", axis=1, tiled=True),
-        ffn_growth,
-        preferred_element_type=jnp.float32,
-    ).astype(jnp.bfloat16)
-    w3 = width_growth.reshape(rows, n_d, blk).transpose(1, 0, 2)
-    grown_weights, pall = _dp_ring(panels, w3)
-    all_panels = pall.reshape(2, n_t, xw, panels.shape[2])
+    hb = blk // 2
+    w3h = width_growth.reshape(rows, n_d, 2, hb).transpose(1, 2, 0, 3)
+    grown = []
+    parts = []
+    panels = tw_blocks
+    for m in range(2):
+        panels, sw = lax.optimization_barrier((panels, small_weights[m]))
+        if not m:
+            tw_blocks = panels
+        s_rows = lax.all_gather(sw, "tensor", axis=0, tiled=True)
+        panels = jnp.dot(s_rows, ffn_growth.T, preferred_element_type=jnp.float32).astype(jnp.bfloat16)
+        g, pall = _dp_ring(panels.reshape(2, hb, panels.shape[1]), w3h, m)
+        grown.append(g)
+        parts.append(pall.reshape(n_t, xw, panels.shape[1]))
+    grown_weights = jnp.stack(grown)
+    all_panels = jnp.stack(parts)
     pre_values = jnp.einsum(
         "kts,mksc->tmc",
         tw_blocks,

time: 314 us -> 394 us (1.25)
  waiting for transfers between devices: 46.6 us -> 77.9 us
  local copies, waits for them, and re-layouts: 15.6 us -> 39.2 us
  Pallas kernels: 208 us -> 225 us
  matrix products: 28 us -> 34.1 us
    all_gather x1 -> x2, waiting for transfers between devices: 45.9 us -> 77.9 us  [on_device(): s_rows = lax.all_gather(sw, 'tensor', axis=0, tiled=True)]
    pallas_call x1 -> x2, Pallas kernels: 111 us -> 141 us  [_dp_ring(): pl.pallas_call(functools.partial(_dp_ring_kernel, n), out_shape=(jax.Shap...]
    unnamed x4 -> x12, local copies, waits for them, and re-layouts: 8.13 us -> 28.6 us
    pallas_call x1, Pallas kernels: 97.1 us -> 83.8 us  [_tw(): pl.pallas_call(functools.partial(_tw_kernel, nt, nd), out_shape=jax.Shape...]
    dot_general x1 -> x2, matrix products: 20.6 us -> 26.3 us  [on_device(): jnp.dot(s_rows, ffn_growth.T, preferred_element_type=jnp.float32)]
  transfers between devices with their start and end apart: 1 -> 2, of which waited for: 1 -> 1; matrix products, arithmetic and copies ran while one was open for 4% -> 3% of each run, Pallas kernels for 31% -> 21%
where the time goes in v5:
time: 394 us; the launch traced here: 393 us
  Pallas kernels  225 us (57%)
  waiting for transfers between devices  77.9 us (20%)
  local copies, waits for them, and re-layouts  39.2 us (10%)
  matrix products  34.1 us (9%)
  between operations  14.1 us (4%)
    pallas_call x2, Pallas kernels, _dp_ring(): pl.pallas_call(functools.partial(_dp_ring_kernel, n), out_shape=(jax.Shap...  141 us
    pallas_call x1, Pallas kernels, _tw(): pl.pallas_call(functools.partial(_tw_kernel, nt, nd), out_shape=jax.Shape...  83.8 us
    all_gather x2, waiting for transfers between devices, on_device(): s_rows = lax.all_gather(sw, 'tensor', axis=0, tiled=True)  77.9 us
    unnamed x12, local copies, waits for them, and re-layouts  28.6 us
    dot_general x2, matrix products, on_device(): jnp.dot(s_rows, ffn_growth.T, preferred_element_type=jnp.float32)  26.3 us
  transfers between devices with their start and end apart: 2, of which 1 were waited for; matrix products, arithmetic and copies ran while one was open for 3% of the time, Pallas kernels for 21%

profile of v5, /device:TPU:6, one launch (start us, length us, event | category | flops | bytes accessed | tf_op | source)
XLA Modules:
  0.0 392.6 jit_solution(654761070258506813)
XLA Ops:
  7.2 0.0 all-gather.5.cloned.1.call-start
  7.2 3.1 fusion.13
  10.3 0.9 copy.28
  11.2 1.1 constant_dynamic-slice_fusion.wcol_ref
  12.4 0.0 copy-start.2
  12.4 0.9 copy-done.2
  13.3 83.8 %shard_map.59 = bf16[16,256,208]{2,1,0:T(8,128)(2,1)S(1)} custom-call(bf16[256,256]{1,0:T(8,128)(2,1)S(1)} %copy-done.2, bf16[512,208]{1,0:T(8,128)(2,1)S(1)} %constant_dynamic-slice_fusion.wcol_ref), custom_call_target="tpu_custom_call" | custom-call | flops 436207616 | bytes 461373440 | tf_op jit(solution)/shard_map/pallas_call | solution.py:224
  97.0 0.0 all-gather.5.cloned.1.call-update
  97.1 0.2 all-gather.7.cloned.1.call-start
  97.3 0.9 copy.27
  98.2 77.9 %all-gather.5.cloned.1.call-done = bf16[16,26,8960]{2,1,0:T(8,128)(2,1)} async-done(((bf16[1,26,8960]{2,1,0:T(8,128)(2,1)}), bf16[16,26,8960]{2,1,0:T(8,128)(2,1)}) %all-gather.5.cloned.1.call-update) | async-done | bytes 7454736 | tf_op jit(solution)/shard_map/all_gather | solution.py:267
  176.0 7.8 %reshape.17 = bf16[416,8960]{1,0:T(8,128)(2,1)} reshape(bf16[16,26,8960]{2,1,0:T(8,128)(2,1)} %all-gather.5.cloned.1.call-done) | data formatting | bytes 14909440
  183.9 13.1 %convolution_convert_fusion.1 = bf16[416,688]{1,0:T(8,128)(2,1)S(1)} fusion(bf16[416,8960]{1,0:T(8,128)(2,1)} %reshape.17, bf16[688,8960]{1,0:T(8,128)(2,1)} %param.6), kind=kOutput, calls=%fused_computation.8 | convolution fusion | flops 5129133568 | bytes 20356096 | tf_op jit(solution)/shard_map/dot_general | solution.py:268
  197.0 0.0 all-gather.7.cloned.1.call-update
  197.0 5.6 %copy.15 = bf16[512,3328]{0,1:T(8,128)(2,1)} copy(bf16[512,3328]{1,0:T(8,128)(2,1)} %param.7) | data formatting | bytes 6815744 | tf_op args[3]
  202.5 6.3 %copy.16 = bf16[512,8,2,208]{3,0,2,1:T(8,128)(2,1)} copy(bf16[512,8,2,208]{0,3,2,1:T(8,128)(2,1)} %bitcast.44) | data formatting | bytes 6815744 | tf_op jit(solution)/shard_map/reshape | solution.py:259
  208.9 0.0 copy-start
  208.9 2.2 copy-done
  211.0 81.8 %shard_map.60 = (bf16[512,688]{1,0:T(8,128)(2,1)S(1)}, bf16[8,2,208,688]{3,2,1,0:T(8,128)(2,1)}) custom-call(bf16[2,208,688]{2,1,0:T(8,128)(2,1)S(1)} %bitcast.42, bf16[8,2,512,208]{3,2,1,0:T(8,128)(2,1)S(1)} %bitcast.38), custom_call_target="tpu_custom_call" | custom-call | flops 2344615936 | bytes 9158656 | tf_op jit(solution)/shard_map/pallas_call | solution.py:92
  292.9 0.0 all-gather.7.cloned.1.call-done
  292.9 7.8 %reshape.19 = bf16[416,8960]{1,0:T(8,128)(2,1)} reshape(bf16[16,26,8960]{2,1,0:T(8,128)(2,1)} %all-gather.7.cloned.1.call-done) | data formatting | bytes 14909440
  300.8 0.0 copy-start.1
  300.8 13.2 %convolution_convert_fusion = bf16[416,688]{1,0:T(8,128)(2,1)S(1)} fusion(bf16[416,8960]{1,0:T(8,128)(2,1)} %reshape.19, bf16[688,8960]{1,0:T(8,128)(2,1)} %param.6), kind=kOutput, calls=%fused_computation.7 | convolution fusion | flops 5129133568 | bytes 20356096 | tf_op jit(solution)/shard_map/dot_general | solution.py:268
  314.0 0.0 copy-done.1
  314.0 59.1 %shard_map.61 = (bf16[512,688]{1,0:T(8,128)(2,1)S(1)}, bf16[8,2,208,688]{3,2,1,0:T(8,128)(2,1)}) custom-call(bf16[2,208,688]{2,1,0:T(8,128)(2,1)S(1)} %bitcast.43, bf16[8,2,512,208]{3,2,1,0:T(8,128)(2,1)S(1)} %bitcast.39), custom_call_target="tpu_custom_call" | custom-call | flops 2344615936 | bytes 9158656 | tf_op jit(solution)/shard_map/pallas_call | solution.py:92
  373.1 1.4 pad_maximum_fusion
  374.4 2.5 copy.19
  376.9 7.8 %fusion.5 = f32[256,2,688]{0,2,1:T(8,128)S(1)} fusion(bf16[1,16,208,688]{3,2,1,0:T(8,128)(2,1)} %bitcast.46, bf16[1,16,208,688]{3,2,1,0:T(8,128)(2,1)} %bitcast.45, bf16[16,256,208]{2,1,0:T(8,128)(2,1)S(1)} %shard_map.59), kind=kOutput, calls=%fused_computation.6 | convolution fusion | flops 2362933248 | bytes 12271616 | tf_op jit(solution)/shard_map/kts,mksc->tmc/dot_general | solution.py:274
  384.8 0.9 fusion.11
Async XLA Ops:
  7.2 168.9 %all-gather.5.cloned.1.call-start = ((), (), s32[]{:S(2)}) async-start(), calls=%async_computation | async-start | bytes 9748480 | tf_op jit(solution)/shard_map/all_gather | solution.py:267
  12.4 0.9 copy-start.2
  97.1 195.8 %all-gather.7.cloned.1.call-start = ((), (), s32[]{:S(2)}) async-start(), calls=%async_computation.1 | async-start | bytes 9748480 | tf_op jit(solution)/shard_map/all_gather | solution.py:267
  208.9 2.2 copy-start
  300.8 13.2 %copy-start.1 = (bf16[512,8,2,208]{3,0,2,1:T(8,128)(2,1)S(1)}, bf16[512,8,2,208]{3,0,2,1:T(8,128)(2,1)}, u32[]{:S(2)}) copy-start(bf16[512,8,2,208]{3,0,2,1:T(8,128)(2,1)} %copy.16) | copy-start | bytes 10223620
Sparse Core Ops, SparseCore 0:
  97.2 78.8 all-gather.4
  197.1 95.5 all-gather.6

commit v6 on v3

--- a/solution.py
+++ b/solution.py
@@ -20,12 +20,15 @@
     return h * 4 + h * 3 + (1 - 2 * h) * (p % 4)
 
 
-def _dp_ring_kernel(n, p_ref, w3_ref, grown_ref, pall_ref, recv, acc, ssem, rsem, lsem, osem):
+def _dp_ring_kernel(n, p_ref, w3_ref, tw_ref, grown_ref, hid_ref, recv, acc, pre, ssem, rsem, osem):
     t = lax.axis_index("tensor")
     d = lax.axis_index("dp")
     pos = _ring_pos(d)
     right = _ring_dev((pos + 1) % n)
     left = _ring_dev((pos + n - 1) % n)
+    blk = p_ref.shape[1]
+    xw = tw_ref.shape[2]
+    per = blk // xw
 
     barrier = pltpu.get_barrier_semaphore()
     for nb in (left, right):
@@ -39,8 +42,15 @@
         own.append(c)
     for c in own:
         c.wait()
-    for m in range(2):
-        pltpu.make_async_copy(recv.at[m, d], pall_ref.at[m, d], lsem.at[m, d]).start()
+
+    def contrib(m, o):
+        g = jnp.dot(w3_ref[o], recv[m, o], preferred_element_type=jnp.float32)
+        h = None
+        for q in range(per):
+            part = jnp.dot(tw_ref[per * o + q], recv[m, o, pl.ds(q * xw, xw), :],
+                           preferred_element_type=jnp.float32)
+            h = part if h is None else h + part
+        return g, h
 
     def step(k, carry):
         o0 = _ring_dev((pos - k + n) % n)
@@ -55,63 +65,66 @@
             device_id=(left, t), device_id_type=MESH)
         c0.start()
         c1.start()
-        g0 = jnp.dot(w3_ref[o0], recv[0, o0], preferred_element_type=jnp.float32)
-        g1 = jnp.dot(w3_ref[o1], recv[1, o1], preferred_element_type=jnp.float32)
+        g0, h0 = contrib(0, o0)
+        g1, h1 = contrib(1, o1)
 
         @pl.when(k == 0)
         def _():
             acc[0] = g0
             acc[1] = g1
+            pre[0] = h0
+            pre[1] = h1
 
         @pl.when(k > 0)
         def _():
             acc[0] += g0
             acc[1] += g1
+            pre[0] += h0
+            pre[1] += h1
 
         c0.wait()
         c1.wait()
-        n0 = _ring_dev((pos - k - 1 + n) % n)
-        n1 = _ring_dev((pos + k + 1) % n)
-        pltpu.make_async_copy(recv.at[0, n0], pall_ref.at[0, n0], lsem.at[0, n0]).start()
-        pltpu.make_async_copy(recv.at[1, n1], pall_ref.at[1, n1], lsem.at[1, n1]).start()
         return carry
 
     lax.fori_loop(0, n - 1, step, 0)
     o0 = _ring_dev((pos - (n - 1) + n) % n)
     o1 = _ring_dev((pos + n - 1) % n)
-    acc[0] += jnp.dot(w3_ref[o0], recv[0, o0], preferred_element_type=jnp.float32)
-    acc[1] += jnp.dot(w3_ref[o1], recv[1, o1], preferred_element_type=jnp.float32)
+    g0, h0 = contrib(0, o0)
+    g1, h1 = contrib(1, o1)
+    acc[0] += g0
+    acc[1] += g1
     grown_ref[...] = acc[...].astype(grown_ref.dtype)
-    for m in range(2):
-        for o in range(n):
-            pltpu.make_async_copy(recv.at[m, o], pall_ref.at[m, o], lsem.at[m, o]).wait()
-
-
-def _dp_ring(panels, w3):
+    gate = pre[0] + h0
+    up = pre[1] + h1
+    hid_ref[...] = (gate / (1.0 + jnp.exp(-gate)) * up).astype(hid_ref.dtype)
+
+
+def _dp_ring(panels, w3, tw_blocks):
     n, rows, blk = w3.shape
     _, _, cols = panels.shape
-    flops = 2 * 2 * rows * blk * cols * n
+    nt, tok, xw = tw_blocks.shape
+    flops = 2 * 2 * rows * blk * cols * n + 2 * 2 * tok * xw * nt * cols
     return pl.pallas_call(
         functools.partial(_dp_ring_kernel, n),
         out_shape=(
             jax.ShapeDtypeStruct((2, rows, cols), jnp.bfloat16),
-            jax.ShapeDtypeStruct((2, n, blk, cols), jnp.bfloat16),
+            jax.ShapeDtypeStruct((tok, cols), jnp.bfloat16),
         ),
-        in_specs=[pl.BlockSpec(memory_space=pltpu.VMEM)] * 2,
-        out_specs=(pl.BlockSpec(memory_space=pltpu.VMEM), pl.BlockSpec(memory_space=pl.ANY)),
+        in_specs=[pl.BlockSpec(memory_space=pltpu.VMEM)] * 3,
+        out_specs=(pl.BlockSpec(memory_space=pltpu.VMEM), pl.BlockSpec(memory_space=pltpu.VMEM)),
         scratch_shapes=[
             pltpu.VMEM((2, n, blk, cols), jnp.bfloat16),
             pltpu.VMEM((2, rows, cols), jnp.float32),
+            pltpu.VMEM((2, tok, cols), jnp.float32),
             pltpu.SemaphoreType.DMA((2, n - 1)),
             pltpu.SemaphoreType.DMA((2, n - 1)),
-            pltpu.SemaphoreType.DMA((2, n)),
             pltpu.SemaphoreType.DMA((2,)),
         ],
         compiler_params=pltpu.CompilerParams(
             collective_id=0, has_side_effects=True, vmem_limit_bytes=56 * 1024 * 1024),
         cost_estimate=pl.CostEstimate(
-            flops=flops, transcendentals=0, bytes_accessed=2 * 2 * n * blk * cols * 2),
-    )(panels, w3)
+            flops=flops, transcendentals=tok * cols, bytes_accessed=2 * 2 * n * blk * cols * 2),
+    )(panels, w3, tw_blocks)
 
 
 def _tw_kernel(nt, nd, tok_ref, wcol_ref, out_ref, tbuf, wbuf, xbuf,
@@ -264,15 +277,7 @@
         preferred_element_type=jnp.float32,
     ).astype(jnp.bfloat16)
     w3 = width_growth.reshape(rows, n_d, blk).transpose(1, 0, 2)
-    grown_weights, pall = _dp_ring(panels, w3)
-    all_panels = pall.reshape(2, n_t, xw, panels.shape[2])
-    pre_values = jnp.einsum(
-        "kts,mksc->tmc",
-        tw_blocks,
-        all_panels,
-        preferred_element_type=jnp.float32,
-    )
-    hidden = (jax.nn.silu(pre_values[:, 0, :]) * pre_values[:, 1, :]).astype(jnp.bfloat16)
+    grown_weights, hidden = _dp_ring(panels, w3, tw_blocks)
     return (grown_weights, hidden)
 
 

time: 314 us -> 306 us (0.975)
  matrix products: 28 us -> 20.6 us
    dot_general x1 -> x0, matrix products: 7.4 us -> none  [on_device(): jnp.einsum('kts,mksc->tmc', tw_blocks, all_panels, preferred_element_type...]
    pallas_call x1, Pallas kernels: 97.1 us -> 102 us  [_tw(): pl.pallas_call(functools.partial(_tw_kernel, nt, nd), out_shape=jax.Shape...]
    pallas_call x0 -> x2, local copies, waits for them, and re-layouts: none -> 4.42 us  [_dp_ring(): pl.pallas_call(functools.partial(_dp_ring_kernel, n), out_shape=(jax.Shap...]
    unnamed x4 -> x5, local copies, waits for them, and re-layouts: 8.13 us -> 5.57 us
  transfers between devices with their start and end apart: 1 -> 1, of which waited for: 1 -> 1; matrix products, arithmetic and copies ran while one was open for 4% -> 3% of each run, Pallas kernels for 31% -> 34%
where the time goes in v6:
time: 306 us; the launch traced here: 304 us
  Pallas kernels  210 us (69%)
  waiting for transfers between devices  43.7 us (14%)
  matrix products  20.6 us (7%)
  local copies, waits for them, and re-layouts  15.7 us (5%)
  between operations  14.1 us (5%)
    pallas_call x1, Pallas kernels, _dp_ring(): pl.pallas_call(functools.partial(_dp_ring_kernel, n), out_shape=(jax.Shap...  108 us
    pallas_call x1, Pallas kernels, _tw(): pl.pallas_call(functools.partial(_tw_kernel, nt, nd), out_shape=jax.Shape...  102 us
    all_gather x1, waiting for transfers between devices, on_device(): lax.all_gather(small_weights, 'tensor', axis=1, tiled=True)  43 us
    dot_general x1, matrix products, on_device(): jnp.einsum('msf,cf->msc', lax.all_gather(small_weights, 'tensor', axis=1,...  20.6 us
  transfers between devices with their start and end apart: 1, of which 1 were waited for; matrix products, arithmetic and copies ran while one was open for 3% of the time, Pallas kernels for 34%

profile of v6, /device:TPU:6, one launch (start us, length us, event | category | flops | bytes accessed | tf_op | source)
XLA Modules:
  0.0 304.1 jit_solution(16851159085950188421)
XLA Ops:
  7.2 0.0 all-gather.2.cloned.1.call-start
  7.2 0.7 all-gather.2.cloned.1.call-update
  7.9 4.3 %copy.15 = bf16[512,3328]{0,1:T(8,128)(2,1)S(1)} copy(bf16[512,3328]{1,0:T(8,128)(2,1)} %param.7) | data formatting | bytes 6815744 | tf_op args[3]
  12.2 0.0 copy-start.1
  12.2 4.6 %copy.16 = bf16[512,8,416]{2,0,1:T(8,128)(2,1)} copy(bf16[512,8,416]{0,2,1:T(8,128)(2,1)S(1)} %bitcast.7) | data formatting | bytes 6815744 | tf_op jit(solution)/shard_map/reshape | solution.py:279
  16.8 1.1 constant_dynamic-slice_fusion.wcol_ref
  17.9 0.0 copy-done.1
  17.9 101.9 %shard_map.59.tw_ref = bf16[16,256,208]{2,1,0:T(8,128)(2,1)S(1)} custom-call(bf16[256,256]{1,0:T(8,128)(2,1)S(1)} %copy-done.1, bf16[512,208]{1,0:T(8,128)(2,1)S(1)} %constant_dynamic-slice_fusion.wcol_ref), custom_call_target="tpu_custom_call" | custom-call | flops 436207616 | bytes 7208960 | tf_op jit(solution)/shard_map/pallas_call | solution.py:239
  119.8 0.0 copy-start
  119.8 1.3 copy-done
  121.1 43.0 %all-gather.2.cloned.1.call-done = bf16[2,416,8960]{2,0,1:T(2,128)(2,1)} async-done(((bf16[2,26,8960]{2,0,1:T(2,128)(2,1)}), bf16[2,416,8960]{2,0,1:T(2,128)(2,1)}) %all-gather.2.cloned.1.call-update) | async-done | bytes 14909456 | tf_op jit(solution)/shard_map/all_gather | solution.py:275
  164.2 20.6 %fusion.3.p_ref = bf16[2,416,688]{2,1,0:T(8,128)(2,1)} fusion(bf16[688,8960]{1,0:T(8,128)(2,1)} %param.6, bf16[2,416,8960]{2,0,1:T(2,128)(2,1)} %all-gather.2.cloned.1.call-done), kind=kOutput, calls=%fused_computation.3 | convolution fusion | flops 10258267136 | bytes 28383232 | tf_op jit(solution)/shard_map/msf,cf->msc/dot_general | solution.py:273
  184.8 108.1 %shard_map.60 = (bf16[2,512,688]{2,1,0:T(8,128)(2,1)}, bf16[256,688]{1,0:T(8,128)(2,1)}) custom-call(bf16[2,416,688]{2,1,0:T(8,128)(2,1)} %fusion.3.p_ref, bf16[8,512,416]{2,1,0:T(8,128)(2,1)} %bitcast.8, bf16[16,256,208]{2,1,0:T(8,128)(2,1)} %copy-done), custom_call_target="tpu_custom_call" | custom-call | flops 7033847808 | bytes 18317312 | tf_op jit(solution)/shard_map/pallas_call | solution.py:107
  292.8 2.5 copy.17
  295.4 1.9 copy.18
Async XLA Ops:
  7.2 157.0 %all-gather.2.cloned.1.call-start = ((), (), s32[]{:S(2)}) async-start(), calls=%async_computation | async-start | bytes 15841280 | tf_op jit(solution)/shard_map/all_gather | solution.py:275
  12.2 5.8 %copy-start.1 = (bf16[256,256]{1,0:T(8,128)(2,1)S(1)}, bf16[256,256]{1,0:T(8,128)(2,1)}, u32[]{:S(2)}) copy-start(bf16[256,256]{1,0:T(8,128)(2,1)} %tok_ref.1) | copy-start | bytes 393220
  119.8 1.3 copy-start
Sparse Core Ops, SparseCore 0:
  10.5 153.5 all-gather.1

commit v7 on v6

--- a/solution.py
+++ b/solution.py
@@ -5,9 +5,17 @@
 from jax import lax
 from jax.experimental import pallas as pl
 from jax.experimental.pallas import tpu as pltpu
-from jax.sharding import PartitionSpec as P
+from jax.sharding import Mesh, PartitionSpec as P
 
 MESH = pl.DeviceIdType.MESH
+
+
+def _tidx():
+    return lax.axis_index("tp") * 2 + lax.axis_index("core")
+
+
+def _dev(d, t):
+    return (d, t // 2, t % 2)
 
 
 def _ring_pos(d):
@@ -21,7 +29,7 @@
 
 
 def _dp_ring_kernel(n, p_ref, w3_ref, tw_ref, grown_ref, hid_ref, recv, acc, pre, ssem, rsem, osem):
-    t = lax.axis_index("tensor")
+    t = _tidx()
     d = lax.axis_index("dp")
     pos = _ring_pos(d)
     right = _ring_dev((pos + 1) % n)
@@ -32,7 +40,7 @@
 
     barrier = pltpu.get_barrier_semaphore()
     for nb in (left, right):
-        pl.semaphore_signal(barrier, inc=1, device_id=(nb, t), device_id_type=MESH)
+        pl.semaphore_signal(barrier, inc=1, device_id=_dev(nb, t), device_id_type=MESH)
     pl.semaphore_wait(barrier, 2)
 
     own = []
@@ -58,11 +66,11 @@
         c0 = pltpu.make_async_remote_copy(
             src_ref=recv.at[0, o0], dst_ref=recv.at[0, o0],
             send_sem=ssem.at[0, k], recv_sem=rsem.at[0, k],
-            device_id=(right, t), device_id_type=MESH)
+            device_id=_dev(right, t), device_id_type=MESH)
         c1 = pltpu.make_async_remote_copy(
             src_ref=recv.at[1, o1], dst_ref=recv.at[1, o1],
             send_sem=ssem.at[1, k], recv_sem=rsem.at[1, k],
-            device_id=(left, t), device_id_type=MESH)
+            device_id=_dev(left, t), device_id_type=MESH)
         c0.start()
         c1.start()
         g0, h0 = contrib(0, o0)
@@ -129,18 +137,18 @@
 
 def _tw_kernel(nt, nd, tok_ref, wcol_ref, out_ref, tbuf, wbuf, xbuf,
                ts_sem, tr_sem, ws_sem, wr_sem, xs_sem, xr_sem, l_sem):
-    t = lax.axis_index("tensor")
+    t = _tidx()
     d = lax.axis_index("dp")
     rb = tok_ref.shape[1]
 
     barrier = pltpu.get_barrier_semaphore()
 
     def greet_t(j, c):
-        pl.semaphore_signal(barrier, inc=1, device_id=(d, (t + j) % nt), device_id_type=MESH)
+        pl.semaphore_signal(barrier, inc=1, device_id=_dev(d, (t + j) % nt), device_id_type=MESH)
         return c
 
     def greet_d(j, c):
-        pl.semaphore_signal(barrier, inc=1, device_id=((d + j) % nd, t), device_id_type=MESH)
+        pl.semaphore_signal(barrier, inc=1, device_id=_dev((d + j) % nd, t), device_id_type=MESH)
         return c
 
     lax.fori_loop(1, nt, greet_t, 0)
@@ -155,22 +163,22 @@
     def t_copy(p):
         return pltpu.make_async_remote_copy(
             src_ref=tok_ref, dst_ref=tbuf.at[t], send_sem=ts_sem.at[p], recv_sem=tr_sem.at[t],
-            device_id=(d, p), device_id_type=MESH)
+            device_id=_dev(d, p), device_id_type=MESH)
 
     def t_recv(p):
         return pltpu.make_async_remote_copy(
             src_ref=tok_ref, dst_ref=tbuf.at[p], send_sem=ts_sem.at[p], recv_sem=tr_sem.at[p],
-            device_id=(d, p), device_id_type=MESH)
+            device_id=_dev(d, p), device_id_type=MESH)
 
     def w_copy(p):
         return pltpu.make_async_remote_copy(
             src_ref=wcol_ref, dst_ref=wbuf.at[d], send_sem=ws_sem.at[p], recv_sem=wr_sem.at[d],
-            device_id=(p, t), device_id_type=MESH)
+            device_id=_dev(p, t), device_id_type=MESH)
 
     def w_recv(p):
         return pltpu.make_async_remote_copy(
             src_ref=wcol_ref, dst_ref=wbuf.at[p], send_sem=ws_sem.at[p], recv_sem=wr_sem.at[p],
-            device_id=(p, t), device_id_type=MESH)
+            device_id=_dev(p, t), device_id_type=MESH)
 
     def send_t(j, c):
         t_copy((t + j) % nt).start()
@@ -211,12 +219,12 @@
     def x_copy(p):
         return pltpu.make_async_remote_copy(
             src_ref=xbuf.at[t], dst_ref=xbuf.at[t], send_sem=xs_sem.at[p], recv_sem=xr_sem.at[t],
-            device_id=(d, p), device_id_type=MESH)
+            device_id=_dev(d, p), device_id_type=MESH)
 
     def x_recv(p):
         return pltpu.make_async_remote_copy(
             src_ref=xbuf.at[p], dst_ref=xbuf.at[p], send_sem=xs_sem.at[p], recv_sem=xr_sem.at[p],
-            device_id=(d, p), device_id_type=MESH)
+            device_id=_dev(d, p), device_id_type=MESH)
 
     def send_x(j, c):
         x_copy((t + j) % nt).start()
@@ -262,31 +270,41 @@
 
 
 def on_device(tokens, small_weights, ffn_growth, width_growth):
-    n_t = lax.axis_size("tensor")
+    n_c = lax.axis_size("core")
+    n_t = lax.axis_size("tp") * n_c
     n_d = lax.axis_size("dp")
-    t = lax.axis_index("tensor")
+    t = _tidx()
     rows, ds = width_growth.shape
     xw = ds // n_t
     blk = ds // n_d
     w_cols = lax.dynamic_slice_in_dim(width_growth, t * xw, xw, axis=1)
     tw_blocks = _tw(tokens, w_cols, n_t, n_d)
-    panels = jnp.einsum(
-        "msf,cf->msc",
-        lax.all_gather(small_weights, "tensor", axis=1, tiled=True),
-        ffn_growth,
-        preferred_element_type=jnp.float32,
-    ).astype(jnp.bfloat16)
+    mine = lax.all_gather(small_weights, "tp", axis=1, tiled=True)
+    tw_blocks, sent = lax.optimization_barrier((tw_blocks, mine))
+    other = lax.ppermute(sent, "core", perm=[(0, 1), (1, 0)])
+    ffn_t = ffn_growth.T
+    p_mine = jnp.dot(mine, ffn_t, preferred_element_type=jnp.float32).astype(jnp.bfloat16)
+    p_other = jnp.dot(other, ffn_t, preferred_element_type=jnp.float32).astype(jnp.bfloat16)
+    first = lax.axis_index("core") == 0
+    cols = p_mine.shape[2]
+    per_dev = small_weights.shape[1]
+    halves = [jnp.where(first, p_mine, p_other), jnp.where(first, p_other, p_mine)]
+    halves = [h.reshape(2, n_t // n_c, per_dev, cols) for h in halves]
+    panels = jnp.stack(halves, axis=2).reshape(2, blk, cols)
     w3 = width_growth.reshape(rows, n_d, blk).transpose(1, 0, 2)
     grown_weights, hidden = _dp_ring(panels, w3, tw_blocks)
     return (grown_weights, hidden)
 
 
 def solution(mesh):
-    placed = (P("dp", "tensor"), P(None, ("dp", "tensor"), None), P("tensor", None), P("dp", None))
+    n_d = mesh.shape["dp"]
+    sub = Mesh(mesh.devices.reshape(n_d, -1, 2), ("dp", "tp", "core"))
+    tn = ("tp", "core")
+    placed = (P("dp", tn), P(None, ("dp",) + tn, None), P(tn, None), P("dp", None))
     return jax.shard_map(
         on_device,
-        mesh=mesh,
+        mesh=sub,
         in_specs=placed,
-        out_specs=(P(None, "dp", "tensor"), P("dp", "tensor")),
+        out_specs=(P(None, "dp", tn), P("dp", tn)),
         check_vma=False,
     )

time: 306 us -> 328 us (1.072)
  local copies, waits for them, and re-layouts: 15.7 us -> 26.6 us
  matrix products: 20.6 us -> 26.4 us
    optimization_barrier x0 -> x1, local copies, waits for them, and re-layouts: none -> 6.9 us  [on_device(): tw_blocks, sent = lax.optimization_barrier((tw_blocks, mine))]
    dot_general x1 -> x2, matrix products: 20.6 us -> 26.4 us  [the longest x1 13.3 us: on_device(): jnp.dot(mine, ffn_t, preferred_element_type=jnp.float32)]
    pallas_call x1, Pallas kernels: 108 us -> 113 us  [_dp_ring(): pl.pallas_call(functools.partial(_dp_ring_kernel, n), out_shape=(jax.Shap...]
  transfers between devices with their start and end apart: 1 -> 2, of which waited for: 1 -> 1; matrix products, arithmetic and copies ran while one was open for 3% -> 7% of each run, Pallas kernels for 34% -> 30%
where the time goes in v7:
time: 328 us; the launch traced here: 327 us
  Pallas kernels  212 us (65%)
  waiting for transfers between devices  45.5 us (14%)
  local copies, waits for them, and re-layouts  26.6 us (8%)
  matrix products  26.4 us (8%)
  between operations  14.1 us (4%)
    pallas_call x1, Pallas kernels, _dp_ring(): pl.pallas_call(functools.partial(_dp_ring_kernel, n), out_shape=(jax.Shap...  113 us
    pallas_call x1, Pallas kernels, _tw(): pl.pallas_call(functools.partial(_tw_kernel, nt, nd), out_shape=jax.Shape...  99.2 us
    all_gather x1, waiting for transfers between devices, on_device(): mine = lax.all_gather(small_weights, 'tp', axis=1, tiled=True)  44.8 us
    dot_general x1, matrix products, on_device(): jnp.dot(mine, ffn_t, preferred_element_type=jnp.float32)  13.3 us
    dot_general x1, matrix products, on_device(): jnp.dot(other, ffn_t, preferred_element_type=jnp.float32)  13.1 us
    optimization_barrier x1, local copies, waits for them, and re-layouts, on_device(): tw_blocks, sent = lax.optimization_barrier((tw_blocks, mine))  6.9 us
  transfers between devices with their start and end apart: 2, of which 1 were waited for; matrix products, arithmetic and copies ran while one was open for 7% of the time, Pallas kernels for 30%

profile of v7, /device:TPU:6, one launch (start us, length us, event | category | flops | bytes accessed | tf_op | source)
XLA Modules:
  0.0 326.5 jit_solution(3151816488929579239)
XLA Ops:
  7.2 0.0 all-gather.2.cloned.1.call-start
  7.2 0.7 all-gather.2.cloned.1.call-update
  7.9 1.1 constant_dynamic-slice_fusion.wcol_ref
  9.1 0.0 copy-start.1
  9.1 0.9 copy-done.1
  10.0 99.2 %shard_map.59.tw_ref = bf16[16,256,208]{2,1,0:T(8,128)(2,1)S(1)} custom-call(bf16[256,256]{1,0:T(8,128)(2,1)S(1)} %copy-done.1, bf16[512,208]{1,0:T(8,128)(2,1)S(1)} %constant_dynamic-slice_fusion.wcol_ref), custom_call_target="tpu_custom_call" | custom-call | flops 436207616 | bytes 7208960 | tf_op jit(solution)/shard_map/pallas_call | solution.py:247
  109.2 0.0 copy-start
  109.2 1.3 copy-done
  110.5 44.8 %all-gather.2.cloned.1.call-done = bf16[2,208,8960]{2,0,1:T(2,128)(2,1)} async-done(((bf16[2,26,8960]{2,0,1:T(2,128)(2,1)}), bf16[2,208,8960]{2,0,1:T(2,128)(2,1)}) %all-gather.2.cloned.1.call-update) | async-done | bytes 7454736 | tf_op jit(solution)/shard_map/all_gather | solution.py:282
  155.3 6.9 %copy.21 = bf16[2,208,8960]{2,1,0:T(8,128)(2,1)} copy(bf16[2,208,8960]{2,0,1:T(2,128)(2,1)} %all-gather.2.cloned.1.call-done) | data formatting | bytes 14909440 | tf_op jit(solution)/shard_map/optimization_barrier | solution.py:283
  162.2 0.0 collective-permute-start
  162.2 4.2 %copy.25 = bf16[512,3328]{0,1:T(8,128)(2,1)S(1)} copy(bf16[512,3328]{1,0:T(8,128)(2,1)} %param.7) | data formatting | bytes 6815744 | tf_op args[3]
  166.4 4.6 %copy.26 = bf16[512,8,416]{2,0,1:T(8,128)(2,1)} copy(bf16[512,8,416]{0,2,1:T(8,128)(2,1)S(1)} %bitcast.17) | data formatting | bytes 6815744 | tf_op jit(solution)/shard_map/reshape | solution.py:294
  171.1 13.3 %fusion.5 = bf16[2,208,688]{2,1,0:T(8,128)(2,1)S(1)} fusion(bf16[688,8960]{1,0:T(8,128)(2,1)} %param.6, bf16[2,208,8960]{2,0,1:T(2,128)(2,1)} %all-gather.2.cloned.1.call-done), kind=kOutput, calls=%fused_computation.5 | convolution fusion | flops 5129133568 | bytes 20356096 | tf_op jit(solution)/shard_map/dot_general | solution.py:286
  184.4 0.0 collective-permute-done
  184.4 13.1 %broadcast_select_fusion.1 = (bf16[2,208,688]{2,1,0:T(8,128)(2,1)S(1)}, bf16[2,208,688]{2,1,0:T(8,128)(2,1)S(1)}) fusion(bf16[2,208,688]{2,1,0:T(8,128)(2,1)S(1)} %fusion.5, pred[]{:T(512)S(6)} %eq.3, bf16[2,208,8960]{2,1,0:T(8,128)(2,1)} %collective-permute-done, bf16[688,8960]{1,0:T(8,128)(2,1)} %param.6), kind=kOutput, calls=%fused_computation.9 | convolution fusion | flops 5129705984 | bytes 21500928 | tf_op jit(solution)/shard_map/dot_general | solution.py:287
  197.5 0.5 copy.23
  198.0 0.5 copy.22
  198.5 1.9 pad_maximum_fusion
  200.4 0.9 copy.24
  201.3 1.2 copy.27.p_ref
  202.5 112.8 %shard_map.60 = (bf16[2,512,688]{2,1,0:T(8,128)(2,1)}, bf16[256,688]{1,0:T(8,128)(2,1)}) custom-call(bf16[2,416,688]{2,1,0:T(8,128)(2,1)} %copy.27.p_ref, bf16[8,512,416]{2,1,0:T(8,128)(2,1)} %bitcast.19, bf16[16,256,208]{2,1,0:T(8,128)(2,1)} %copy-done), custom_call_target="tpu_custom_call" | custom-call | flops 7033847808 | bytes 18317312 | tf_op jit(solution)/shard_map/pallas_call | solution.py:115
  315.3 2.5 copy.28
  317.8 1.9 copy.29
Async XLA Ops:
  7.2 148.1 %all-gather.2.cloned.1.call-start = ((), (), s32[]{:S(2)}) async-start(), calls=%async_computation | async-start | bytes 8386560 | tf_op jit(solution)/shard_map/all_gather | solution.py:282
  9.1 0.9 copy-start.1
  109.2 1.3 copy-start
  162.2 22.2 %collective-permute-start = (bf16[2,208,8960]{2,1,0:T(8,128)(2,1)}, bf16[2,208,8960]{2,1,0:T(8,128)(2,1)}, u32[]{:S(2)}, u32[]{:S(2)}) collective-permute-start(bf16[2,208,8960]{2,1,0:T(8,128)(2,1)} %copy.21), channel_id=1, source_target_pairs={{0,1},{1,0},{2,3},{3,2},{4,5},{5,4},{6,7},{7,6},{8,9},{9,8},{10,11... | collective-permute-start | bytes 22364168 | tf_op jit(solution)/shard_map/ppermute | solution.py:284
Sparse Core Ops, SparseCore 0:
  10.3 144.9 all-gather.1

commit v8 on v2

v8 whole, which is shorter than its diff:
```python
import functools

import jax
import jax.numpy as jnp
from jax import lax
from jax.experimental import pallas as pl
from jax.experimental.pallas import tpu as pltpu
from jax.sharding import PartitionSpec as P

MESH = pl.DeviceIdType.MESH


def _ring_pos(d):
    h = d // 4
    return h * 7 + (1 - 2 * h) * (d % 4)


def _ring_dev(p):
    h = p // 4
    return h * 4 + h * 3 + (1 - 2 * h) * (p % 4)


def _dp_ring_kernel(n, nt, p_ref, w3_ref, tf_ref, wg_ref, grown_ref, hid_ref,
                    recv, acc, xbuf, ssem, rsem, xs_sem, xr_sem, osem):
    t = lax.axis_index("tensor")
    d = lax.axis_index("dp")
    pos = _ring_pos(d)
    right = _ring_dev((pos + 1) % n)
    left = _ring_dev((pos + n - 1) % n)
    blk = p_ref.shape[1]
    rb = tf_ref.shape[2]
    xw = wg_ref.shape[2]
    per_w = wg_ref.shape[1] // rb
    per = blk // xw

    barrier = pltpu.get_barrier_semaphore()
    for nb in (left, right):
        pl.semaphore_signal(barrier, inc=1, device_id=(nb, t), device_id_type=MESH)

    def greet_t(j, c):
        pl.semaphore_signal(barrier, inc=1, device_id=(d, (t + j) % nt), device_id_type=MESH)
        return c

    lax.fori_loop(1, nt, greet_t, 0)
    pl.semaphore_wait(barrier, 2 + nt - 1)

    own = []
    for m in range(2):
        c = pltpu.make_async_copy(p_ref.at[m], recv.at[m, d], osem.at[m])
        c.start()
        own.append(c)

    tw = None
    for q in range(nt):
        part = jnp.dot(tf_ref[q], wg_ref[q // per_w, pl.ds((q % per_w) * rb, rb), :],
                       preferred_element_type=jnp.float32)
        tw = part if tw is None else tw + part
    xbuf[t] = tw.astype(xbuf.dtype)

    def x_copy(p):
        return pltpu.make_async_remote_copy(
            src_ref=xbuf.at[t], dst_ref=xbuf.at[t], send_sem=xs_sem.at[p], recv_sem=xr_sem.at[t],
            device_id=(d, p), device_id_type=MESH)

    def x_recv(p):
        return pltpu.make_async_remote_copy(
            src_ref=xbuf.at[p], dst_ref=xbuf.at[p], send_sem=xs_sem.at[p], recv_sem=xr_sem.at[p],
            device_id=(d, p), device_id_type=MESH)

    def send_x(j, c):
        x_copy((t + j) % nt).start()
        return c

    lax.fori_loop(1, nt, send_x, 0)
    for c in own:
        c.wait()

    def step(k, carry):
        o0 = _ring_dev((pos - k + n) % n)
        o1 = _ring_dev((pos + k) % n)
        c0 = pltpu.make_async_remote_copy(
            src_ref=recv.at[0, o0], dst_ref=recv.at[0, o0],
            send_sem=ssem.at[0, k], recv_sem=rsem.at[0, k],
            device_id=(right, t), device_id_type=MESH)
        c1 = pltpu.make_async_remote_copy(
            src_ref=recv.at[1, o1], dst_ref=recv.at[1, o1],
            send_sem=ssem.at[1, k], recv_sem=rsem.at[1, k],
            device_id=(left, t), device_id_type=MESH)
        c0.start()
        c1.start()
        g0 = jnp.dot(w3_ref[o0], recv[0, o0], preferred_element_type=jnp.float32)
        g1 = jnp.dot(w3_ref[o1], recv[1, o1], preferred_element_type=jnp.float32)

        @pl.when(k == 0)
        def _():
            acc[0] = g0
            acc[1] = g1

        @pl.when(k > 0)
        def _():
            acc[0] += g0
            acc[1] += g1

        c0.wait()
        c1.wait()
        return carry

    lax.fori_loop(0, n - 1, step, 0)
    o0 = _ring_dev((pos - (n - 1) + n) % n)
    o1 = _ring_dev((pos + n - 1) % n)
    acc[0] += jnp.dot(w3_ref[o0], recv[0, o0], preferred_element_type=jnp.float32)
    acc[1] += jnp.dot(w3_ref[o1], recv[1, o1], preferred_element_type=jnp.float32)
    grown_ref[...] = acc[...].astype(grown_ref.dtype)

    def wait_x(j, c):
        p = (t + j) % nt
        x_copy(p).wait_send()
        x_recv(p).wait_recv()
        return c

    lax.fori_loop(1, nt, wait_x, 0)
    pre = []
    for m in range(2):
        s = None
        for q in range(nt):
            part = jnp.dot(xbuf[q], recv[m, q // per, pl.ds((q % per) * xw, xw), :],
                           preferred_element_type=jnp.float32)
            s = part if s is None else s + part
        pre.append(s)
    gate = pre[0]
    hid_ref[...] = (gate / (1.0 + jnp.exp(-gate)) * pre[1]).astype(hid_ref.dtype)


def _dp_ring(panels, w3, t_full, w_gath):
    n, rows, blk = w3.shape
    _, _, cols = panels.shape
    nt, tok, rb = t_full.shape
    xw = w_gath.shape[2]
    flops = 2 * 2 * rows * blk * cols * n + 2 * 2 * tok * xw * nt * cols + 2 * tok * rb * nt * xw
    return pl.pallas_call(
        functools.partial(_dp_ring_kernel, n, nt),
        out_shape=(
            jax.ShapeDtypeStruct((2, rows, cols), jnp.bfloat16),
            jax.ShapeDtypeStruct((tok, cols), jnp.bfloat16),
        ),
        in_specs=[pl.BlockSpec(memory_space=pltpu.VMEM)] * 4,
        out_specs=(pl.BlockSpec(memory_space=pltpu.VMEM), pl.BlockSpec(memory_space=pltpu.VMEM)),
        scratch_shapes=[
            pltpu.VMEM((2, n, blk, cols), jnp.bfloat16),
            pltpu.VMEM((2, rows, cols), jnp.float32),
            pltpu.VMEM((nt, tok, xw), jnp.bfloat16),
            pltpu.SemaphoreType.DMA((2, n - 1)),
            pltpu.SemaphoreType.DMA((2, n - 1)),
            pltpu.SemaphoreType.DMA((nt,)),
            pltpu.SemaphoreType.DMA((nt,)),
            pltpu.SemaphoreType.DMA((2,)),
        ],
        compiler_params=pltpu.CompilerParams(
            collective_id=0, has_side_effects=True, vmem_limit_bytes=60 * 1024 * 1024),
        cost_estimate=pl.CostEstimate(
            flops=flops, transcendentals=tok * cols, bytes_accessed=2 * 2 * n * blk * cols * 2),
    )(panels, w3, t_full, w_gath)


def _wg_kernel(nd, wcol_ref, out_ref, wbuf, ws_sem, wr_sem, l_sem):
    t = lax.axis_index("tensor")
    d = lax.axis_index("dp")
    barrier = pltpu.get_barrier_semaphore()

    def greet_d(j, c):
        pl.semaphore_signal(barrier, inc=1, device_id=((d + j) % nd, t), device_id_type=MESH)
        return c

    lax.fori_loop(1, nd, greet_d, 0)
    pl.semaphore_wait(barrier, nd - 1)
    c1 = pltpu.make_async_copy(wcol_ref, wbuf.at[d], l_sem.at[0])
    c1.start()

    def w_copy(p):
        return pltpu.make_async_remote_copy(
            src_ref=wcol_ref, dst_ref=wbuf.at[d], send_sem=ws_sem.at[p], recv_sem=wr_sem.at[d],
            device_id=(p, t), device_id_type=MESH)

    def w_recv(p):
        return pltpu.make_async_remote_copy(
            src_ref=wcol_ref, dst_ref=wbuf.at[p], send_sem=ws_sem.at[p], recv_sem=wr_sem.at[p],
            device_id=(p, t), device_id_type=MESH)

    def send_d(j, c):
        w_copy((d + j) % nd).start()
        return c

    def wait_d(j, c):
        p = (d + j) % nd
        w_copy(p).wait_send()
        w_recv(p).wait_recv()
        return c

    lax.fori_loop(1, nd, send_d, 0)
    lax.fori_loop(1, nd, wait_d, 0)
    c1.wait()
    out_ref[...] = wbuf[...]


def _wg(wcol, nd):
    rows, xw = wcol.shape
    return pl.pallas_call(
        functools.partial(_wg_kernel, nd),
        out_shape=jax.ShapeDtypeStruct((nd, rows, xw), jnp.bfloat16),
        in_specs=[pl.BlockSpec(memory_space=pltpu.VMEM)],
        out_specs=pl.BlockSpec(memory_space=pltpu.VMEM),
        scratch_shapes=[
            pltpu.VMEM((nd, rows, xw), jnp.bfloat16),
            pltpu.SemaphoreType.DMA((nd,)),
            pltpu.SemaphoreType.DMA((nd,)),
            pltpu.SemaphoreType.DMA((1,)),
        ],
        compiler_params=pltpu.CompilerParams(
            collective_id=1, has_side_effects=True, vmem_limit_bytes=32 * 1024 * 1024),
        cost_estimate=pl.CostEstimate(
            flops=0, transcendentals=0, bytes_accessed=nd * rows * xw * 2 * 64),
    )(wcol)


def on_device(tokens, small_weights, ffn_growth, width_growth):
    n_t = lax.axis_size("tensor")
    n_d = lax.axis_size("dp")
    t = lax.axis_index("tensor")
    rows, ds = width_growth.shape
    xw = ds // n_t
    blk = ds // n_d
    w_cols = lax.dynamic_slice_in_dim(width_growth, t * xw, xw, axis=1)
    w_gath = _wg(w_cols, n_d)
    m, per_dev, fs = small_weights.shape
    tok, rb = tokens.shape
    t_rows = -(-tok * rb // fs)
    t_pad = jnp.pad(tokens.reshape(-1), (0, t_rows * fs - tok * rb)).reshape(t_rows, fs)
    ext = jnp.concatenate([small_weights.reshape(m * per_dev, fs), t_pad], axis=0)
    g = lax.all_gather(ext, "tensor", axis=0, tiled=False)
    s_part = g[:, : m * per_dev, :]
    t_full = g[:, m * per_dev:, :].reshape(n_t, t_rows * fs)[:, : tok * rb].reshape(n_t, tok, rb)
    p_dev = jnp.einsum(
        "kjf,cf->kjc", s_part, ffn_growth, preferred_element_type=jnp.float32
    ).astype(jnp.bfloat16)
    cols = p_dev.shape[2]
    panels = p_dev.reshape(n_t, m, per_dev, cols).transpose(1, 0, 2, 3).reshape(m, blk, cols)
    w3 = width_growth.reshape(rows, n_d, blk).transpose(1, 0, 2)
    grown_weights, hidden = _dp_ring(panels, w3, t_full, w_gath)
    return (grown_weights, hidden)


def solution(mesh):
    placed = (P("dp", "tensor"), P(None, ("dp", "tensor"), None), P("tensor", None), P("dp", None))
    return jax.shard_map(
        on_device,
        mesh=mesh,
        in_specs=placed,
        out_specs=(P(None, "dp", "tensor"), P("dp", "tensor")),
        check_vma=False,
    )
```

time: 360 us -> 319 us (0.89)
  waiting for transfers between devices: 185 us -> 75.5 us
  Pallas kernels: 113 us -> 184 us
  matrix products: 32.7 us -> 17.5 us
  local copies, waits for them, and re-layouts: 13.2 us -> 25.5 us
    all_gather x4 -> x1, waiting for transfers between devices: 183 us -> 75.5 us  [on_device(): g = lax.all_gather(ext, 'tensor', axis=0, tiled=False)]
    pallas_call x1 -> x2, Pallas kernels: 113 us -> 184 us  [the longest x1 140 us: _dp_ring(): pl.pallas_call(functools.partial(_dp_ring_kernel, n, nt), out_shape=(jax....]
    dot_general x3 -> x1, matrix products: 32.7 us -> 17.5 us  [on_device(): jnp.einsum('kjf,cf->kjc', s_part, ffn_growth, preferred_element_type=jnp....]
    unnamed x2 -> x9, local copies, waits for them, and re-layouts: 6.77 us -> 10 us
  transfers between devices with their start and end apart: 4 -> 1, of which waited for: 3 -> 1; matrix products, arithmetic and copies ran while one was open for 10% -> 3% of each run, Pallas kernels for 31% -> 14%
where the time goes in v8:
time: 319 us; the launch traced here: 318 us
  Pallas kernels  184 us (58%)
  waiting for transfers between devices  75.5 us (24%)
  local copies, waits for them, and re-layouts  25.5 us (8%)
  matrix products  17.5 us (5%)
  between operations  14.2 us (4%)
    pallas_call x1, Pallas kernels, _dp_ring(): pl.pallas_call(functools.partial(_dp_ring_kernel, n, nt), out_shape=(jax....  140 us
    all_gather x1, waiting for transfers between devices, on_device(): g = lax.all_gather(ext, 'tensor', axis=0, tiled=False)  75.5 us
    pallas_call x1, Pallas kernels, _wg(): pl.pallas_call(functools.partial(_wg_kernel, nd), out_shape=jax.ShapeDtyp...  44.1 us
    dot_general x1, matrix products, on_device(): jnp.einsum('kjf,cf->kjc', s_part, ffn_growth, preferred_element_type=jnp....  17.5 us
    unnamed x9, local copies, waits for them, and re-layouts  10 us
  transfers between devices with their start and end apart: 1, of which 1 were waited for; matrix products, arithmetic and copies ran while one was open for 3% of the time, Pallas kernels for 14%

profile of v8, /device:TPU:6, one launch (start us, length us, event | category | flops | bytes accessed | tf_op | source)
XLA Modules:
  0.0 317.8 jit_solution(2965633218618543901)
XLA Ops:
  7.2 0.0 all-gather.4.cloned.1.call-start
  7.2 1.0 copy.26
  8.2 0.2 reshape.30
  8.4 1.3 copy.18
  9.7 0.2 reshape.28
  10.0 1.1 maximum_bitcast_fusion
  11.1 0.0 all-gather.4.cloned.1.call-update
  11.1 4.3 %copy.21 = bf16[512,3328]{0,1:T(8,128)(2,1)S(1)} copy(bf16[512,3328]{1,0:T(8,128)(2,1)} %param.7) | data formatting | bytes 6815744 | tf_op args[3]
  15.4 1.1 constant_dynamic-slice_fusion.wcol_ref
  16.5 44.1 %shard_map.59.wg_ref = bf16[8,512,208]{2,1,0:T(8,128)(2,1)S(1)} custom-call(bf16[512,208]{1,0:T(8,128)(2,1)S(1)} %constant_dynamic-slice_fusion.wcol_ref), custom_call_target="tpu_custom_call" | custom-call | bytes 109051904 | tf_op jit(solution)/shard_map/pallas_call | solution.py:207
  60.7 0.0 copy-start
  60.7 1.3 copy-done
  62.0 4.5 %copy.22 = bf16[512,8,416]{2,0,1:T(8,128)(2,1)} copy(bf16[512,8,416]{0,2,1:T(8,128)(2,1)S(1)} %bitcast.19) | data formatting | bytes 6815744 | tf_op jit(solution)/shard_map/reshape | solution.py:247
  66.5 75.5 %all-gather.4.cloned.1.call-done = bf16[16,60,8960]{2,1,0:T(8,128)(2,1)} async-done(((bf16[1,60,8960]{2,1,0:T(8,128)(2,1)}), bf16[16,60,8960]{2,1,0:T(8,128)(2,1)}) %all-gather.4.cloned.1.call-update) | async-done | bytes 17203216 | tf_op jit(solution)/shard_map/all_gather | solution.py:239
  142.0 17.5 %fusion.3 = bf16[16,52,688]{2,1,0:T(8,128)(2,1)S(1)} fusion(bf16[688,8960]{1,0:T(8,128)(2,1)} %param.6, bf16[16,60,8960]{2,1,0:T(8,128)(2,1)} %all-gather.4.cloned.1.call-done), kind=kOutput, calls=%fused_computation.3 | convolution fusion | flops 10258267136 | bytes 29530112 | tf_op jit(solution)/shard_map/kjf,cf->kjc/dot_general | solution.py:242
  159.5 0.2 copy.19
  159.7 1.3 copy.20
  161.1 1.2 copy.23.p_ref
  162.2 3.0 slice.13
  165.2 0.4 copy.27
  165.6 0.1 slice.14
  165.7 1.8 copy.28
  167.5 139.9 %shard_map.60 = (bf16[2,512,688]{2,1,0:T(8,128)(2,1)}, bf16[256,688]{1,0:T(8,128)(2,1)}) custom-call(bf16[2,416,688]{2,1,0:T(8,128)(2,1)} %copy.23.p_ref, bf16[8,512,416]{2,1,0:T(8,128)(2,1)} %bitcast.25, bf16[16,256,256]{2,1,0:T(8,128)(2,1)} %bitcast.26, bf16[8,512,208]{2,1,0:T(8,128)(2,1)} %copy-done), custom_call_target="tpu_custom_call" | custom-call | flops 7470055424 | bytes 18317312 | tf_op jit(solution)/shard_map/pallas_call | solution.py:140
  307.4 0.0 copy-start.1
  307.5 2.6 copy.24
  310.0 0.0 copy-done.1
  310.0 0.9 copy.25
  (1 shorter events, 0.0 us)
Async XLA Ops:
  7.2 134.8 %all-gather.4.cloned.1.call-start = ((), (), s32[]{:S(2)}) async-start(), calls=%async_computation | async-start | bytes 19496960 | tf_op jit(solution)/shard_map/all_gather | solution.py:239
  60.7 1.3 copy-start
  307.4 2.6 copy-start.1
Sparse Core Ops, SparseCore 0:
  11.2 130.6 all-gather.3

commit v9 on v6

--- a/solution.py
+++ b/solution.py
@@ -20,53 +20,87 @@
     return h * 4 + h * 3 + (1 - 2 * h) * (p % 4)
 
 
+def _cross_pos(d):
+    z = d % 4
+    return 2 * z + (d // 4 + z) % 2
+
+
+def _cross_dev(p):
+    i = p // 2
+    return ((i + p % 2) % 2) * 4 + i
+
+
+def _flip_z(d, c):
+    z = d % 4
+    return d + c * (1 - 2 * (z % 2))
+
+
+def _flip_y(d, c):
+    y = d // 4
+    return d + c * (1 - 2 * y) * 4
+
+
 def _dp_ring_kernel(n, p_ref, w3_ref, tw_ref, grown_ref, hid_ref, recv, acc, pre, ssem, rsem, osem):
     t = lax.axis_index("tensor")
     d = lax.axis_index("dp")
-    pos = _ring_pos(d)
-    right = _ring_dev((pos + 1) % n)
-    left = _ring_dev((pos + n - 1) % n)
-    blk = p_ref.shape[1]
+    c = t % 2
+    pos_a = _ring_pos(_flip_z(d, c))
+    pos_b = _cross_pos(_flip_y(d, c))
+
+    def dev_a(p):
+        return _flip_z(_ring_dev(p % n), c)
+
+    def dev_b(p):
+        return _flip_y(_cross_dev(p % n), c)
+
+    flows = [
+        (dev_a, pos_a, 1),
+        (dev_a, pos_a, -1),
+        (dev_b, pos_b, 1),
+        (dev_b, pos_b, -1),
+    ]
     xw = tw_ref.shape[2]
-    per = blk // xw
 
     barrier = pltpu.get_barrier_semaphore()
-    for nb in (left, right):
-        pl.semaphore_signal(barrier, inc=1, device_id=(nb, t), device_id_type=MESH)
-    pl.semaphore_wait(barrier, 2)
+    for dev, pos, sgn in flows:
+        pl.semaphore_signal(barrier, inc=1, device_id=(dev(pos + sgn + n), t), device_id_type=MESH)
+    pl.semaphore_wait(barrier, 4)
 
     own = []
-    for m in range(2):
-        c = pltpu.make_async_copy(p_ref.at[m], recv.at[m, d], osem.at[m])
-        c.start()
-        own.append(c)
-    for c in own:
-        c.wait()
-
-    def contrib(m, o):
-        g = jnp.dot(w3_ref[o], recv[m, o], preferred_element_type=jnp.float32)
-        h = None
-        for q in range(per):
-            part = jnp.dot(tw_ref[per * o + q], recv[m, o, pl.ds(q * xw, xw), :],
-                           preferred_element_type=jnp.float32)
-            h = part if h is None else h + part
+    for q in range(4):
+        cp = pltpu.make_async_copy(p_ref.at[q], recv.at[q, d], osem.at[q])
+        cp.start()
+        own.append(cp)
+    for cp in own:
+        cp.wait()
+
+    def origin(q, k):
+        dev, pos, sgn = flows[q]
+        return dev(pos - sgn * k + n)
+
+    def contrib(q, o):
+        g = jnp.dot(w3_ref[o, q % 2], recv[q, o], preferred_element_type=jnp.float32)
+        h = jnp.dot(tw_ref[2 * o + q % 2], recv[q, o], preferred_element_type=jnp.float32)
         return g, h
 
     def step(k, carry):
-        o0 = _ring_dev((pos - k + n) % n)
-        o1 = _ring_dev((pos + k) % n)
-        c0 = pltpu.make_async_remote_copy(
-            src_ref=recv.at[0, o0], dst_ref=recv.at[0, o0],
-            send_sem=ssem.at[0, k], recv_sem=rsem.at[0, k],
-            device_id=(right, t), device_id_type=MESH)
-        c1 = pltpu.make_async_remote_copy(
-            src_ref=recv.at[1, o1], dst_ref=recv.at[1, o1],
-            send_sem=ssem.at[1, k], recv_sem=rsem.at[1, k],
-            device_id=(left, t), device_id_type=MESH)
-        c0.start()
-        c1.start()
-        g0, h0 = contrib(0, o0)
-        g1, h1 = contrib(1, o1)
+        copies = []
+        origins = []
+        for q in range(4):
+            dev, pos, sgn = flows[q]
+            o = origin(q, k)
+            cp = pltpu.make_async_remote_copy(
+                src_ref=recv.at[q, o], dst_ref=recv.at[q, o],
+                send_sem=ssem.at[q, k], recv_sem=rsem.at[q, k],
+                device_id=(dev(pos + sgn + n), t), device_id_type=MESH)
+            cp.start()
+            copies.append(cp)
+            origins.append(o)
+        parts = [contrib(q, origins[q]) for q in range(4)]
+        g0 = parts[0][0] + parts[1][0]
+        g1 = parts[2][0] + parts[3][0]
+        h0 = parts[0][1] + parts[1][1]
+        h1 = parts[2][1] + parts[3][1]
 
         @pl.when(k == 0)
         def _():
@@ -82,28 +116,25 @@
             pre[0] += h0
             pre[1] += h1
 
-        c0.wait()
-        c1.wait()
+        for cp in copies:
+            cp.wait()
         return carry
 
     lax.fori_loop(0, n - 1, step, 0)
-    o0 = _ring_dev((pos - (n - 1) + n) % n)
-    o1 = _ring_dev((pos + n - 1) % n)
-    g0, h0 = contrib(0, o0)
-    g1, h1 = contrib(1, o1)
-    acc[0] += g0
-    acc[1] += g1
+    parts = [contrib(q, origin(q, n - 1)) for q in range(4)]
+    acc[0] += parts[0][0] + parts[1][0]
+    acc[1] += parts[2][0] + parts[3][0]
     grown_ref[...] = acc[...].astype(grown_ref.dtype)
-    gate = pre[0] + h0
-    up = pre[1] + h1
+    gate = pre[0] + parts[0][1] + parts[1][1]
+    up = pre[1] + parts[2][1] + parts[3][1]
     hid_ref[...] = (gate / (1.0 + jnp.exp(-gate)) * up).astype(hid_ref.dtype)
 
 
-def _dp_ring(panels, w3, tw_blocks):
-    n, rows, blk = w3.shape
-    _, _, cols = panels.shape
+def _dp_ring(quarters, w3h, tw_blocks):
+    n, _, rows, hb = w3h.shape
+    _, _, cols = quarters.shape
     nt, tok, xw = tw_blocks.shape
-    flops = 2 * 2 * rows * blk * cols * n + 2 * 2 * tok * xw * nt * cols
+    flops = 2 * 2 * rows * hb * 2 * cols * n + 2 * 2 * tok * xw * nt * cols
     return pl.pallas_call(
         functools.partial(_dp_ring_kernel, n),
         out_shape=(
@@ -113,18 +144,18 @@
         in_specs=[pl.BlockSpec(memory_space=pltpu.VMEM)] * 3,
         out_specs=(pl.BlockSpec(memory_space=pltpu.VMEM), pl.BlockSpec(memory_space=pltpu.VMEM)),
         scratch_shapes=[
-            pltpu.VMEM((2, n, blk, cols), jnp.bfloat16),
+            pltpu.VMEM((4, n, hb, cols), jnp.bfloat16),
             pltpu.VMEM((2, rows, cols), jnp.float32),
             pltpu.VMEM((2, tok, cols), jnp.float32),
-            pltpu.SemaphoreType.DMA((2, n - 1)),
-            pltpu.SemaphoreType.DMA((2, n - 1)),
-            pltpu.SemaphoreType.DMA((2,)),
+            pltpu.SemaphoreType.DMA((4, n - 1)),
+            pltpu.SemaphoreType.DMA((4, n - 1)),
+            pltpu.SemaphoreType.DMA((4,)),
         ],
         compiler_params=pltpu.CompilerParams(
             collective_id=0, has_side_effects=True, vmem_limit_bytes=56 * 1024 * 1024),
         cost_estimate=pl.CostEstimate(
-            flops=flops, transcendentals=tok * cols, bytes_accessed=2 * 2 * n * blk * cols * 2),
-    )(panels, w3, tw_blocks)
+            flops=flops, transcendentals=tok * cols, bytes_accessed=4 * n * hb * cols * 2),
+    )(quarters, w3h, tw_blocks)
 
 
 def _tw_kernel(nt, nd, tok_ref, wcol_ref, out_ref, tbuf, wbuf, xbuf,
@@ -276,8 +307,10 @@
         ffn_growth,
         preferred_element_type=jnp.float32,
     ).astype(jnp.bfloat16)
-    w3 = width_growth.reshape(rows, n_d, blk).transpose(1, 0, 2)
-    grown_weights, hidden = _dp_ring(panels, w3, tw_blocks)
+    hb = blk // 2
+    w3h = width_growth.reshape(rows, n_d, 2, hb).transpose(1, 2, 0, 3)
+    quarters = panels.reshape(4, hb, panels.shape[2])
+    grown_weights, hidden = _dp_ring(quarters, w3h, tw_blocks)
     return (grown_weights, hidden)
 
 

time: 306 us -> 287 us (0.938)
  Pallas kernels: 210 us -> 191 us
    pallas_call x1, Pallas kernels: 108 us -> 88.9 us  [_dp_ring(): pl.pallas_call(functools.partial(_dp_ring_kernel, n), out_shape=(jax.Shap...]
  transfers between devices with their start and end apart: 1 -> 1, of which waited for: 1 -> 1; matrix products, arithmetic and copies ran while one was open for 3% -> 3% of each run, Pallas kernels for 34% -> 36%
where the time goes in v9:
time: 287 us; the launch traced here: 284 us
  Pallas kernels  191 us (67%)
  waiting for transfers between devices  44.1 us (15%)
  matrix products  20.6 us (7%)
  local copies, waits for them, and re-layouts  15.1 us (5%)
  between operations  14.1 us (5%)
    pallas_call x1, Pallas kernels, _tw(): pl.pallas_call(functools.partial(_tw_kernel, nt, nd), out_shape=jax.Shape...  102 us
    pallas_call x1, Pallas kernels, _dp_ring(): pl.pallas_call(functools.partial(_dp_ring_kernel, n), out_shape=(jax.Shap...  88.9 us
    all_gather x1, waiting for transfers between devices, on_device(): lax.all_gather(small_weights, 'tensor', axis=1, tiled=True)  43.4 us
    dot_general x1, matrix products, on_device(): jnp.einsum('msf,cf->msc', lax.all_gather(small_weights, 'tensor', axis=1,...  20.6 us
  transfers between devices with their start and end apart: 1, of which 1 were waited for; matrix products, arithmetic and copies ran while one was open for 3% of the time, Pallas kernels for 36%

profile of v9, /device:TPU:6, one launch (start us, length us, event | category | flops | bytes accessed | tf_op | source)
XLA Modules:
  0.0 284.5 jit_solution(5447056481486840895)
XLA Ops:
  7.2 0.0 all-gather.2.cloned.1.call-start
  7.2 0.7 all-gather.2.cloned.1.call-update
  7.9 4.3 %copy.15 = bf16[512,3328]{0,1:T(8,128)(2,1)S(1)} copy(bf16[512,3328]{1,0:T(8,128)(2,1)} %param.7) | data formatting | bytes 6815744 | tf_op args[3]
  12.2 0.0 copy-start.1
  12.2 4.0 %copy.16 = bf16[512,8,2,208]{3,0,2,1:T(8,128)(2,1)} copy(bf16[512,8,2,208]{0,3,2,1:T(8,128)(2,1)S(1)} %bitcast.8) | data formatting | bytes 6815744 | tf_op jit(solution)/shard_map/reshape | solution.py:311
  16.2 1.1 constant_dynamic-slice_fusion.wcol_ref
  17.3 0.0 copy-done.1
  17.3 101.6 %shard_map.59.tw_ref = bf16[16,256,208]{2,1,0:T(8,128)(2,1)S(1)} custom-call(bf16[256,256]{1,0:T(8,128)(2,1)S(1)} %copy-done.1, bf16[512,208]{1,0:T(8,128)(2,1)S(1)} %constant_dynamic-slice_fusion.wcol_ref), custom_call_target="tpu_custom_call" | custom-call | flops 436207616 | bytes 7208960 | tf_op jit(solution)/shard_map/pallas_call | solution.py:270
  118.9 0.0 copy-start
  118.9 1.3 copy-done
  120.2 43.4 %all-gather.2.cloned.1.call-done = bf16[2,416,8960]{2,0,1:T(2,128)(2,1)} async-done(((bf16[2,26,8960]{2,0,1:T(2,128)(2,1)}), bf16[2,416,8960]{2,0,1:T(2,128)(2,1)}) %all-gather.2.cloned.1.call-update) | async-done | bytes 14909456 | tf_op jit(solution)/shard_map/all_gather | solution.py:306
  163.7 20.6 %fusion.3 = bf16[2,416,688]{2,1,0:T(8,128)(2,1)} fusion(bf16[688,8960]{1,0:T(8,128)(2,1)} %param.6, bf16[2,416,8960]{2,0,1:T(2,128)(2,1)} %all-gather.2.cloned.1.call-done), kind=kOutput, calls=%fused_computation.3 | convolution fusion | flops 10258267136 | bytes 28383232 | tf_op jit(solution)/shard_map/msf,cf->msc/dot_general | solution.py:304
  184.2 88.9 %shard_map.60 = (bf16[2,512,688]{2,1,0:T(8,128)(2,1)}, bf16[256,688]{1,0:T(8,128)(2,1)}) custom-call(bf16[4,208,688]{2,1,0:T(8,128)(2,1)} %bitcast.10, bf16[8,2,512,208]{3,2,1,0:T(8,128)(2,1)} %bitcast.9, bf16[16,256,208]{2,1,0:T(8,128)(2,1)} %copy-done), custom_call_target="tpu_custom_call" | custom-call | flops 7033847808 | bytes 9158656 | tf_op jit(solution)/shard_map/pallas_call | solution.py:138
  273.2 2.5 copy.17
  275.7 1.9 copy.18
Async XLA Ops:
  7.2 156.5 %all-gather.2.cloned.1.call-start = ((), (), s32[]{:S(2)}) async-start(), calls=%async_computation | async-start | bytes 15841280 | tf_op jit(solution)/shard_map/all_gather | solution.py:306
  12.2 5.1 %copy-start.1 = (bf16[256,256]{1,0:T(8,128)(2,1)S(1)}, bf16[256,256]{1,0:T(8,128)(2,1)}, u32[]{:S(2)}) copy-start(bf16[256,256]{1,0:T(8,128)(2,1)} %tok_ref.1) | copy-start | bytes 393220
  118.9 1.3 copy-start
Sparse Core Ops, SparseCore 0:
  10.5 153.0 all-gather.1

commit v10 on v9

v10 whole, which is shorter than its diff:
```python
import functools

import jax
import jax.numpy as jnp
from jax import lax
from jax.experimental import pallas as pl
from jax.experimental.pallas import tpu as pltpu
from jax.sharding import PartitionSpec as P

MESH = pl.DeviceIdType.MESH


def _ring_pos(d):
    h = d // 4
    return h * 7 + (1 - 2 * h) * (d % 4)


def _ring_dev(p):
    h = p // 4
    return h * 4 + h * 3 + (1 - 2 * h) * (p % 4)


def _cross_pos(d):
    z = d % 4
    return 2 * z + (d // 4 + z) % 2


def _cross_dev(p):
    i = p // 2
    return ((i + p % 2) % 2) * 4 + i


def _flip_z(d, c):
    z = d % 4
    return d + c * (1 - 2 * (z % 2))


def _flip_y(d, c):
    y = d // 4
    return d + c * (1 - 2 * y) * 4


def _dp_ring_kernel(n, p_ref, w3_ref, grown_ref, pall_ref, recv, acc, ssem, rsem, lsem, osem):
    t = lax.axis_index("tensor")
    d = lax.axis_index("dp")
    c = t % 2
    pos_a = _ring_pos(_flip_z(d, c))
    pos_b = _cross_pos(_flip_y(d, c))

    def dev_a(p):
        return _flip_z(_ring_dev(p % n), c)

    def dev_b(p):
        return _flip_y(_cross_dev(p % n), c)

    flows = [
        (dev_a, pos_a, 1),
        (dev_a, pos_a, -1),
        (dev_b, pos_b, 1),
        (dev_b, pos_b, -1),
    ]

    barrier = pltpu.get_barrier_semaphore()
    for dev, pos, sgn in flows:
        pl.semaphore_signal(barrier, inc=1, device_id=(dev(pos + sgn + n), t), device_id_type=MESH)
    pl.semaphore_wait(barrier, 4)

    own = []
    for q in range(4):
        cp = pltpu.make_async_copy(p_ref.at[q], recv.at[q, d], osem.at[q])
        cp.start()
        own.append(cp)
    for cp in own:
        cp.wait()
    for q in range(4):
        pltpu.make_async_copy(recv.at[q, d], pall_ref.at[q // 2, d, q % 2], lsem.at[q, d]).start()

    def origin(q, k):
        dev, pos, sgn = flows[q]
        return dev(pos - sgn * k + n)

    def contrib(q, o):
        return jnp.dot(w3_ref[o, q % 2], recv[q, o], preferred_element_type=jnp.float32)

    def step(k, carry):
        copies = []
        origins = []
        for q in range(4):
            dev, pos, sgn = flows[q]
            o = origin(q, k)
            cp = pltpu.make_async_remote_copy(
                src_ref=recv.at[q, o], dst_ref=recv.at[q, o],
                send_sem=ssem.at[q, k], recv_sem=rsem.at[q, k],
                device_id=(dev(pos + sgn + n), t), device_id_type=MESH)
            cp.start()
            copies.append(cp)
            origins.append(o)
        parts = [contrib(q, origins[q]) for q in range(4)]
        g0 = parts[0] + parts[1]
        g1 = parts[2] + parts[3]

        @pl.when(k == 0)
        def _():
            acc[0] = g0
            acc[1] = g1

        @pl.when(k > 0)
        def _():
            acc[0] += g0
            acc[1] += g1

        for q in range(4):
            copies[q].wait()
            nxt = origin(q, k + 1)
            pltpu.make_async_copy(recv.at[q, nxt], pall_ref.at[q // 2, nxt, q % 2], lsem.at[q, nxt]).start()
        return carry

    lax.fori_loop(0, n - 1, step, 0)
    parts = [contrib(q, origin(q, n - 1)) for q in range(4)]
    acc[0] += parts[0] + parts[1]
    acc[1] += parts[2] + parts[3]
    grown_ref[...] = acc[...].astype(grown_ref.dtype)
    for q in range(4):
        for o in range(n):
            pltpu.make_async_copy(recv.at[q, o], pall_ref.at[q // 2, o, q % 2], lsem.at[q, o]).wait()


def _dp_ring(quarters, w3h):
    n, _, rows, hb = w3h.shape
    _, _, cols = quarters.shape
    flops = 2 * 2 * rows * hb * 2 * cols * n
    return pl.pallas_call(
        functools.partial(_dp_ring_kernel, n),
        out_shape=(
            jax.ShapeDtypeStruct((2, rows, cols), jnp.bfloat16),
            jax.ShapeDtypeStruct((2, n, 2, hb, cols), jnp.bfloat16),
        ),
        in_specs=[pl.BlockSpec(memory_space=pltpu.VMEM)] * 2,
        out_specs=(pl.BlockSpec(memory_space=pltpu.VMEM), pl.BlockSpec(memory_space=pl.ANY)),
        scratch_shapes=[
            pltpu.VMEM((4, n, hb, cols), jnp.bfloat16),
            pltpu.VMEM((2, rows, cols), jnp.float32),
            pltpu.SemaphoreType.DMA((4, n - 1)),
            pltpu.SemaphoreType.DMA((4, n - 1)),
            pltpu.SemaphoreType.DMA((4, n)),
            pltpu.SemaphoreType.DMA((4,)),
        ],
        compiler_params=pltpu.CompilerParams(
            collective_id=0, has_side_effects=True, vmem_limit_bytes=56 * 1024 * 1024),
        cost_estimate=pl.CostEstimate(
            flops=flops, transcendentals=0, bytes_accessed=4 * n * hb * cols * 2),
    )(quarters, w3h)


def _wg_kernel(nd, wcol_ref, out_ref, wbuf, ws_sem, wr_sem, l_sem):
    t = lax.axis_index("tensor")
    d = lax.axis_index("dp")
    barrier = pltpu.get_barrier_semaphore()

    def greet_d(j, c):
        pl.semaphore_signal(barrier, inc=1, device_id=((d + j) % nd, t), device_id_type=MESH)
        return c

    lax.fori_loop(1, nd, greet_d, 0)
    pl.semaphore_wait(barrier, nd - 1)
    c1 = pltpu.make_async_copy(wcol_ref, wbuf.at[d], l_sem.at[0])
    c1.start()

    def w_copy(p):
        return pltpu.make_async_remote_copy(
            src_ref=wcol_ref, dst_ref=wbuf.at[d], send_sem=ws_sem.at[p], recv_sem=wr_sem.at[d],
            device_id=(p, t), device_id_type=MESH)

    def w_recv(p):
        return pltpu.make_async_remote_copy(
            src_ref=wcol_ref, dst_ref=wbuf.at[p], send_sem=ws_sem.at[p], recv_sem=wr_sem.at[p],
            device_id=(p, t), device_id_type=MESH)

    def send_d(j, c):
        w_copy((d + j) % nd).start()
        return c

    def wait_d(j, c):
        p = (d + j) % nd
        w_copy(p).wait_send()
        w_recv(p).wait_recv()
        return c

    lax.fori_loop(1, nd, send_d, 0)
    lax.fori_loop(1, nd, wait_d, 0)
    c1.wait()
    out_ref[...] = wbuf[...]


def _wg(wcol, nd):
    rows, xw = wcol.shape
    return pl.pallas_call(
        functools.partial(_wg_kernel, nd),
        out_shape=jax.ShapeDtypeStruct((nd, rows, xw), jnp.bfloat16),
        in_specs=[pl.BlockSpec(memory_space=pltpu.VMEM)],
        out_specs=pl.BlockSpec(memory_space=pltpu.VMEM),
        scratch_shapes=[
            pltpu.VMEM((nd, rows, xw), jnp.bfloat16),
            pltpu.SemaphoreType.DMA((nd,)),
            pltpu.SemaphoreType.DMA((nd,)),
            pltpu.SemaphoreType.DMA((1,)),
        ],
        compiler_params=pltpu.CompilerParams(
            collective_id=1, has_side_effects=True, vmem_limit_bytes=32 * 1024 * 1024),
        cost_estimate=pl.CostEstimate(
            flops=0, transcendentals=0, bytes_accessed=nd * rows * xw * 2 * 64),
    )(wcol)


def on_device(tokens, small_weights, ffn_growth, width_growth):
    n_t = lax.axis_size("tensor")
    n_d = lax.axis_size("dp")
    t = lax.axis_index("tensor")
    rows, ds = width_growth.shape
    xw = ds // n_t
    blk = ds // n_d
    w_cols = lax.dynamic_slice_in_dim(width_growth, t * xw, xw, axis=1)
    w_gath = _wg(w_cols, n_d)
    m, per_dev, fs = small_weights.shape
    tok, rb = tokens.shape
    t_rows = -(-tok * rb // fs)
    t_pad = jnp.pad(tokens.reshape(-1), (0, t_rows * fs - tok * rb)).reshape(t_rows, fs)
    ext = jnp.concatenate([small_weights.reshape(m * per_dev, fs), t_pad], axis=0)
    g = lax.all_gather(ext, "tensor", axis=0, tiled=False)
    s_part = g[:, : m * per_dev, :]
    t_full = g[:, m * per_dev:, :].reshape(n_t, t_rows * fs)[:, : tok * rb].reshape(n_t, tok, rb)
    t_row = t_full.transpose(1, 0, 2).reshape(tok, n_t * rb)
    tw_part = jnp.dot(t_row, w_gath.reshape(n_d * rows, xw), preferred_element_type=jnp.float32)
    tw_t = lax.all_gather(tw_part.astype(jnp.bfloat16).T, "tensor", axis=0, tiled=True)
    p_dev = jnp.einsum(
        "kjf,cf->kjc", s_part, ffn_growth, preferred_element_type=jnp.float32
    ).astype(jnp.bfloat16)
    cols = p_dev.shape[2]
    panels = p_dev.reshape(n_t, m, per_dev, cols).transpose(1, 0, 2, 3).reshape(m, blk, cols)
    hb = blk // 2
    w3h = width_growth.reshape(rows, n_d, 2, hb).transpose(1, 2, 0, 3)
    quarters = panels.reshape(4, hb, cols)
    grown_weights, pall = _dp_ring(quarters, w3h)
    all_panels = pall.reshape(m, ds, cols)
    pre_values = jnp.einsum(
        "st,msc->tmc", tw_t, all_panels, preferred_element_type=jnp.float32
    )
    hidden = (jax.nn.silu(pre_values[:, 0, :]) * pre_values[:, 1, :]).astype(jnp.bfloat16)
    return (grown_weights, hidden)


def solution(mesh):
    placed = (P("dp", "tensor"), P(None, ("dp", "tensor"), None), P("tensor", None), P("dp", None))
    return jax.shard_map(
        on_device,
        mesh=mesh,
        in_specs=placed,
        out_specs=(P(None, "dp", "tensor"), P("dp", "tensor")),
        check_vma=False,
    )
```

time: 287 us -> 293 us (1.021)
  Pallas kernels: 191 us -> 144 us
  waiting for transfers between devices: 44.1 us -> 73.7 us
  local copies, waits for them, and re-layouts: 15.1 us -> 29.5 us
  matrix products: 20.6 us -> 29.2 us
    pallas_call x1, Pallas kernels: 102 us -> 44.1 us  [_wg(): pl.pallas_call(functools.partial(_wg_kernel, nd), out_shape=jax.ShapeDtyp...]
    all_gather x1 -> x2, waiting for transfers between devices: 43.4 us -> 73.7 us  [the longest x1 73.7 us: on_device(): g = lax.all_gather(ext, 'tensor', axis=0, tiled=False)]
    pallas_call x1, Pallas kernels: 88.9 us -> 99.6 us  [_dp_ring(): pl.pallas_call(functools.partial(_dp_ring_kernel, n), out_shape=(jax.Shap...]
    dot_general x1 -> x3, matrix products: 20.6 us -> 29.2 us  [the longest x1 17.7 us: on_device(): jnp.einsum('kjf,cf->kjc', s_part, ffn_growth, preferred_element_type=jnp....]
    unnamed x5 -> x6, local copies, waits for them, and re-layouts: 5.57 us -> 12.6 us
    pallas_call x2 -> x0, local copies, waits for them, and re-layouts: 4.42 us -> none  [_dp_ring(): pl.pallas_call(functools.partial(_dp_ring_kernel, n), out_shape=(jax.Shap...]
    transpose x0 -> x2, local copies, waits for them, and re-layouts: none -> 4.32 us  [the longest x1 3.9 us: on_device(): t_row = t_full.transpose(1, 0, 2).reshape(tok, n_t * rb)]
    slice x0 -> x2, local copies, waits for them, and re-layouts: none -> 3.1 us  [on_device(): g[:, m * per_dev:, :].reshape(n_t, t_rows * fs)[:, :tok * rb]]
  transfers between devices with their start and end apart: 1 -> 2, of which waited for: 1 -> 1; matrix products, arithmetic and copies ran while one was open for 3% -> 12% of each run, Pallas kernels for 36% -> 49%
where the time goes in v10:
time: 293 us; the launch traced here: 292 us
  Pallas kernels  144 us (49%)
  waiting for transfers between devices  73.7 us (25%)
  local copies, waits for them, and re-layouts  29.5 us (10%)
  matrix products  29.2 us (10%)
  between operations  14.1 us (5%)
    pallas_call x1, Pallas kernels, _dp_ring(): pl.pallas_call(functools.partial(_dp_ring_kernel, n), out_shape=(jax.Shap...  99.6 us
    all_gather x1, waiting for transfers between devices, on_device(): g = lax.all_gather(ext, 'tensor', axis=0, tiled=False)  73.7 us
    pallas_call x1, Pallas kernels, _wg(): pl.pallas_call(functools.partial(_wg_kernel, nd), out_shape=jax.ShapeDtyp...  44.1 us
    dot_general x1, matrix products, on_device(): jnp.einsum('kjf,cf->kjc', s_part, ffn_growth, preferred_element_type=jnp....  17.7 us
    unnamed x6, local copies, waits for them, and re-layouts  12.6 us
    dot_general x1, matrix products, on_device(): jnp.einsum('st,msc->tmc', tw_t, all_panels, preferred_element_type=jnp.fl...  8.41 us
    reshape x1, local copies, waits for them, and re-layouts, on_device(): w3h = width_growth.reshape(rows, n_d, 2, hb).transpose(1, 2, 0, 3)  6.24 us
  transfers between devices with their start and end apart: 2, of which 1 were waited for; matrix products, arithmetic and copies ran while one was open for 12% of the time, Pallas kernels for 49%

profile of v10, /device:TPU:6, one launch (start us, length us, event | category | flops | bytes accessed | tf_op | source)
XLA Modules:
  0.0 292.4 jit_solution(8469466190803314796)
XLA Ops:
  7.2 0.0 all-gather.7.cloned.1.call-start
  7.2 1.0 copy.34
  8.2 0.2 reshape.36
  8.4 1.3 copy.25
  9.7 0.2 reshape.34
  10.0 1.1 maximum_bitcast_fusion
  11.1 0.0 all-gather.7.cloned.1.call-update
  11.1 0.0 all-gather.5.cloned.1.call-start
  11.2 5.6 %copy.28 = bf16[512,3328]{0,1:T(8,128)(2,1)} copy(bf16[512,3328]{1,0:T(8,128)(2,1)} %param.7) | data formatting | bytes 6815744 | tf_op args[3]
  16.7 1.1 constant_dynamic-slice_fusion.wcol_ref
  17.9 44.1 %shard_map.60 = bf16[8,512,208]{2,1,0:T(8,128)(2,1)S(1)} custom-call(bf16[512,208]{1,0:T(8,128)(2,1)S(1)} %constant_dynamic-slice_fusion.wcol_ref), custom_call_target="tpu_custom_call" | custom-call | bytes 109051904 | tf_op jit(solution)/shard_map/pallas_call | solution.py:197
  62.0 6.2 %copy.29 = bf16[512,8,2,208]{3,0,2,1:T(8,128)(2,1)} copy(bf16[512,8,2,208]{0,3,2,1:T(8,128)(2,1)} %bitcast.40) | data formatting | bytes 6815744 | tf_op jit(solution)/shard_map/reshape | solution.py:241
  68.3 73.7 %all-gather.7.cloned.1.call-done = bf16[16,60,8960]{2,1,0:T(8,128)(2,1)} async-done(((bf16[1,60,8960]{2,1,0:T(8,128)(2,1)}), bf16[16,60,8960]{2,1,0:T(8,128)(2,1)}) %all-gather.7.cloned.1.call-update) | async-done | bytes 17203216 | tf_op jit(solution)/shard_map/all_gather | solution.py:229
  142.0 3.0 %slice.21 = bf16[16,8,8960]{2,1,0:T(8,128)(2,1)S(1)} slice(bf16[16,60,8960]{2,1,0:T(8,128)(2,1)} %all-gather.7.cloned.1.call-done), slice={[0:16], [52:60], [0:8960]} | slice | bytes 4587520 | tf_op jit(solution)/shard_map/slice | solution.py:231
  144.9 0.4 copy.35
  145.3 0.1 slice.22
  145.5 1.8 copy.36
  147.2 3.9 %copy.30 = bf16[256,16,256]{0,2,1:T(8,128)(2,1)} copy(bf16[256,16,256]{2,0,1:T(8,128)(2,1)} %bitcast.44) | data formatting | bytes 4194304 | tf_op jit(solution)/shard_map/transpose | solution.py:232
  151.1 3.1 %convolution_convert_fusion = bf16[208,256]{1,0:T(8,128)(2,1)} fusion(bf16[4096,208]{1,0:T(8,128)(2,1)S(1)} %bitcast.39, bf16[256,4096]{0,1:T(8,128)(2,1)} %bitcast.47), kind=kOutput, calls=%fused_computation.7 | convolution fusion | flops 436260864 | bytes 3907584 | tf_op jit(solution)/shard_map/dot_general | solution.py:233
  154.2 0.0 all-gather.5.cloned.1.call-update
  154.2 17.7 %fusion.5 = bf16[16,52,688]{2,1,0:T(8,128)(2,1)S(1)} fusion(bf16[688,8960]{1,0:T(8,128)(2,1)} %param.6, bf16[16,60,8960]{2,1,0:T(8,128)(2,1)} %all-gather.7.cloned.1.call-done), kind=kOutput, calls=%fused_computation.5 | convolution fusion | flops 10258267136 | bytes 29530112 | tf_op jit(solution)/shard_map/kjf,cf->kjc/dot_general | solution.py:235
  172.0 0.2 copy.26
  172.2 0.4 copy.27
  172.6 1.5 reshape_reshape.3.p_ref
  174.1 99.6 %shard_map.59 = (bf16[2,512,688]{2,1,0:T(8,128)(2,1)}, bf16[2,8,2,208,688]{4,3,2,1,0:T(8,128)(2,1)}) custom-call(bf16[4,208,688]{2,1,0:T(8,128)(2,1)} %reshape_reshape.3.p_ref, bf16[8,2,512,208]{3,2,1,0:T(8,128)(2,1)} %bitcast.46), custom_call_target="tpu_custom_call" | custom-call | flops 4689231872 | bytes 9158656 | tf_op jit(solution)/shard_map/pallas_call | solution.py:132
  273.7 2.5 copy.32
  276.2 0.0 all-gather.5.cloned.1.call-done
  276.2 8.4 %fusion.3 = f32[256,2,688]{0,2,1:T(8,128)S(1)} fusion(bf16[2,3328,688]{2,1,0:T(8,128)(2,1)} %bitcast.50, bf16[3328,256]{1,0:T(8,128)(2,1)} %all-gather.5.cloned.1.call-done), kind=kOutput, calls=%fused_computation.3 | convolution fusion | flops 2344615936 | bytes 12271616 | tf_op jit(solution)/shard_map/st,msc->tmc/dot_general | solution.py:245
  284.7 0.9 fusion.11
  (1 shorter events, 0.0 us)
Async XLA Ops:
  7.2 134.8 %all-gather.7.cloned.1.call-start = ((), (), s32[]{:S(2)}) async-start(), calls=%async_computation.1 | async-start | bytes 19496960 | tf_op jit(solution)/shard_map/all_gather | solution.py:229
  11.1 265.1 %all-gather.5.cloned.1.call-start = ((), (), s32[]{:S(2)}) async-start(), calls=%async_computation | async-start | bytes 1810432 | tf_op jit(solution)/shard_map/all_gather | solution.py:234
Sparse Core Ops, SparseCore 0:
  11.2 130.6 all-gather.6
  154.3 49.1 all-gather.4

commit v11 on v9

--- a/solution.py
+++ b/solution.py
@@ -71,8 +71,6 @@
         cp = pltpu.make_async_copy(p_ref.at[q], recv.at[q, d], osem.at[q])
         cp.start()
         own.append(cp)
-    for cp in own:
-        cp.wait()
 
     def origin(q, k):
         dev, pos, sgn = flows[q]
@@ -83,19 +81,22 @@
         h = jnp.dot(tw_ref[2 * o + q % 2], recv[q, o], preferred_element_type=jnp.float32)
         return g, h
 
-    def step(k, carry):
+    def step(k, carry, first=False):
         copies = []
         origins = []
         for q in range(4):
             dev, pos, sgn = flows[q]
             o = origin(q, k)
             cp = pltpu.make_async_remote_copy(
-                src_ref=recv.at[q, o], dst_ref=recv.at[q, o],
+                src_ref=p_ref.at[q] if first else recv.at[q, o], dst_ref=recv.at[q, o],
                 send_sem=ssem.at[q, k], recv_sem=rsem.at[q, k],
                 device_id=(dev(pos + sgn + n), t), device_id_type=MESH)
             cp.start()
             copies.append(cp)
             origins.append(o)
+        if first:
+            for cp in own:
+                cp.wait()
         parts = [contrib(q, origins[q]) for q in range(4)]
         g0 = parts[0][0] + parts[1][0]
         g1 = parts[2][0] + parts[3][0]
@@ -120,7 +121,8 @@
             cp.wait()
         return carry
 
-    lax.fori_loop(0, n - 1, step, 0)
+    step(0, 0, first=True)
+    lax.fori_loop(1, n - 1, step, 0)
     parts = [contrib(q, origin(q, n - 1)) for q in range(4)]
     acc[0] += parts[0][0] + parts[1][0]
     acc[1] += parts[2][0] + parts[3][0]

time: 287 us -> 287 us (level)
  no operation moved by 1% of the time
where the time goes in v11:
time: 287 us; the launch traced here: 285 us
  Pallas kernels  191 us (67%)
  waiting for transfers between devices  44.1 us (15%)
  matrix products  20.6 us (7%)
  local copies, waits for them, and re-layouts  15.1 us (5%)
  between operations  14.1 us (5%)
    pallas_call x1, Pallas kernels, _tw(): pl.pallas_call(functools.partial(_tw_kernel, nt, nd), out_shape=jax.Shape...  102 us
    pallas_call x1, Pallas kernels, _dp_ring(): pl.pallas_call(functools.partial(_dp_ring_kernel, n), out_shape=(jax.Shap...  89.1 us
    all_gather x1, waiting for transfers between devices, on_device(): lax.all_gather(small_weights, 'tensor', axis=1, tiled=True)  43.4 us
    dot_general x1, matrix products, on_device(): jnp.einsum('msf,cf->msc', lax.all_gather(small_weights, 'tensor', axis=1,...  20.6 us
  transfers between devices with their start and end apart: 1, of which 1 were waited for; matrix products, arithmetic and copies ran while one was open for 3% of the time, Pallas kernels for 36%

profile of v11, /device:TPU:6, one launch (start us, length us, event | category | flops | bytes accessed | tf_op | source)
XLA Modules:
  0.0 284.6 jit_solution(5396676508280681581)
XLA Ops:
  7.2 0.0 all-gather.2.cloned.1.call-start
  7.2 0.7 all-gather.2.cloned.1.call-update
  7.9 4.3 %copy.15 = bf16[512,3328]{0,1:T(8,128)(2,1)S(1)} copy(bf16[512,3328]{1,0:T(8,128)(2,1)} %param.7) | data formatting | bytes 6815744 | tf_op args[3]
  12.2 0.0 copy-start.1
  12.2 4.0 %copy.16 = bf16[512,8,2,208]{3,0,2,1:T(8,128)(2,1)} copy(bf16[512,8,2,208]{0,3,2,1:T(8,128)(2,1)S(1)} %bitcast.8) | data formatting | bytes 6815744 | tf_op jit(solution)/shard_map/reshape | solution.py:313
  16.2 1.1 constant_dynamic-slice_fusion.wcol_ref
  17.3 0.0 copy-done.1
  17.3 101.6 %shard_map.59.tw_ref = bf16[16,256,208]{2,1,0:T(8,128)(2,1)S(1)} custom-call(bf16[256,256]{1,0:T(8,128)(2,1)S(1)} %copy-done.1, bf16[512,208]{1,0:T(8,128)(2,1)S(1)} %constant_dynamic-slice_fusion.wcol_ref), custom_call_target="tpu_custom_call" | custom-call | flops 436207616 | bytes 7208960 | tf_op jit(solution)/shard_map/pallas_call | solution.py:272
  118.9 0.0 copy-start
  118.9 1.3 copy-done
  120.2 43.4 %all-gather.2.cloned.1.call-done = bf16[2,416,8960]{2,0,1:T(2,128)(2,1)} async-done(((bf16[2,26,8960]{2,0,1:T(2,128)(2,1)}), bf16[2,416,8960]{2,0,1:T(2,128)(2,1)}) %all-gather.2.cloned.1.call-update) | async-done | bytes 14909456 | tf_op jit(solution)/shard_map/all_gather | solution.py:308
  163.7 20.6 %fusion.3 = bf16[2,416,688]{2,1,0:T(8,128)(2,1)} fusion(bf16[688,8960]{1,0:T(8,128)(2,1)} %param.6, bf16[2,416,8960]{2,0,1:T(2,128)(2,1)} %all-gather.2.cloned.1.call-done), kind=kOutput, calls=%fused_computation.3 | convolution fusion | flops 10258267136 | bytes 28383232 | tf_op jit(solution)/shard_map/msf,cf->msc/dot_general | solution.py:306
  184.2 89.1 %shard_map.60 = (bf16[2,512,688]{2,1,0:T(8,128)(2,1)}, bf16[256,688]{1,0:T(8,128)(2,1)}) custom-call(bf16[4,208,688]{2,1,0:T(8,128)(2,1)} %bitcast.10, bf16[8,2,512,208]{3,2,1,0:T(8,128)(2,1)} %bitcast.9, bf16[16,256,208]{2,1,0:T(8,128)(2,1)} %copy-done), custom_call_target="tpu_custom_call" | custom-call | flops 7033847808 | bytes 9158656 | tf_op jit(solution)/shard_map/pallas_call | solution.py:140
  273.3 2.5 copy.17
  275.9 1.9 copy.18
Async XLA Ops:
  7.2 156.5 %all-gather.2.cloned.1.call-start = ((), (), s32[]{:S(2)}) async-start(), calls=%async_computation | async-start | bytes 15841280 | tf_op jit(solution)/shard_map/all_gather | solution.py:308
  12.2 5.1 %copy-start.1 = (bf16[256,256]{1,0:T(8,128)(2,1)S(1)}, bf16[256,256]{1,0:T(8,128)(2,1)}, u32[]{:S(2)}) copy-start(bf16[256,256]{1,0:T(8,128)(2,1)} %tok_ref.1) | copy-start | bytes 393220
  118.9 1.3 copy-start
Sparse Core Ops, SparseCore 0:
  10.5 153.0 all-gather.1

commit v12 on v10

--- a/solution.py
+++ b/solution.py
@@ -40,7 +40,7 @@
     return d + c * (1 - 2 * y) * 4
 
 
-def _dp_ring_kernel(n, p_ref, w3_ref, grown_ref, pall_ref, recv, acc, ssem, rsem, lsem, osem):
+def _dp_ring_kernel(n, p_ref, w3_ref, tw_ref, grown_ref, hid_ref, recv, acc, pre, ssem, rsem, osem):
     t = lax.axis_index("tensor")
     d = lax.axis_index("dp")
     c = t % 2
@@ -59,6 +59,7 @@
         (dev_b, pos_b, 1),
         (dev_b, pos_b, -1),
     ]
+    xw = tw_ref.shape[2]
 
     barrier = pltpu.get_barrier_semaphore()
     for dev, pos, sgn in flows:
@@ -72,15 +73,16 @@
         own.append(cp)
     for cp in own:
         cp.wait()
-    for q in range(4):
-        pltpu.make_async_copy(recv.at[q, d], pall_ref.at[q // 2, d, q % 2], lsem.at[q, d]).start()
 
     def origin(q, k):
         dev, pos, sgn = flows[q]
         return dev(pos - sgn * k + n)
 
     def contrib(q, o):
-        return jnp.dot(w3_ref[o, q % 2], recv[q, o], preferred_element_type=jnp.float32)
+        g = jnp.dot(w3_ref[o, q % 2], recv[q, o], preferred_element_type=jnp.float32)
+        h = jnp.dot(tw_ref[(t - 2 * o - q % 2 + 2 * n) % tw_ref.shape[0]], recv[q, o],
+                    preferred_element_type=jnp.float32)
+        return g, h
 
     def step(k, carry):
         copies = []
@@ -96,60 +98,65 @@
             copies.append(cp)
             origins.append(o)
         parts = [contrib(q, origins[q]) for q in range(4)]
-        g0 = parts[0] + parts[1]
-        g1 = parts[2] + parts[3]
+        g0 = parts[0][0] + parts[1][0]
+        g1 = parts[2][0] + parts[3][0]
+        h0 = parts[0][1] + parts[1][1]
+        h1 = parts[2][1] + parts[3][1]
 
         @pl.when(k == 0)
         def _():
             acc[0] = g0
             acc[1] = g1
+            pre[0] = h0
+            pre[1] = h1
 
         @pl.when(k > 0)
         def _():
             acc[0] += g0
             acc[1] += g1
-
-        for q in range(4):
-            copies[q].wait()
-            nxt = origin(q, k + 1)
-            pltpu.make_async_copy(recv.at[q, nxt], pall_ref.at[q // 2, nxt, q % 2], lsem.at[q, nxt]).start()
+            pre[0] += h0
+            pre[1] += h1
+
+        for cp in copies:
+            cp.wait()
         return carry
 
     lax.fori_loop(0, n - 1, step, 0)
     parts = [contrib(q, origin(q, n - 1)) for q in range(4)]
-    acc[0] += parts[0] + parts[1]
-    acc[1] += parts[2] + parts[3]
+    acc[0] += parts[0][0] + parts[1][0]
+    acc[1] += parts[2][0] + parts[3][0]
     grown_ref[...] = acc[...].astype(grown_ref.dtype)
-    for q in range(4):
-        for o in range(n):
-            pltpu.make_async_copy(recv.at[q, o], pall_ref.at[q // 2, o, q % 2], lsem.at[q, o]).wait()
-
-
-def _dp_ring(quarters, w3h):
+    gate = pre[0] + parts[0][1] + parts[1][1]
+    up = pre[1] + parts[2][1] + parts[3][1]
+    hid_ref[...] = (gate / (1.0 + jnp.exp(-gate)) * up).astype(hid_ref.dtype)
+
+
+def _dp_ring(quarters, w3h, tw_blocks):
     n, _, rows, hb = w3h.shape
     _, _, cols = quarters.shape
-    flops = 2 * 2 * rows * hb * 2 * cols * n
+    nt, tok, xw = tw_blocks.shape
+    flops = 2 * 2 * rows * hb * 2 * cols * n + 2 * 2 * tok * xw * nt * cols
     return pl.pallas_call(
         functools.partial(_dp_ring_kernel, n),
         out_shape=(
             jax.ShapeDtypeStruct((2, rows, cols), jnp.bfloat16),
-            jax.ShapeDtypeStruct((2, n, 2, hb, cols), jnp.bfloat16),
+            jax.ShapeDtypeStruct((tok, cols), jnp.bfloat16),
         ),
-        in_specs=[pl.BlockSpec(memory_space=pltpu.VMEM)] * 2,
-        out_specs=(pl.BlockSpec(memory_space=pltpu.VMEM), pl.BlockSpec(memory_space=pl.ANY)),
+        in_specs=[pl.BlockSpec(memory_space=pltpu.VMEM)] * 3,
+        out_specs=(pl.BlockSpec(memory_space=pltpu.VMEM), pl.BlockSpec(memory_space=pltpu.VMEM)),
         scratch_shapes=[
             pltpu.VMEM((4, n, hb, cols), jnp.bfloat16),
             pltpu.VMEM((2, rows, cols), jnp.float32),
+            pltpu.VMEM((2, tok, cols), jnp.float32),
             pltpu.SemaphoreType.DMA((4, n - 1)),
             pltpu.SemaphoreType.DMA((4, n - 1)),
-            pltpu.SemaphoreType.DMA((4, n)),
             pltpu.SemaphoreType.DMA((4,)),
         ],
         compiler_params=pltpu.CompilerParams(
             collective_id=0, has_side_effects=True, vmem_limit_bytes=56 * 1024 * 1024),
         cost_estimate=pl.CostEstimate(
-            flops=flops, transcendentals=0, bytes_accessed=4 * n * hb * cols * 2),
-    )(quarters, w3h)
+            flops=flops, transcendentals=tok * cols, bytes_accessed=4 * n * hb * cols * 2),
+    )(quarters, w3h, tw_blocks)
 
 
 def _wg_kernel(nd, wcol_ref, out_ref, wbuf, ws_sem, wr_sem, l_sem):
@@ -231,7 +238,13 @@
     t_full = g[:, m * per_dev:, :].reshape(n_t, t_rows * fs)[:, : tok * rb].reshape(n_t, tok, rb)
     t_row = t_full.transpose(1, 0, 2).reshape(tok, n_t * rb)
     tw_part = jnp.dot(t_row, w_gath.reshape(n_d * rows, xw), preferred_element_type=jnp.float32)
-    tw_t = lax.all_gather(tw_part.astype(jnp.bfloat16).T, "tensor", axis=0, tiled=True)
+    tw_own = tw_part.astype(jnp.bfloat16)
+    tw_blocks = tw_own[None]
+    s = 1
+    while s < n_t:
+        got = lax.ppermute(tw_blocks, "tensor", perm=[(i, (i + s) % n_t) for i in range(n_t)])
+        tw_blocks = jnp.concatenate([tw_blocks, got], axis=0)
+        s *= 2
     p_dev = jnp.einsum(
         "kjf,cf->kjc", s_part, ffn_growth, preferred_element_type=jnp.float32
     ).astype(jnp.bfloat16)
@@ -240,12 +253,7 @@
     hb = blk // 2
     w3h = width_growth.reshape(rows, n_d, 2, hb).transpose(1, 2, 0, 3)
     quarters = panels.reshape(4, hb, cols)
-    grown_weights, pall = _dp_ring(quarters, w3h)
-    all_panels = pall.reshape(m, ds, cols)
-    pre_values = jnp.einsum(
-        "st,msc->tmc", tw_t, all_panels, preferred_element_type=jnp.float32
-    )
-    hidden = (jax.nn.silu(pre_values[:, 0, :]) * pre_values[:, 1, :]).astype(jnp.bfloat16)
+    grown_weights, hidden = _dp_ring(quarters, w3h, tw_blocks)
     return (grown_weights, hidden)
 
 

time: 293 us -> 315 us (1.075)
  waiting for transfers between devices: 73.7 us -> 99.8 us
  Pallas kernels: 144 us -> 132 us
  starting transfers between devices: 0.08 us -> 10.6 us
  matrix products: 29.2 us -> 20.4 us
  local copies, waits for them, and re-layouts: 29.5 us -> 33.2 us
    all_gather x1, waiting for transfers between devices: 73.7 us -> 88.7 us  [on_device(): g = lax.all_gather(ext, 'tensor', axis=0, tiled=False)]
    ppermute x0 -> x4, waiting for transfers between devices: none -> 11.1 us  [on_device(): lax.ppermute(tw_blocks, 'tensor', perm=[(i, (i + s) % n_t) for i in range...]
    ppermute x0 -> x4, starting transfers between devices: none -> 10.6 us  [on_device(): lax.ppermute(tw_blocks, 'tensor', perm=[(i, (i + s) % n_t) for i in range...]
    pallas_call x1, Pallas kernels: 99.6 us -> 90.9 us  [_dp_ring(): pl.pallas_call(functools.partial(_dp_ring_kernel, n), out_shape=(jax.Shap...]
    dot_general x1 -> x0, matrix products: 8.41 us -> none  [on_device(): jnp.einsum('st,msc->tmc', tw_t, all_panels, preferred_element_type=jnp.fl...]
    pallas_call x0 -> x2, local copies, waits for them, and re-layouts: none -> 3.47 us  [_dp_ring(): pl.pallas_call(functools.partial(_dp_ring_kernel, n), out_shape=(jax.Shap...]
    unnamed x6 -> x16, local copies, waits for them, and re-layouts: 12.6 us -> 12 us
  transfers between devices with their start and end apart: 2 -> 5, of which waited for: 1 -> 4; matrix products, arithmetic and copies ran while one was open for 12% -> 10% of each run, Pallas kernels for 49% -> 13%
where the time goes in v12:
time: 315 us; the launch traced here: 314 us
  Pallas kernels  132 us (42%)
  waiting for transfers between devices  99.8 us (32%)
  local copies, waits for them, and re-layouts  33.2 us (11%)
  matrix products  20.4 us (6%)
  between operations  14.2 us (5%)
  starting transfers between devices  10.6 us (3%)
  other arithmetic  3.37 us (1%)
    pallas_call x1, Pallas kernels, _dp_ring(): pl.pallas_call(functools.partial(_dp_ring_kernel, n), out_shape=(jax.Shap...  90.9 us
    all_gather x1, waiting for transfers between devices, on_device(): g = lax.all_gather(ext, 'tensor', axis=0, tiled=False)  88.7 us
    pallas_call x1, Pallas kernels, _wg(): pl.pallas_call(functools.partial(_wg_kernel, nd), out_shape=jax.ShapeDtyp...  41.1 us
    dot_general x1, matrix products, on_device(): jnp.einsum('kjf,cf->kjc', s_part, ffn_growth, preferred_element_type=jnp....  17.4 us
    unnamed x16, local copies, waits for them, and re-layouts  12 us
    ppermute x4, waiting for transfers between devices, on_device(): lax.ppermute(tw_blocks, 'tensor', perm=[(i, (i + s) % n_t) for i in range...  11.1 us
    ppermute x4, starting transfers between devices, on_device(): lax.ppermute(tw_blocks, 'tensor', perm=[(i, (i + s) % n_t) for i in range...  10.6 us
  transfers between devices with their start and end apart: 5, of which 4 were waited for; matrix products, arithmetic and copies ran while one was open for 10% of the time, Pallas kernels for 13%

profile of v12, /device:TPU:6, one launch (start us, length us, event | category | flops | bytes accessed | tf_op | source)
XLA Modules:
  0.0 313.6 jit_solution(8817142530018323266)
XLA Ops:
  7.2 0.0 all-gather.4.cloned.1.call-start
  7.2 1.0 copy.40
  8.2 0.2 reshape.33
  8.4 1.3 copy.28
  9.7 0.2 reshape.31
  10.0 1.1 maximum_bitcast_fusion
  11.1 0.0 all-gather.4.cloned.1.call-update
  11.1 1.1 constant_dynamic-slice_fusion.wcol_ref
  12.3 41.1 %shard_map.59 = bf16[8,512,208]{2,1,0:T(8,128)(2,1)S(1)} custom-call(bf16[512,208]{1,0:T(8,128)(2,1)S(1)} %constant_dynamic-slice_fusion.wcol_ref), custom_call_target="tpu_custom_call" | custom-call | bytes 109051904 | tf_op jit(solution)/shard_map/pallas_call | solution.py:204
  53.3 88.7 %all-gather.4.cloned.1.call-done = bf16[16,60,8960]{2,1,0:T(8,128)(2,1)} async-done(((bf16[1,60,8960]{2,1,0:T(8,128)(2,1)}), bf16[16,60,8960]{2,1,0:T(8,128)(2,1)}) %all-gather.4.cloned.1.call-update) | async-done | bytes 17203216 | tf_op jit(solution)/shard_map/all_gather | solution.py:236
  142.0 3.0 slice.13
  145.0 0.4 copy.41
  145.4 0.1 slice.14
  145.5 1.8 copy.42
  147.3 3.9 %copy.33 = bf16[256,16,256]{0,2,1:T(8,128)(2,1)} copy(bf16[256,16,256]{2,0,1:T(8,128)(2,1)} %bitcast.31) | data formatting | bytes 4194304 | tf_op jit(solution)/shard_map/transpose | solution.py:239
  151.2 3.0 constant_dynamic-update-slice_fusion.4
  154.2 0.0 copy-start.2
  154.2 0.3 collective-permute-start
  154.5 4.1 %collective-permute-done = bf16[1,256,208]{2,1,0:T(8,128)(2,1)S(1)} collective-permute-done((bf16[1,256,208]{2,1,0:T(8,128)(2,1)S(1)}, bf16[1,256,208]{2,1,0:T(8,128)(2,1)S(1)}, u32[]{:S(2)}, u32[]{:S(2)}) %collective-permute-start) | collective-permute-done | bytes 106528 | tf_op jit(solution)/shard_map/ppermute | solution.py:245
  158.7 6.0 %collective-permute-start.1 = (bf16[2,256,208]{2,1,0:T(8,128)(2,1)S(1)}, bf16[2,256,208]{2,1,0:T(8,128)(2,1)S(1)}, u32[]{:S(2)}, u32[]{:S(2)}) collective-permute-start(bf16[2,256,208]{2,1,0:T(8,128)(2,1)S(1)} %pad_maximum_fusion.2), channel_id=1, source_target_pairs={{0,2},{1,3},{2,4},{3,5},{4,6},{5,7},{6,8},{7,9},{8,10},{9,11},{10,... | collective-permute-start | bytes 638984 | tf_op jit(solution)/shard_map/ppermute | solution.py:245
  164.7 3.9 %collective-permute-done.1 = bf16[2,256,208]{2,1,0:T(8,128)(2,1)S(1)} collective-permute-done((bf16[2,256,208]{2,1,0:T(8,128)(2,1)S(1)}, bf16[2,256,208]{2,1,0:T(8,128)(2,1)S(1)}, u32[]{:S(2)}, u32[]{:S(2)}) %collective-permute-start.1) | collective-permute-done | bytes 213024 | tf_op jit(solution)/shard_map/ppermute | solution.py:245
  168.6 0.9 pad_maximum_fusion.1
  169.5 0.0 copy-done.2
  169.5 0.0 copy-done
  169.5 1.9 collective-permute-start.2
  171.4 4.2 %copy.31 = bf16[512,3328]{0,1:T(8,128)(2,1)S(1)} copy(bf16[512,3328]{1,0:T(8,128)(2,1)} %param.7) | data formatting | bytes 6815744 | tf_op args[3]
  175.7 3.9 %copy.32 = bf16[512,8,2,208]{3,0,2,1:T(8,128)(2,1)} copy(bf16[512,8,2,208]{0,3,2,1:T(8,128)(2,1)S(1)} %bitcast.27) | data formatting | bytes 6815744 | tf_op jit(solution)/shard_map/reshape | solution.py:254
  179.6 3.1 collective-permute-done.2
  182.7 1.3 pad_maximum_fusion
  184.0 0.5 copy.35
  184.6 2.4 collective-permute-start.3
  187.0 17.4 %fusion.3 = bf16[16,52,688]{2,1,0:T(8,128)(2,1)S(1)} fusion(bf16[688,8960]{1,0:T(8,128)(2,1)} %param.6, bf16[16,60,8960]{2,1,0:T(8,128)(2,1)} %all-gather.4.cloned.1.call-done), kind=kOutput, calls=%fused_computation.3 | convolution fusion | flops 10258267136 | bytes 29530112 | tf_op jit(solution)/shard_map/kjf,cf->kjc/dot_general | solution.py:248
  204.4 0.2 copy.29
  204.6 0.4 copy.30
  205.1 0.0 copy-start.1
  205.1 1.5 reshape_reshape.3.p_ref
  206.6 0.7 constant_dynamic-update-slice_fusion.3
  207.2 0.0 copy-done.1
  207.2 0.7 constant_dynamic-update-slice_fusion.2
  207.9 1.9 constant_dynamic-update-slice_fusion.1
  209.8 0.0 collective-permute-done.3
  209.8 1.4 copy.36
  211.3 1.1 constant_dynamic-update-slice_fusion.tw_ref
  212.3 90.9 %shard_map.60 = (bf16[2,512,688]{2,1,0:T(8,128)(2,1)}, bf16[256,688]{1,0:T(8,128)(2,1)}) custom-call(bf16[4,208,688]{2,1,0:T(8,128)(2,1)} %reshape_reshape.3.p_ref, bf16[8,2,512,208]{3,2,1,0:T(8,128)(2,1)} %bitcast.33, bf16[16,256,208]{2,1,0:T(8,128)(2,1)} %constant_dynamic-update-slice_fusion.tw_ref), custom_call_target="tpu_custom_call" | custom-call | flops 7033847808 | bytes 9158656 | tf_op jit(solution)/shard_map/pallas_call | solution.py:139
  303.3 0.0 copy-start.3
  303.3 2.6 copy.37
  305.8 0.0 copy-done.3
  305.8 0.9 copy.38
  (3 shorter events, 0.1 us)
Async XLA Ops:
  7.2 134.9 %all-gather.4.cloned.1.call-start = ((), (), s32[]{:S(2)}) async-start(), calls=%async_computation | async-start | bytes 19496960 | tf_op jit(solution)/shard_map/all_gather | solution.py:236
  154.2 15.3 %copy-start.2 = (bf16[1,256,208]{2,1,0:T(8,128)(2,1)}, bf16[1,256,208]{2,1,0:T(8,128)(2,1)S(1)}, u32[]{:S(2)}) copy-start(bf16[1,256,208]{2,1,0:T(8,128)(2,1)S(1)} %get-tuple-element.11) | copy-start | bytes 319492
  154.2 4.4 %collective-permute-start = (bf16[1,256,208]{2,1,0:T(8,128)(2,1)S(1)}, bf16[1,256,208]{2,1,0:T(8,128)(2,1)S(1)}, u32[]{:S(2)}, u32[]{:S(2)}) collective-permute-start(bf16[1,256,208]{2,1,0:T(8,128)(2,1)S(1)} %get-tuple-element.11), channel_id=1, source_target_pairs={{0,1},{1,2},{2,3},{3,4},{4,5},{5,6},{6,7},{7,8},{8,9},{9,10},{10,1... | collective-permute-start | bytes 319496 | tf_op jit(solution)/shard_map/ppermute | solution.py:245
  158.7 9.9 %collective-permute-start.1 = (bf16[2,256,208]{2,1,0:T(8,128)(2,1)S(1)}, bf16[2,256,208]{2,1,0:T(8,128)(2,1)S(1)}, u32[]{:S(2)}, u32[]{:S(2)}) collective-permute-start(bf16[2,256,208]{2,1,0:T(8,128)(2,1)S(1)} %pad_maximum_fusion.2), channel_id=1, source_target_pairs={{0,2},{1,3},{2,4},{3,5},{4,6},{5,7},{6,8},{7,9},{8,10},{9,11},{10,... | collective-permute-start | bytes 638984 | tf_op jit(solution)/shard_map/ppermute | solution.py:245
  168.6 0.9 copy-start
  169.5 13.2 %collective-permute-start.2 = (bf16[4,256,208]{2,1,0:T(8,128)(2,1)}, bf16[4,256,208]{2,1,0:T(8,128)(2,1)}, u32[]{:S(2)}, u32[]{:S(2)}) collective-permute-start(bf16[4,256,208]{2,1,0:T(8,128)(2,1)} %pad_maximum_fusion.1), channel_id=1, source_target_pairs={{0,4},{1,5},{2,6},{3,7},{4,8},{5,9},{6,10},{7,11},{8,12},{9,13},{1... | collective-permute-start | bytes 1277960 | tf_op jit(solution)/shard_map/ppermute | solution.py:245
  184.6 25.3 %collective-permute-start.3 = (bf16[8,256,208]{1,2,0:T(8,128)(2,1)S(1)}, bf16[8,256,208]{1,2,0:T(8,128)(2,1)}, u32[]{:S(2)}, u32[]{:S(2)}) collective-permute-start(bf16[8,256,208]{1,2,0:T(8,128)(2,1)S(1)} %copy.35), channel_id=1, source_target_pairs={{0,8},{1,9},{2,10},{3,11},{4,12},{5,13},{6,14},{7,15},{8,0},{9,1},... | collective-permute-start | bytes 2555912 | tf_op jit(solution)/shard_map/ppermute | solution.py:245
  205.1 2.2 copy-start.1
  303.3 2.6 copy-start.3
Sparse Core Ops, SparseCore 0:
  11.2 130.7 all-gather.3

commit v13 on v9

--- a/solution.py
+++ b/solution.py
@@ -80,7 +80,8 @@
 
     def contrib(q, o):
         g = jnp.dot(w3_ref[o, q % 2], recv[q, o], preferred_element_type=jnp.float32)
-        h = jnp.dot(tw_ref[2 * o + q % 2], recv[q, o], preferred_element_type=jnp.float32)
+        h = jnp.dot(tw_ref[(t - 2 * o - q % 2 + 2 * n) % tw_ref.shape[0]], recv[q, o],
+                    preferred_element_type=jnp.float32)
         return g, h
 
     def step(k, carry):
@@ -163,35 +164,28 @@
     t = lax.axis_index("tensor")
     d = lax.axis_index("dp")
     rb = tok_ref.shape[1]
+    shifts = []
+    s = 1
+    while s < nt:
+        shifts.append(s)
+        s *= 2
+    peers = sorted({s for s in shifts} | {nt - s for s in shifts})
 
     barrier = pltpu.get_barrier_semaphore()
-
-    def greet_t(j, c):
-        pl.semaphore_signal(barrier, inc=1, device_id=(d, (t + j) % nt), device_id_type=MESH)
-        return c
+    for s in peers:
+        pl.semaphore_signal(barrier, inc=1, device_id=(d, (t + s) % nt), device_id_type=MESH)
 
     def greet_d(j, c):
         pl.semaphore_signal(barrier, inc=1, device_id=((d + j) % nd, t), device_id_type=MESH)
         return c
 
-    lax.fori_loop(1, nt, greet_t, 0)
     lax.fori_loop(1, nd, greet_d, 0)
-    pl.semaphore_wait(barrier, nt - 1 + nd - 1)
-
-    c0 = pltpu.make_async_copy(tok_ref, tbuf.at[t], l_sem.at[0])
+    pl.semaphore_wait(barrier, len(peers) + nd - 1)
+
+    c0 = pltpu.make_async_copy(tok_ref, tbuf.at[0], l_sem.at[0])
     c1 = pltpu.make_async_copy(wcol_ref, wbuf.at[d], l_sem.at[1])
     c0.start()
     c1.start()
-
-    def t_copy(p):
-        return pltpu.make_async_remote_copy(
-            src_ref=tok_ref, dst_ref=tbuf.at[t], send_sem=ts_sem.at[p], recv_sem=tr_sem.at[t],
-            device_id=(d, p), device_id_type=MESH)
-
-    def t_recv(p):
-        return pltpu.make_async_remote_copy(
-            src_ref=tok_ref, dst_ref=tbuf.at[p], send_sem=ts_sem.at[p], recv_sem=tr_sem.at[p],
-            device_id=(d, p), device_id_type=MESH)
 
     def w_copy(p):
         return pltpu.make_async_remote_copy(
@@ -203,22 +197,23 @@
             src_ref=wcol_ref, dst_ref=wbuf.at[p], send_sem=ws_sem.at[p], recv_sem=wr_sem.at[p],
             device_id=(p, t), device_id_type=MESH)
 
-    def send_t(j, c):
-        t_copy((t + j) % nt).start()
-        return c
-
     def send_d(j, c):
         w_copy((d + j) % nd).start()
         return c
 
-    lax.fori_loop(1, nt, send_t, 0)
     lax.fori_loop(1, nd, send_d, 0)
-
-    def wait_t(j, c):
-        p = (t + j) % nt
-        t_copy(p).wait_send()
-        t_recv(p).wait_recv()
-        return c
+    c0.wait()
+
+    def doubling(buf, s_sem, r_sem):
+        for r, s in enumerate(shifts):
+            cp = pltpu.make_async_remote_copy(
+                src_ref=buf.at[pl.ds(0, s)], dst_ref=buf.at[pl.ds(s, s)],
+                send_sem=s_sem.at[r], recv_sem=r_sem.at[r],
+                device_id=(d, (t + s) % nt), device_id_type=MESH)
+            cp.start()
+            cp.wait()
+
+    doubling(tbuf, ts_sem, tr_sem)
 
     def wait_d(j, c):
         p = (d + j) % nd
@@ -226,46 +221,25 @@
         w_recv(p).wait_recv()
         return c
 
-    lax.fori_loop(1, nt, wait_t, 0)
     lax.fori_loop(1, nd, wait_d, 0)
-    c0.wait()
     c1.wait()
 
     per = nt // nd
     acc = None
-    for q in range(nt):
-        part = jnp.dot(tbuf[q], wbuf[q // per, pl.ds((q % per) * rb, rb), :],
+    for j in range(nt):
+        q = (t - j + nt) % nt
+        off = pl.multiple_of((q % per) * rb, rb)
+        part = jnp.dot(tbuf[j], wbuf[q // per, pl.ds(off, rb), :],
                        preferred_element_type=jnp.float32)
         acc = part if acc is None else acc + part
-    xbuf[t] = acc.astype(xbuf.dtype)
-
-    def x_copy(p):
-        return pltpu.make_async_remote_copy(
-            src_ref=xbuf.at[t], dst_ref=xbuf.at[t], send_sem=xs_sem.at[p], recv_sem=xr_sem.at[t],
-            device_id=(d, p), device_id_type=MESH)
-
-    def x_recv(p):
-        return pltpu.make_async_remote_copy(
-            src_ref=xbuf.at[p], dst_ref=xbuf.at[p], send_sem=xs_sem.at[p], recv_sem=xr_sem.at[p],
-            device_id=(d, p), device_id_type=MESH)
-
-    def send_x(j, c):
-        x_copy((t + j) % nt).start()
-        return c
-
-    def wait_x(j, c):
-        p = (t + j) % nt
-        x_copy(p).wait_send()
-        x_recv(p).wait_recv()
-        return c
-
-    lax.fori_loop(1, nt, send_x, 0)
-    lax.fori_loop(1, nt, wait_x, 0)
+    xbuf[0] = acc.astype(xbuf.dtype)
+    doubling(xbuf, xs_sem, xr_sem)
     out_ref[...] = xbuf[...]
 
 
 def _tw(tokens, wcol, nt, nd):
     tok, rb = tokens.shape
+    rounds = max(1, (nt - 1).bit_length())
     rows, xw = wcol.shape
     return pl.pallas_call(
         functools.partial(_tw_kernel, nt, nd),
@@ -276,12 +250,12 @@
             pltpu.VMEM((nt, tok, rb), jnp.bfloat16),
             pltpu.VMEM((nd, rows, xw), jnp.bfloat16),
             pltpu.VMEM((nt, tok, xw), jnp.bfloat16),
-            pltpu.SemaphoreType.DMA((nt,)),
-            pltpu.SemaphoreType.DMA((nt,)),
+            pltpu.SemaphoreType.DMA((rounds,)),
+            pltpu.SemaphoreType.DMA((rounds,)),
             pltpu.SemaphoreType.DMA((nd,)),
             pltpu.SemaphoreType.DMA((nd,)),
-            pltpu.SemaphoreType.DMA((nt,)),
-            pltpu.SemaphoreType.DMA((nt,)),
+            pltpu.SemaphoreType.DMA((rounds,)),
+            pltpu.SemaphoreType.DMA((rounds,)),
             pltpu.SemaphoreType.DMA((2,)),
         ],
         compiler_params=pltpu.CompilerParams(

time: 287 us -> 317 us (1.10)
  Pallas kernels: 191 us -> 267 us
  waiting for transfers between devices: 44.1 us -> 0.68 us
    pallas_call x1, Pallas kernels: 102 us -> 173 us  [_tw(): pl.pallas_call(functools.partial(_tw_kernel, nt, nd), out_shape=jax.Shape...]
    all_gather x1, waiting for transfers between devices: 43.4 us -> 0.01 us  [on_device(): lax.all_gather(small_weights, 'tensor', axis=1, tiled=True)]
    pallas_call x1, Pallas kernels: 88.9 us -> 93.3 us  [_dp_ring(): pl.pallas_call(functools.partial(_dp_ring_kernel, n), out_shape=(jax.Shap...]
  transfers between devices with their start and end apart: 1 -> 1, of which waited for: 1 -> 0; matrix products, arithmetic and copies ran while one was open for 3% -> 3% of each run, Pallas kernels for 36% -> 55%
where the time goes in v13:
time: 317 us
  Pallas kernels  267 us (84%)
  matrix products  20.6 us (6%)
  local copies, waits for them, and re-layouts  15.1 us (5%)
  between operations  14.1 us (4%)
    pallas_call x1, Pallas kernels, _tw(): pl.pallas_call(functools.partial(_tw_kernel, nt, nd), out_shape=jax.Shape...  173 us
    pallas_call x1, Pallas kernels, _dp_ring(): pl.pallas_call(functools.partial(_dp_ring_kernel, n), out_shape=(jax.Shap...  93.3 us
    dot_general x1, matrix products, on_device(): jnp.einsum('msf,cf->msc', lax.all_gather(small_weights, 'tensor', axis=1,...  20.6 us
  transfers between devices with their start and end apart: 1, of which 0 were waited for; matrix products, arithmetic and copies ran while one was open for 3% of the time, Pallas kernels for 55%

profile of v13, /device:TPU:6, one launch (start us, length us, event | category | flops | bytes accessed | tf_op | source)
XLA Modules:
  0.0 317.0 jit_solution(421256199479054297)
XLA Ops:
  7.2 0.0 all-gather.2.cloned.1.call-start
  7.2 0.7 all-gather.2.cloned.1.call-update
  7.9 4.3 %copy.15 = bf16[512,3328]{0,1:T(8,128)(2,1)S(1)} copy(bf16[512,3328]{1,0:T(8,128)(2,1)} %param.7) | data formatting | bytes 6815744 | tf_op args[3]
  12.2 0.0 copy-start.1
  12.2 4.0 %copy.16 = bf16[512,8,2,208]{3,0,2,1:T(8,128)(2,1)} copy(bf16[512,8,2,208]{0,3,2,1:T(8,128)(2,1)S(1)} %bitcast.8) | data formatting | bytes 6815744 | tf_op jit(solution)/shard_map/reshape | solution.py:285
  16.2 1.1 constant_dynamic-slice_fusion.wcol_ref
  17.3 0.0 copy-done.1
  17.3 173.3 %shard_map.59.tw_ref = bf16[16,256,208]{2,1,0:T(8,128)(2,1)S(1)} custom-call(bf16[256,256]{1,0:T(8,128)(2,1)S(1)} %copy-done.1, bf16[512,208]{1,0:T(8,128)(2,1)S(1)} %constant_dynamic-slice_fusion.wcol_ref), custom_call_target="tpu_custom_call" | custom-call | flops 436207616 | bytes 7208960 | tf_op jit(solution)/shard_map/pallas_call | solution.py:244
  190.6 0.0 copy-start
  190.6 1.3 copy-done
  191.9 0.0 all-gather.2.cloned.1.call-done
  191.9 20.6 %fusion.3 = bf16[2,416,688]{2,1,0:T(8,128)(2,1)} fusion(bf16[688,8960]{1,0:T(8,128)(2,1)} %param.6, bf16[2,416,8960]{2,0,1:T(2,128)(2,1)} %all-gather.2.cloned.1.call-done), kind=kOutput, calls=%fused_computation.3 | convolution fusion | flops 10258267136 | bytes 28383232 | tf_op jit(solution)/shard_map/msf,cf->msc/dot_general | solution.py:278
  212.5 93.3 %shard_map.60 = (bf16[2,512,688]{2,1,0:T(8,128)(2,1)}, bf16[256,688]{1,0:T(8,128)(2,1)}) custom-call(bf16[4,208,688]{2,1,0:T(8,128)(2,1)} %bitcast.10, bf16[8,2,512,208]{3,2,1,0:T(8,128)(2,1)} %bitcast.9, bf16[16,256,208]{2,1,0:T(8,128)(2,1)} %copy-done), custom_call_target="tpu_custom_call" | custom-call | flops 7033847808 | bytes 9158656 | tf_op jit(solution)/shard_map/pallas_call | solution.py:139
  305.8 2.5 copy.17
  308.3 1.9 copy.18
Async XLA Ops:
  7.2 184.8 %all-gather.2.cloned.1.call-start = ((), (), s32[]{:S(2)}) async-start(), calls=%async_computation | async-start | bytes 15841280 | tf_op jit(solution)/shard_map/all_gather | solution.py:280
  12.2 5.1 %copy-start.1 = (bf16[256,256]{1,0:T(8,128)(2,1)S(1)}, bf16[256,256]{1,0:T(8,128)(2,1)}, u32[]{:S(2)}) copy-start(bf16[256,256]{1,0:T(8,128)(2,1)} %tok_ref.1) | copy-start | bytes 393220
  190.6 1.3 copy-start
Sparse Core Ops, SparseCore 0:
  10.5 170.6 all-gather.1

commit v14 on v9

--- a/solution.py
+++ b/solution.py
@@ -301,12 +301,13 @@
     blk = ds // n_d
     w_cols = lax.dynamic_slice_in_dim(width_growth, t * xw, xw, axis=1)
     tw_blocks = _tw(tokens, w_cols, n_t, n_d)
-    panels = jnp.einsum(
-        "msf,cf->msc",
-        lax.all_gather(small_weights, "tensor", axis=1, tiled=True),
-        ffn_growth,
-        preferred_element_type=jnp.float32,
+    m, per_dev, fs = small_weights.shape
+    s_dev = lax.all_gather(small_weights.reshape(m * per_dev, fs), "tensor", axis=0, tiled=False)
+    p_dev = jnp.einsum(
+        "kjf,cf->kjc", s_dev, ffn_growth, preferred_element_type=jnp.float32
     ).astype(jnp.bfloat16)
+    cols_p = p_dev.shape[2]
+    panels = p_dev.reshape(n_t, m, per_dev, cols_p).transpose(1, 0, 2, 3).reshape(m, blk, cols_p)
     hb = blk // 2
     w3h = width_growth.reshape(rows, n_d, 2, hb).transpose(1, 2, 0, 3)
     quarters = panels.reshape(4, hb, panels.shape[2])

time: 287 us -> 293 us (1.021)
  waiting for transfers between devices: 44.1 us -> 49 us
  local copies, waits for them, and re-layouts: 15.1 us -> 19.7 us
  matrix products: 20.6 us -> 17.5 us
    all_gather x1, waiting for transfers between devices: 43.4 us -> 49 us  [on_device(): lax.all_gather(small_weights.reshape(m * per_dev, fs), 'tensor', axis=0,...]
    dot_general x1, matrix products: 20.6 us -> 17.5 us  [on_device(): jnp.einsum('kjf,cf->kjc', s_dev, ffn_growth, preferred_element_type=jnp.f...]
    unnamed x5 -> x6, local copies, waits for them, and re-layouts: 5.57 us -> 6.94 us
  transfers between devices with their start and end apart: 1 -> 1, of which waited for: 1 -> 1; matrix products, arithmetic and copies ran while one was open for 3% -> 3% of each run, Pallas kernels for 36% -> 35%
where the time goes in v14:
time: 293 us; the launch traced here: 290 us
  Pallas kernels  190 us (65%)
  waiting for transfers between devices  49 us (17%)
  local copies, waits for them, and re-layouts  19.7 us (7%)
  matrix products  17.5 us (6%)
  between operations  14.1 us (5%)
    pallas_call x1, Pallas kernels, _tw(): pl.pallas_call(functools.partial(_tw_kernel, nt, nd), out_shape=jax.Shape...  102 us
    pallas_call x1, Pallas kernels, _dp_ring(): pl.pallas_call(functools.partial(_dp_ring_kernel, n), out_shape=(jax.Shap...  88.3 us
    all_gather x1, waiting for transfers between devices, on_device(): lax.all_gather(small_weights.reshape(m * per_dev, fs), 'tensor', axis=0,...  49 us
    dot_general x1, matrix products, on_device(): jnp.einsum('kjf,cf->kjc', s_dev, ffn_growth, preferred_element_type=jnp.f...  17.5 us
    unnamed x6, local copies, waits for them, and re-layouts  6.94 us
  transfers between devices with their start and end apart: 1, of which 1 were waited for; matrix products, arithmetic and copies ran while one was open for 3% of the time, Pallas kernels for 35%

profile of v14, /device:TPU:6, one launch (start us, length us, event | category | flops | bytes accessed | tf_op | source)
XLA Modules:
  0.0 290.5 jit_solution(16256016813562653609)
XLA Ops:
  7.2 0.0 all-gather.2.cloned.1.call-start
  7.2 1.3 copy.17
  8.5 1.2 all_gather_reshape.3
  9.7 0.0 all-gather.2.cloned.1.call-update
  9.7 4.3 %copy.20 = bf16[512,3328]{0,1:T(8,128)(2,1)S(1)} copy(bf16[512,3328]{1,0:T(8,128)(2,1)} %param.7) | data formatting | bytes 6815744 | tf_op args[3]
  14.0 0.0 copy-start.1
  14.0 3.9 %copy.21 = bf16[512,8,2,208]{3,0,2,1:T(8,128)(2,1)} copy(bf16[512,8,2,208]{0,3,2,1:T(8,128)(2,1)S(1)} %bitcast.11) | data formatting | bytes 6815744 | tf_op jit(solution)/shard_map/reshape | solution.py:312
  17.9 1.1 constant_dynamic-slice_fusion.wcol_ref
  19.1 0.0 copy-done.1
  19.1 101.8 %shard_map.59.tw_ref = bf16[16,256,208]{2,1,0:T(8,128)(2,1)S(1)} custom-call(bf16[256,256]{1,0:T(8,128)(2,1)S(1)} %copy-done.1, bf16[512,208]{1,0:T(8,128)(2,1)S(1)} %constant_dynamic-slice_fusion.wcol_ref), custom_call_target="tpu_custom_call" | custom-call | flops 436207616 | bytes 7208960 | tf_op jit(solution)/shard_map/pallas_call | solution.py:270
  120.9 0.0 copy-start
  120.9 1.4 copy-done
  122.2 49.0 %all-gather.2.cloned.1.call-done = bf16[16,52,8960]{2,1,0:T(8,128)(2,1)} async-done(((bf16[1,52,8960]{2,1,0:T(8,128)(2,1)}), bf16[16,52,8960]{2,1,0:T(8,128)(2,1)}) %all-gather.2.cloned.1.call-update) | async-done | bytes 14909456 | tf_op jit(solution)/shard_map/all_gather | solution.py:305
  171.2 17.5 %fusion.2 = bf16[16,52,688]{2,1,0:T(8,128)(2,1)S(1)} fusion(bf16[16,52,8960]{2,1,0:T(8,128)(2,1)} %all-gather.2.cloned.1.call-done, bf16[688,8960]{1,0:T(8,128)(2,1)} %param.6), kind=kOutput, calls=%fused_computation.2 | convolution fusion | flops 10258267136 | bytes 28383232 | tf_op jit(solution)/shard_map/kjf,cf->kjc/dot_general | solution.py:306
  188.7 0.2 copy.18
  188.9 0.4 copy.19
  189.4 1.5 reshape_reshape.3.p_ref
  190.9 88.3 %shard_map.60 = (bf16[2,512,688]{2,1,0:T(8,128)(2,1)}, bf16[256,688]{1,0:T(8,128)(2,1)}) custom-call(bf16[4,208,688]{2,1,0:T(8,128)(2,1)} %reshape_reshape.3.p_ref, bf16[8,2,512,208]{3,2,1,0:T(8,128)(2,1)} %bitcast.13, bf16[16,256,208]{2,1,0:T(8,128)(2,1)} %copy-done), custom_call_target="tpu_custom_call" | custom-call | flops 7033847808 | bytes 9158656 | tf_op jit(solution)/shard_map/pallas_call | solution.py:138
  279.2 2.5 copy.22
  281.7 1.9 copy.23
Async XLA Ops:
  7.2 164.1 %all-gather.2.cloned.1.call-start = ((), (), s32[]{:S(2)}) async-start(), calls=%async_computation | async-start | bytes 17059840 | tf_op jit(solution)/shard_map/all_gather | solution.py:305
  14.0 5.1 %copy-start.1 = (bf16[256,256]{1,0:T(8,128)(2,1)S(1)}, bf16[256,256]{1,0:T(8,128)(2,1)}, u32[]{:S(2)}) copy-start(bf16[256,256]{1,0:T(8,128)(2,1)} %tok_ref.1) | copy-start | bytes 393220
  120.9 1.4 copy-start
Sparse Core Ops, SparseCore 0:
  10.9 160.2 all-gather.1

commit v15 on v9

--- a/solution.py
+++ b/solution.py
@@ -301,11 +301,9 @@
     blk = ds // n_d
     w_cols = lax.dynamic_slice_in_dim(width_growth, t * xw, xw, axis=1)
     tw_blocks = _tw(tokens, w_cols, n_t, n_d)
+    s_rows = lax.all_gather(small_weights.transpose(1, 0, 2), "tensor", axis=0, tiled=True)
     panels = jnp.einsum(
-        "msf,cf->msc",
-        lax.all_gather(small_weights, "tensor", axis=1, tiled=True),
-        ffn_growth,
-        preferred_element_type=jnp.float32,
+        "smf,cf->msc", s_rows, ffn_growth, preferred_element_type=jnp.float32
     ).astype(jnp.bfloat16)
     hb = blk // 2
     w3h = width_growth.reshape(rows, n_d, 2, hb).transpose(1, 2, 0, 3)

time: 287 us -> 287 us (level)
  no operation moved by 1% of the time
where the time goes in v15:
time: 287 us; the launch traced here: 285 us
  Pallas kernels  191 us (67%)
  waiting for transfers between devices  44.1 us (15%)
  matrix products  20.6 us (7%)
  local copies, waits for them, and re-layouts  15.1 us (5%)
  between operations  14.1 us (5%)
    pallas_call x1, Pallas kernels, _tw(): pl.pallas_call(functools.partial(_tw_kernel, nt, nd), out_shape=jax.Shape...  102 us
    pallas_call x1, Pallas kernels, _dp_ring(): pl.pallas_call(functools.partial(_dp_ring_kernel, n), out_shape=(jax.Shap...  89 us
    all_gather x1, waiting for transfers between devices, on_device(): lax.all_gather(small_weights.transpose(1, 0, 2), 'tensor', axis=0, tiled=...  43.4 us
    dot_general x1, matrix products, on_device(): jnp.einsum('smf,cf->msc', s_rows, ffn_growth, preferred_element_type=jnp....  20.6 us
  transfers between devices with their start and end apart: 1, of which 1 were waited for; matrix products, arithmetic and copies ran while one was open for 3% of the time, Pallas kernels for 36%

profile of v15, /device:TPU:6, one launch (start us, length us, event | category | flops | bytes accessed | tf_op | source)
XLA Modules:
  0.0 284.5 jit_solution(17875339611829439302)
XLA Ops:
  7.2 0.0 all-gather.2.cloned.1.call-start
  7.2 0.7 all-gather.2.cloned.1.call-update
  7.9 4.3 %copy.15 = bf16[512,3328]{0,1:T(8,128)(2,1)S(1)} copy(bf16[512,3328]{1,0:T(8,128)(2,1)} %param.7) | data formatting | bytes 6815744 | tf_op args[3]
  12.2 0.0 copy-start.1
  12.2 4.0 %copy.16 = bf16[512,8,2,208]{3,0,2,1:T(8,128)(2,1)} copy(bf16[512,8,2,208]{0,3,2,1:T(8,128)(2,1)S(1)} %bitcast.11) | data formatting | bytes 6815744 | tf_op jit(solution)/shard_map/reshape | solution.py:309
  16.2 1.1 constant_dynamic-slice_fusion.wcol_ref
  17.3 0.0 copy-done.1
  17.3 101.6 %shard_map.59.tw_ref = bf16[16,256,208]{2,1,0:T(8,128)(2,1)S(1)} custom-call(bf16[256,256]{1,0:T(8,128)(2,1)S(1)} %copy-done.1, bf16[512,208]{1,0:T(8,128)(2,1)S(1)} %constant_dynamic-slice_fusion.wcol_ref), custom_call_target="tpu_custom_call" | custom-call | flops 436207616 | bytes 7208960 | tf_op jit(solution)/shard_map/pallas_call | solution.py:270
  118.9 0.0 copy-start
  118.9 1.3 copy-done
  120.2 43.4 %all-gather.2.cloned.1.call-done = bf16[416,2,8960]{2,1,0:T(2,128)(2,1)} async-done(((bf16[26,2,8960]{2,1,0:T(2,128)(2,1)}), bf16[416,2,8960]{2,1,0:T(2,128)(2,1)}) %all-gather.2.cloned.1.call-update) | async-done | bytes 14909456 | tf_op jit(solution)/shard_map/all_gather | solution.py:304
  163.7 20.6 %fusion.3 = bf16[688,416,2]{0,1,2:T(8,128)(2,1)} fusion(bf16[416,2,8960]{2,1,0:T(2,128)(2,1)} %all-gather.2.cloned.1.call-done, bf16[688,8960]{1,0:T(8,128)(2,1)} %param.6), kind=kOutput, calls=%fused_computation.3 | convolution fusion | flops 10258267136 | bytes 28383232 | tf_op jit(solution)/shard_map/smf,cf->msc/dot_general | solution.py:305
  184.3 89.0 %shard_map.60 = (bf16[2,512,688]{2,1,0:T(8,128)(2,1)}, bf16[256,688]{1,0:T(8,128)(2,1)}) custom-call(bf16[4,208,688]{2,1,0:T(8,128)(2,1)} %bitcast.14, bf16[8,2,512,208]{3,2,1,0:T(8,128)(2,1)} %bitcast.12, bf16[16,256,208]{2,1,0:T(8,128)(2,1)} %copy-done), custom_call_target="tpu_custom_call" | custom-call | flops 7033847808 | bytes 9158656 | tf_op jit(solution)/shard_map/pallas_call | solution.py:138
  273.3 2.5 copy.17
  275.8 1.9 copy.18
Async XLA Ops:
  7.2 156.5 %all-gather.2.cloned.1.call-start = ((), (), s32[]{:S(2)}) async-start(), calls=%async_computation | async-start | bytes 15841280 | tf_op jit(solution)/shard_map/all_gather | solution.py:304
  12.2 5.1 %copy-start.1 = (bf16[256,256]{1,0:T(8,128)(2,1)S(1)}, bf16[256,256]{1,0:T(8,128)(2,1)}, u32[]{:S(2)}) copy-start(bf16[256,256]{1,0:T(8,128)(2,1)} %tok_ref.1) | copy-start | bytes 393220
  118.9 1.3 copy-start
Sparse Core Ops, SparseCore 0:
  10.5 153.0 all-gather.1

commit v16 on v15

--- a/solution.py
+++ b/solution.py
@@ -124,10 +124,11 @@
     parts = [contrib(q, origin(q, n - 1)) for q in range(4)]
     acc[0] += parts[0][0] + parts[1][0]
     acc[1] += parts[2][0] + parts[3][0]
-    grown_ref[...] = acc[...].astype(grown_ref.dtype)
+    for mm in range(2):
+        grown_ref[mm] = acc[mm].T.astype(grown_ref.dtype)
     gate = pre[0] + parts[0][1] + parts[1][1]
     up = pre[1] + parts[2][1] + parts[3][1]
-    hid_ref[...] = (gate / (1.0 + jnp.exp(-gate)) * up).astype(hid_ref.dtype)
+    hid_ref[...] = (gate / (1.0 + jnp.exp(-gate)) * up).T.astype(hid_ref.dtype)
 
 
 def _dp_ring(quarters, w3h, tw_blocks):
@@ -138,8 +139,8 @@
     return pl.pallas_call(
         functools.partial(_dp_ring_kernel, n),
         out_shape=(
-            jax.ShapeDtypeStruct((2, rows, cols), jnp.bfloat16),
-            jax.ShapeDtypeStruct((tok, cols), jnp.bfloat16),
+            jax.ShapeDtypeStruct((2, cols, rows), jnp.bfloat16),
+            jax.ShapeDtypeStruct((cols, tok), jnp.bfloat16),
         ),
         in_specs=[pl.BlockSpec(memory_space=pltpu.VMEM)] * 3,
         out_specs=(pl.BlockSpec(memory_space=pltpu.VMEM), pl.BlockSpec(memory_space=pltpu.VMEM)),
@@ -308,7 +309,9 @@
     hb = blk // 2
     w3h = width_growth.reshape(rows, n_d, 2, hb).transpose(1, 2, 0, 3)
     quarters = panels.reshape(4, hb, panels.shape[2])
-    grown_weights, hidden = _dp_ring(quarters, w3h, tw_blocks)
+    grown_t, hidden_t = _dp_ring(quarters, w3h, tw_blocks)
+    grown_weights = grown_t.transpose(0, 2, 1)
+    hidden = hidden_t.T
     return (grown_weights, hidden)
 
 

time: 287 us -> 287 us (level)
    pallas_call x2 -> x0, local copies, waits for them, and re-layouts: 4.42 us -> none  [_dp_ring(): pl.pallas_call(functools.partial(_dp_ring_kernel, n), out_shape=(jax.Shap...]
    unnamed x5 -> x7, local copies, waits for them, and re-layouts: 5.57 us -> 9.84 us
where the time goes in v16:
time: 287 us; the launch traced here: 285 us
  Pallas kernels  191 us (67%)
  waiting for transfers between devices  44.1 us (15%)
  matrix products  20.6 us (7%)
  local copies, waits for them, and re-layouts  14.9 us (5%)
  between operations  14.1 us (5%)
    pallas_call x1, Pallas kernels, _tw(): pl.pallas_call(functools.partial(_tw_kernel, nt, nd), out_shape=jax.Shape...  102 us
    pallas_call x1, Pallas kernels, _dp_ring(): pl.pallas_call(functools.partial(_dp_ring_kernel, n), out_shape=(jax.Shap...  89.2 us
    all_gather x1, waiting for transfers between devices, on_device(): lax.all_gather(small_weights.transpose(1, 0, 2), 'tensor', axis=0, tiled=...  43.4 us
    dot_general x1, matrix products, on_device(): jnp.einsum('smf,cf->msc', s_rows, ffn_growth, preferred_element_type=jnp....  20.6 us
    unnamed x7, local copies, waits for them, and re-layouts  9.84 us
  transfers between devices with their start and end apart: 1, of which 1 were waited for; matrix products, arithmetic and copies ran while one was open for 3% of the time, Pallas kernels for 36%

profile of v16, /device:TPU:6, one launch (start us, length us, event | category | flops | bytes accessed | tf_op | source)
XLA Modules:
  0.0 284.6 jit_solution(14684120939545258678)
XLA Ops:
  7.2 0.0 all-gather.2.cloned.1.call-start
  7.2 0.7 all-gather.2.cloned.1.call-update
  7.9 4.3 %copy.11 = bf16[512,3328]{0,1:T(8,128)(2,1)S(1)} copy(bf16[512,3328]{1,0:T(8,128)(2,1)} %param.7) | data formatting | bytes 6815744 | tf_op args[3]
  12.2 0.0 copy-start.1
  12.2 4.0 %copy.12 = bf16[512,8,2,208]{3,0,2,1:T(8,128)(2,1)} copy(bf16[512,8,2,208]{0,3,2,1:T(8,128)(2,1)S(1)} %bitcast.13) | data formatting | bytes 6815744 | tf_op jit(solution)/shard_map/reshape | solution.py:310
  16.2 1.1 constant_dynamic-slice_fusion.wcol_ref
  17.3 0.0 copy-done.1
  17.3 101.6 %shard_map.59.tw_ref = bf16[16,256,208]{2,1,0:T(8,128)(2,1)S(1)} custom-call(bf16[256,256]{1,0:T(8,128)(2,1)S(1)} %copy-done.1, bf16[512,208]{1,0:T(8,128)(2,1)S(1)} %constant_dynamic-slice_fusion.wcol_ref), custom_call_target="tpu_custom_call" | custom-call | flops 436207616 | bytes 7208960 | tf_op jit(solution)/shard_map/pallas_call | solution.py:271
  118.9 0.0 copy-start
  118.9 1.3 copy-done
  120.2 43.4 %all-gather.2.cloned.1.call-done = bf16[416,2,8960]{2,1,0:T(2,128)(2,1)} async-done(((bf16[26,2,8960]{2,1,0:T(2,128)(2,1)}), bf16[416,2,8960]{2,1,0:T(2,128)(2,1)}) %all-gather.2.cloned.1.call-update) | async-done | bytes 14909456 | tf_op jit(solution)/shard_map/all_gather | solution.py:305
  163.7 20.6 %fusion.3 = bf16[688,416,2]{0,1,2:T(8,128)(2,1)} fusion(bf16[416,2,8960]{2,1,0:T(2,128)(2,1)} %all-gather.2.cloned.1.call-done, bf16[688,8960]{1,0:T(8,128)(2,1)} %param.6), kind=kOutput, calls=%fused_computation.3 | convolution fusion | flops 10258267136 | bytes 28383232 | tf_op jit(solution)/shard_map/smf,cf->msc/dot_general | solution.py:306
  184.3 89.2 %shard_map.60 = (bf16[2,688,512]{2,1,0:T(8,128)(2,1)}, bf16[688,256]{1,0:T(8,128)(2,1)}) custom-call(bf16[4,208,688]{2,1,0:T(8,128)(2,1)} %bitcast.18, bf16[8,2,512,208]{3,2,1,0:T(8,128)(2,1)} %bitcast.14, bf16[16,256,208]{2,1,0:T(8,128)(2,1)} %copy-done), custom_call_target="tpu_custom_call" | custom-call | flops 7033847808 | bytes 9158656 | tf_op jit(solution)/shard_map/pallas_call | solution.py:139
  273.5 2.5 copy.19
  276.0 1.7 copy.20
Async XLA Ops:
  7.2 156.5 %all-gather.2.cloned.1.call-start = ((), (), s32[]{:S(2)}) async-start(), calls=%async_computation | async-start | bytes 15841280 | tf_op jit(solution)/shard_map/all_gather | solution.py:305
  12.2 5.1 %copy-start.1 = (bf16[256,256]{1,0:T(8,128)(2,1)S(1)}, bf16[256,256]{1,0:T(8,128)(2,1)}, u32[]{:S(2)}) copy-start(bf16[256,256]{1,0:T(8,128)(2,1)} %tok_ref.1) | copy-start | bytes 393220
  118.9 1.3 copy-start
Sparse Core Ops, SparseCore 0:
  10.5 153.0 all-gather.1

commit v17 on v15

--- a/solution.py
+++ b/solution.py
@@ -83,20 +83,25 @@
         h = jnp.dot(tw_ref[2 * o + q % 2], recv[q, o], preferred_element_type=jnp.float32)
         return g, h
 
+    hb = recv.shape[2]
+    cut = (hb // 2) // 16 * 16
+    subs = ((0, cut), (cut, hb - cut))
+
+    def send(q, sub, k):
+        dev, pos, sgn = flows[q]
+        o = origin(q, k)
+        lo, ln = subs[sub]
+        return pltpu.make_async_remote_copy(
+            src_ref=recv.at[q, o, pl.ds(lo, ln)], dst_ref=recv.at[q, o, pl.ds(lo, ln)],
+            send_sem=ssem.at[q, sub, k], recv_sem=rsem.at[q, sub, k],
+            device_id=(dev(pos + sgn + n), t), device_id_type=MESH)
+
+    for q in range(4):
+        for sub in range(2):
+            send(q, sub, 0).start()
+
     def step(k, carry):
-        copies = []
-        origins = []
-        for q in range(4):
-            dev, pos, sgn = flows[q]
-            o = origin(q, k)
-            cp = pltpu.make_async_remote_copy(
-                src_ref=recv.at[q, o], dst_ref=recv.at[q, o],
-                send_sem=ssem.at[q, k], recv_sem=rsem.at[q, k],
-                device_id=(dev(pos + sgn + n), t), device_id_type=MESH)
-            cp.start()
-            copies.append(cp)
-            origins.append(o)
-        parts = [contrib(q, origins[q]) for q in range(4)]
+        parts = [contrib(q, origin(q, k)) for q in range(4)]
         g0 = parts[0][0] + parts[1][0]
         g1 = parts[2][0] + parts[3][0]
         h0 = parts[0][1] + parts[1][1]
@@ -116,8 +121,13 @@
             pre[0] += h0
             pre[1] += h1
 
-        for cp in copies:
-            cp.wait()
+        for sub in range(2):
+            for q in range(4):
+                send(q, sub, k).wait()
+
+                @pl.when(k + 1 < n - 1)
+                def _():
+                    send(q, sub, k + 1).start()
         return carry
 
     lax.fori_loop(0, n - 1, step, 0)
@@ -147,8 +157,8 @@
             pltpu.VMEM((4, n, hb, cols), jnp.bfloat16),
             pltpu.VMEM((2, rows, cols), jnp.float32),
             pltpu.VMEM((2, tok, cols), jnp.float32),
-            pltpu.SemaphoreType.DMA((4, n - 1)),
-            pltpu.SemaphoreType.DMA((4, n - 1)),
+            pltpu.SemaphoreType.DMA((4, 2, n - 1)),
+            pltpu.SemaphoreType.DMA((4, 2, n - 1)),
             pltpu.SemaphoreType.DMA((4,)),
         ],
         compiler_params=pltpu.CompilerParams(

time: 287 us -> 281 us (0.979)
  Pallas kernels: 191 us -> 185 us
    pallas_call x1, Pallas kernels: 89 us -> 83.4 us  [_dp_ring(): pl.pallas_call(functools.partial(_dp_ring_kernel, n), out_shape=(jax.Shap...]
where the time goes in v17:
time: 281 us; the launch traced here: 279 us
  Pallas kernels  185 us (66%)
  waiting for transfers between devices  44.1 us (16%)
  matrix products  20.6 us (7%)
  local copies, waits for them, and re-layouts  15.1 us (5%)
  between operations  14.1 us (5%)
    pallas_call x1, Pallas kernels, _tw(): pl.pallas_call(functools.partial(_tw_kernel, nt, nd), out_shape=jax.Shape...  102 us
    pallas_call x1, Pallas kernels, _dp_ring(): pl.pallas_call(functools.partial(_dp_ring_kernel, n), out_shape=(jax.Shap...  83.4 us
    all_gather x1, waiting for transfers between devices, on_device(): lax.all_gather(small_weights.transpose(1, 0, 2), 'tensor', axis=0, tiled=...  43.4 us
    dot_general x1, matrix products, on_device(): jnp.einsum('smf,cf->msc', s_rows, ffn_growth, preferred_element_type=jnp....  20.6 us
  transfers between devices with their start and end apart: 1, of which 1 were waited for; matrix products, arithmetic and copies ran while one was open for 3% of the time, Pallas kernels for 36%

profile of v17, /device:TPU:6, one launch (start us, length us, event | category | flops | bytes accessed | tf_op | source)
XLA Modules:
  0.0 279.0 jit_solution(3767922253911056665)
XLA Ops:
  7.2 0.0 all-gather.2.cloned.1.call-start
  7.2 0.7 all-gather.2.cloned.1.call-update
  7.9 4.3 %copy.15 = bf16[512,3328]{0,1:T(8,128)(2,1)S(1)} copy(bf16[512,3328]{1,0:T(8,128)(2,1)} %param.7) | data formatting | bytes 6815744 | tf_op args[3]
  12.2 0.0 copy-start.1
  12.2 4.0 %copy.16 = bf16[512,8,2,208]{3,0,2,1:T(8,128)(2,1)} copy(bf16[512,8,2,208]{0,3,2,1:T(8,128)(2,1)S(1)} %bitcast.11) | data formatting | bytes 6815744 | tf_op jit(solution)/shard_map/reshape | solution.py:319
  16.2 1.1 constant_dynamic-slice_fusion.wcol_ref
  17.3 0.0 copy-done.1
  17.3 101.6 %shard_map.59.tw_ref = bf16[16,256,208]{2,1,0:T(8,128)(2,1)S(1)} custom-call(bf16[256,256]{1,0:T(8,128)(2,1)S(1)} %copy-done.1, bf16[512,208]{1,0:T(8,128)(2,1)S(1)} %constant_dynamic-slice_fusion.wcol_ref), custom_call_target="tpu_custom_call" | custom-call | flops 436207616 | bytes 7208960 | tf_op jit(solution)/shard_map/pallas_call | solution.py:280
  118.9 0.0 copy-start
  118.9 1.3 copy-done
  120.2 43.4 %all-gather.2.cloned.1.call-done = bf16[416,2,8960]{2,1,0:T(2,128)(2,1)} async-done(((bf16[26,2,8960]{2,1,0:T(2,128)(2,1)}), bf16[416,2,8960]{2,1,0:T(2,128)(2,1)}) %all-gather.2.cloned.1.call-update) | async-done | bytes 14909456 | tf_op jit(solution)/shard_map/all_gather | solution.py:314
  163.7 20.6 %fusion.3 = bf16[688,416,2]{0,1,2:T(8,128)(2,1)} fusion(bf16[416,2,8960]{2,1,0:T(2,128)(2,1)} %all-gather.2.cloned.1.call-done, bf16[688,8960]{1,0:T(8,128)(2,1)} %param.6), kind=kOutput, calls=%fused_computation.3 | convolution fusion | flops 10258267136 | bytes 28383232 | tf_op jit(solution)/shard_map/smf,cf->msc/dot_general | solution.py:315
  184.3 83.4 %shard_map.60 = (bf16[2,512,688]{2,1,0:T(8,128)(2,1)}, bf16[256,688]{1,0:T(8,128)(2,1)}) custom-call(bf16[4,208,688]{2,1,0:T(8,128)(2,1)} %bitcast.14, bf16[8,2,512,208]{3,2,1,0:T(8,128)(2,1)} %bitcast.12, bf16[16,256,208]{2,1,0:T(8,128)(2,1)} %copy-done), custom_call_target="tpu_custom_call" | custom-call | flops 7033847808 | bytes 9158656 | tf_op jit(solution)/shard_map/pallas_call | solution.py:148
  267.7 2.5 copy.17
  270.2 1.9 copy.18
Async XLA Ops:
  7.2 156.5 %all-gather.2.cloned.1.call-start = ((), (), s32[]{:S(2)}) async-start(), calls=%async_computation | async-start | bytes 15841280 | tf_op jit(solution)/shard_map/all_gather | solution.py:314
  12.2 5.1 %copy-start.1 = (bf16[256,256]{1,0:T(8,128)(2,1)S(1)}, bf16[256,256]{1,0:T(8,128)(2,1)}, u32[]{:S(2)}) copy-start(bf16[256,256]{1,0:T(8,128)(2,1)} %tok_ref.1) | copy-start | bytes 393220
  118.9 1.3 copy-start
Sparse Core Ops, SparseCore 0:
  10.5 153.0 all-gather.1

commit v18 on v17

--- a/solution.py
+++ b/solution.py
@@ -84,8 +84,8 @@
         return g, h
 
     hb = recv.shape[2]
-    cut = (hb // 2) // 16 * 16
-    subs = ((0, cut), (cut, hb - cut))
+    cut = (hb // 3) // 16 * 16
+    subs = ((0, cut), (cut, cut), (2 * cut, hb - 2 * cut))
 
     def send(q, sub, k):
         dev, pos, sgn = flows[q]
@@ -97,7 +97,7 @@
             device_id=(dev(pos + sgn + n), t), device_id_type=MESH)
 
     for q in range(4):
-        for sub in range(2):
+        for sub in range(len(subs)):
             send(q, sub, 0).start()
 
     def step(k, carry):
@@ -121,7 +121,7 @@
             pre[0] += h0
             pre[1] += h1
 
-        for sub in range(2):
+        for sub in range(len(subs)):
             for q in range(4):
                 send(q, sub, k).wait()
 
@@ -157,8 +157,8 @@
             pltpu.VMEM((4, n, hb, cols), jnp.bfloat16),
             pltpu.VMEM((2, rows, cols), jnp.float32),
             pltpu.VMEM((2, tok, cols), jnp.float32),
-            pltpu.SemaphoreType.DMA((4, 2, n - 1)),
-            pltpu.SemaphoreType.DMA((4, 2, n - 1)),
+            pltpu.SemaphoreType.DMA((4, 3, n - 1)),
+            pltpu.SemaphoreType.DMA((4, 3, n - 1)),
             pltpu.SemaphoreType.DMA((4,)),
         ],
         compiler_params=pltpu.CompilerParams(

time: 281 us -> 281 us (level)
  no operation moved by 1% of the time
where the time goes in v18:
time: 281 us; the launch traced here: 280 us
  Pallas kernels  186 us (66%)
  waiting for transfers between devices  44.1 us (16%)
  matrix products  20.6 us (7%)
  local copies, waits for them, and re-layouts  15.1 us (5%)
  between operations  14.1 us (5%)
    pallas_call x1, Pallas kernels, _tw(): pl.pallas_call(functools.partial(_tw_kernel, nt, nd), out_shape=jax.Shape...  102 us
    pallas_call x1, Pallas kernels, _dp_ring(): pl.pallas_call(functools.partial(_dp_ring_kernel, n), out_shape=(jax.Shap...  84 us
    all_gather x1, waiting for transfers between devices, on_device(): lax.all_gather(small_weights.transpose(1, 0, 2), 'tensor', axis=0, tiled=...  43.4 us
    dot_general x1, matrix products, on_device(): jnp.einsum('smf,cf->msc', s_rows, ffn_growth, preferred_element_type=jnp....  20.6 us
  transfers between devices with their start and end apart: 1, of which 1 were waited for; matrix products, arithmetic and copies ran while one was open for 3% of the time, Pallas kernels for 36%

profile of v18, /device:TPU:6, one launch (start us, length us, event | category | flops | bytes accessed | tf_op | source)
XLA Modules:
  0.0 279.5 jit_solution(17423554504168281483)
XLA Ops:
  7.2 0.0 all-gather.2.cloned.1.call-start
  7.2 0.7 all-gather.2.cloned.1.call-update
  7.9 4.3 %copy.15 = bf16[512,3328]{0,1:T(8,128)(2,1)S(1)} copy(bf16[512,3328]{1,0:T(8,128)(2,1)} %param.7) | data formatting | bytes 6815744 | tf_op args[3]
  12.2 0.0 copy-start.1
  12.2 4.0 %copy.16 = bf16[512,8,2,208]{3,0,2,1:T(8,128)(2,1)} copy(bf16[512,8,2,208]{0,3,2,1:T(8,128)(2,1)S(1)} %bitcast.11) | data formatting | bytes 6815744 | tf_op jit(solution)/shard_map/reshape | solution.py:319
  16.2 1.1 constant_dynamic-slice_fusion.wcol_ref
  17.3 0.0 copy-done.1
  17.3 101.6 %shard_map.59.tw_ref = bf16[16,256,208]{2,1,0:T(8,128)(2,1)S(1)} custom-call(bf16[256,256]{1,0:T(8,128)(2,1)S(1)} %copy-done.1, bf16[512,208]{1,0:T(8,128)(2,1)S(1)} %constant_dynamic-slice_fusion.wcol_ref), custom_call_target="tpu_custom_call" | custom-call | flops 436207616 | bytes 7208960 | tf_op jit(solution)/shard_map/pallas_call | solution.py:280
  118.9 0.0 copy-start
  118.9 1.3 copy-done
  120.2 43.4 %all-gather.2.cloned.1.call-done = bf16[416,2,8960]{2,1,0:T(2,128)(2,1)} async-done(((bf16[26,2,8960]{2,1,0:T(2,128)(2,1)}), bf16[416,2,8960]{2,1,0:T(2,128)(2,1)}) %all-gather.2.cloned.1.call-update) | async-done | bytes 14909456 | tf_op jit(solution)/shard_map/all_gather | solution.py:314
  163.7 20.6 %fusion.3 = bf16[688,416,2]{0,1,2:T(8,128)(2,1)} fusion(bf16[416,2,8960]{2,1,0:T(2,128)(2,1)} %all-gather.2.cloned.1.call-done, bf16[688,8960]{1,0:T(8,128)(2,1)} %param.6), kind=kOutput, calls=%fused_computation.3 | convolution fusion | flops 10258267136 | bytes 28383232 | tf_op jit(solution)/shard_map/smf,cf->msc/dot_general | solution.py:315
  184.3 84.0 %shard_map.60 = (bf16[2,512,688]{2,1,0:T(8,128)(2,1)}, bf16[256,688]{1,0:T(8,128)(2,1)}) custom-call(bf16[4,208,688]{2,1,0:T(8,128)(2,1)} %bitcast.14, bf16[8,2,512,208]{3,2,1,0:T(8,128)(2,1)} %bitcast.12, bf16[16,256,208]{2,1,0:T(8,128)(2,1)} %copy-done), custom_call_target="tpu_custom_call" | custom-call | flops 7033847808 | bytes 9158656 | tf_op jit(solution)/shard_map/pallas_call | solution.py:148
  268.2 2.5 copy.17
  270.8 1.9 copy.18
Async XLA Ops:
  7.2 156.5 %all-gather.2.cloned.1.call-start = ((), (), s32[]{:S(2)}) async-start(), calls=%async_computation | async-start | bytes 15841280 | tf_op jit(solution)/shard_map/all_gather | solution.py:314
  12.2 5.1 %copy-start.1 = (bf16[256,256]{1,0:T(8,128)(2,1)S(1)}, bf16[256,256]{1,0:T(8,128)(2,1)}, u32[]{:S(2)}) copy-start(bf16[256,256]{1,0:T(8,128)(2,1)} %tok_ref.1) | copy-start | bytes 393220
  118.9 1.3 copy-start
Sparse Core Ops, SparseCore 0:
  10.5 153.0 all-gather.1

commit v19 on v17

--- a/solution.py
+++ b/solution.py
@@ -84,7 +84,7 @@
         return g, h
 
     hb = recv.shape[2]
-    cut = (hb // 2) // 16 * 16
+    cut = (hb // 3) // 16 * 16
     subs = ((0, cut), (cut, hb - cut))
 
     def send(q, sub, k):

time: 281 us -> 281 us (level)
  no operation moved by 1% of the time
where the time goes in v19:
time: 281 us; the launch traced here: 279 us
  Pallas kernels  185 us (66%)
  waiting for transfers between devices  44.1 us (16%)
  matrix products  20.6 us (7%)
  local copies, waits for them, and re-layouts  15.1 us (5%)
  between operations  14.1 us (5%)
    pallas_call x1, Pallas kernels, _tw(): pl.pallas_call(functools.partial(_tw_kernel, nt, nd), out_shape=jax.Shape...  102 us
    pallas_call x1, Pallas kernels, _dp_ring(): pl.pallas_call(functools.partial(_dp_ring_kernel, n), out_shape=(jax.Shap...  83.4 us
    all_gather x1, waiting for transfers between devices, on_device(): lax.all_gather(small_weights.transpose(1, 0, 2), 'tensor', axis=0, tiled=...  43.4 us
    dot_general x1, matrix products, on_device(): jnp.einsum('smf,cf->msc', s_rows, ffn_growth, preferred_element_type=jnp....  20.6 us
  transfers between devices with their start and end apart: 1, of which 1 were waited for; matrix products, arithmetic and copies ran while one was open for 3% of the time, Pallas kernels for 36%

profile of v19, /device:TPU:6, one launch (start us, length us, event | category | flops | bytes accessed | tf_op | source)
XLA Modules:
  0.0 279.0 jit_solution(179606042821835061)
XLA Ops:
  7.2 0.0 all-gather.2.cloned.1.call-start
  7.2 0.7 all-gather.2.cloned.1.call-update
  7.9 4.3 %copy.15 = bf16[512,3328]{0,1:T(8,128)(2,1)S(1)} copy(bf16[512,3328]{1,0:T(8,128)(2,1)} %param.7) | data formatting | bytes 6815744 | tf_op args[3]
  12.2 0.0 copy-start.1
  12.2 4.0 %copy.16 = bf16[512,8,2,208]{3,0,2,1:T(8,128)(2,1)} copy(bf16[512,8,2,208]{0,3,2,1:T(8,128)(2,1)S(1)} %bitcast.11) | data formatting | bytes 6815744 | tf_op jit(solution)/shard_map/reshape | solution.py:319
  16.2 1.1 constant_dynamic-slice_fusion.wcol_ref
  17.3 0.0 copy-done.1
  17.3 101.6 %shard_map.59.tw_ref = bf16[16,256,208]{2,1,0:T(8,128)(2,1)S(1)} custom-call(bf16[256,256]{1,0:T(8,128)(2,1)S(1)} %copy-done.1, bf16[512,208]{1,0:T(8,128)(2,1)S(1)} %constant_dynamic-slice_fusion.wcol_ref), custom_call_target="tpu_custom_call" | custom-call | flops 436207616 | bytes 7208960 | tf_op jit(solution)/shard_map/pallas_call | solution.py:280
  118.9 0.0 copy-start
  118.9 1.3 copy-done
  120.2 43.4 %all-gather.2.cloned.1.call-done = bf16[416,2,8960]{2,1,0:T(2,128)(2,1)} async-done(((bf16[26,2,8960]{2,1,0:T(2,128)(2,1)}), bf16[416,2,8960]{2,1,0:T(2,128)(2,1)}) %all-gather.2.cloned.1.call-update) | async-done | bytes 14909456 | tf_op jit(solution)/shard_map/all_gather | solution.py:314
  163.7 20.6 %fusion.3 = bf16[688,416,2]{0,1,2:T(8,128)(2,1)} fusion(bf16[416,2,8960]{2,1,0:T(2,128)(2,1)} %all-gather.2.cloned.1.call-done, bf16[688,8960]{1,0:T(8,128)(2,1)} %param.6), kind=kOutput, calls=%fused_computation.3 | convolution fusion | flops 10258267136 | bytes 28383232 | tf_op jit(solution)/shard_map/smf,cf->msc/dot_general | solution.py:315
  184.3 83.4 %shard_map.60 = (bf16[2,512,688]{2,1,0:T(8,128)(2,1)}, bf16[256,688]{1,0:T(8,128)(2,1)}) custom-call(bf16[4,208,688]{2,1,0:T(8,128)(2,1)} %bitcast.14, bf16[8,2,512,208]{3,2,1,0:T(8,128)(2,1)} %bitcast.12, bf16[16,256,208]{2,1,0:T(8,128)(2,1)} %copy-done), custom_call_target="tpu_custom_call" | custom-call | flops 7033847808 | bytes 9158656 | tf_op jit(solution)/shard_map/pallas_call | solution.py:148
  267.7 2.5 copy.17
  270.2 1.9 copy.18
Async XLA Ops:
  7.2 156.5 %all-gather.2.cloned.1.call-start = ((), (), s32[]{:S(2)}) async-start(), calls=%async_computation | async-start | bytes 15841280 | tf_op jit(solution)/shard_map/all_gather | solution.py:314
  12.2 5.1 %copy-start.1 = (bf16[256,256]{1,0:T(8,128)(2,1)S(1)}, bf16[256,256]{1,0:T(8,128)(2,1)}, u32[]{:S(2)}) copy-start(bf16[256,256]{1,0:T(8,128)(2,1)} %tok_ref.1) | copy-start | bytes 393220
  118.9 1.3 copy-start
Sparse Core Ops, SparseCore 0:
  10.5 153.0 all-gather.1

commit v20 on v19

--- a/solution.py
+++ b/solution.py
@@ -84,7 +84,7 @@
         return g, h
 
     hb = recv.shape[2]
-    cut = (hb // 3) // 16 * 16
+    cut = (hb // 4) // 16 * 16
     subs = ((0, cut), (cut, hb - cut))
 
     def send(q, sub, k):

time: 281 us -> 281 us (level)
  no operation moved by 1% of the time
where the time goes in v20:
time: 281 us; the launch traced here: 279 us
  Pallas kernels  185 us (66%)
  waiting for transfers between devices  44.1 us (16%)
  matrix products  20.6 us (7%)
  local copies, waits for them, and re-layouts  15.1 us (5%)
  between operations  14.1 us (5%)
    pallas_call x1, Pallas kernels, _tw(): pl.pallas_call(functools.partial(_tw_kernel, nt, nd), out_shape=jax.Shape...  102 us
    pallas_call x1, Pallas kernels, _dp_ring(): pl.pallas_call(functools.partial(_dp_ring_kernel, n), out_shape=(jax.Shap...  83.4 us
    all_gather x1, waiting for transfers between devices, on_device(): lax.all_gather(small_weights.transpose(1, 0, 2), 'tensor', axis=0, tiled=...  43.4 us
    dot_general x1, matrix products, on_device(): jnp.einsum('smf,cf->msc', s_rows, ffn_growth, preferred_element_type=jnp....  20.6 us
  transfers between devices with their start and end apart: 1, of which 1 were waited for; matrix products, arithmetic and copies ran while one was open for 3% of the time, Pallas kernels for 36%

profile of v20, /device:TPU:6, one launch (start us, length us, event | category | flops | bytes accessed | tf_op | source)
XLA Modules:
  0.0 279.0 jit_solution(8204297962449677283)
XLA Ops:
  7.2 0.0 all-gather.2.cloned.1.call-start
  7.2 0.7 all-gather.2.cloned.1.call-update
  7.9 4.3 %copy.15 = bf16[512,3328]{0,1:T(8,128)(2,1)S(1)} copy(bf16[512,3328]{1,0:T(8,128)(2,1)} %param.7) | data formatting | bytes 6815744 | tf_op args[3]
  12.2 0.0 copy-start.1
  12.2 4.0 %copy.16 = bf16[512,8,2,208]{3,0,2,1:T(8,128)(2,1)} copy(bf16[512,8,2,208]{0,3,2,1:T(8,128)(2,1)S(1)} %bitcast.11) | data formatting | bytes 6815744 | tf_op jit(solution)/shard_map/reshape | solution.py:319
  16.2 1.1 constant_dynamic-slice_fusion.wcol_ref
  17.3 0.0 copy-done.1
  17.3 101.6 %shard_map.59.tw_ref = bf16[16,256,208]{2,1,0:T(8,128)(2,1)S(1)} custom-call(bf16[256,256]{1,0:T(8,128)(2,1)S(1)} %copy-done.1, bf16[512,208]{1,0:T(8,128)(2,1)S(1)} %constant_dynamic-slice_fusion.wcol_ref), custom_call_target="tpu_custom_call" | custom-call | flops 436207616 | bytes 7208960 | tf_op jit(solution)/shard_map/pallas_call | solution.py:280
  118.9 0.0 copy-start
  118.9 1.3 copy-done
  120.2 43.4 %all-gather.2.cloned.1.call-done = bf16[416,2,8960]{2,1,0:T(2,128)(2,1)} async-done(((bf16[26,2,8960]{2,1,0:T(2,128)(2,1)}), bf16[416,2,8960]{2,1,0:T(2,128)(2,1)}) %all-gather.2.cloned.1.call-update) | async-done | bytes 14909456 | tf_op jit(solution)/shard_map/all_gather | solution.py:314
  163.7 20.6 %fusion.3 = bf16[688,416,2]{0,1,2:T(8,128)(2,1)} fusion(bf16[416,2,8960]{2,1,0:T(2,128)(2,1)} %all-gather.2.cloned.1.call-done, bf16[688,8960]{1,0:T(8,128)(2,1)} %param.6), kind=kOutput, calls=%fused_computation.3 | convolution fusion | flops 10258267136 | bytes 28383232 | tf_op jit(solution)/shard_map/smf,cf->msc/dot_general | solution.py:315
  184.3 83.4 %shard_map.60 = (bf16[2,512,688]{2,1,0:T(8,128)(2,1)}, bf16[256,688]{1,0:T(8,128)(2,1)}) custom-call(bf16[4,208,688]{2,1,0:T(8,128)(2,1)} %bitcast.14, bf16[8,2,512,208]{3,2,1,0:T(8,128)(2,1)} %bitcast.12, bf16[16,256,208]{2,1,0:T(8,128)(2,1)} %copy-done), custom_call_target="tpu_custom_call" | custom-call | flops 7033847808 | bytes 9158656 | tf_op jit(solution)/shard_map/pallas_call | solution.py:148
  267.7 2.5 copy.17
  270.2 1.9 copy.18
Async XLA Ops:
  7.2 156.5 %all-gather.2.cloned.1.call-start = ((), (), s32[]{:S(2)}) async-start(), calls=%async_computation | async-start | bytes 15841280 | tf_op jit(solution)/shard_map/all_gather | solution.py:314
  12.2 5.1 %copy-start.1 = (bf16[256,256]{1,0:T(8,128)(2,1)S(1)}, bf16[256,256]{1,0:T(8,128)(2,1)}, u32[]{:S(2)}) copy-start(bf16[256,256]{1,0:T(8,128)(2,1)} %tok_ref.1) | copy-start | bytes 393220
  118.9 1.3 copy-start
Sparse Core Ops, SparseCore 0:
  10.5 153.0 all-gather.1
